TPU v7x, 256 devices: a whole 4x4x8 slice. The times are simulated.
256 devices in a mesh: gx: 16 (over x, y), gy: 16 (over z, core).
Axes of the slice: x: 4, y: 4, z: 8, core: 2. Of those that a mesh axis runs over, the one named last changes fastest.
Arguments:
- fine_nodes: bfloat16 [524288, 256], P(('gx', 'gy')), may hold values from -6 to 6
- fine_weights: bfloat16 [6, 256, 256], replicated, may hold values from -0.375 to 0.375
- coarse_weights: bfloat16 [6, 256, 256], replicated, may hold values from -0.375 to 0.375
- top_weights: bfloat16 [6, 256, 256], replicated, may hold values from -0.375 to 0.375
- gains: float32 [3, 256], replicated, may hold values from 0.1 to 1.9
- send_list: int32 [16, 16, 4, 512], P('gx', 'gy'), may hold values from 0 to 2047
- fine_sender: int32 [16, 16, 8192], P('gx', 'gy'), may hold values from 0 to 4095, as said below
- fine_receiver: int32 [16, 16, 8192], P('gx', 'gy'), may hold values from 0 to 2048, as said below
- pool_owner: int32 [524288, 1], P(('gx', 'gy')), may hold values from 0 to 15; in each aligned block of 2048 rows (0 to 2047, 2048 to 4095, ...) at most 256 rows name the same one
- pool_local: int32 [524288], P(('gx', 'gy')), may hold values from 0 to 255
- coarse_sender: int32 [16, 16384], P('gy', 'gx'), may hold values from 0 to 4095
- coarse_receiver: int32 [16, 16384], P('gy', 'gx'), may hold values from 0 to 255
- top_parent: int32 [16, 4096], P('gy', 'gx'), may hold values from 0 to 511
- top_sender: int32 [16, 2048], P('gy'), may hold values from 0 to 511
- top_receiver: int32 [16, 2048], P('gy'), may hold values from 0 to 511
Outputs:
- fine_state: bfloat16 [524288, 256], P(('gx', 'gy'))
- coarse_state: bfloat16 [16, 4096, 256], P('gy', 'gx')
Inputs may be any that keep to these rules, and one draw needn't show every extreme that they name: `fine_sender`: values below 2048 name the device's own nodes; larger values name a halo row of a neighbour that exists. `fine_receiver`: 2048 marks an empty slot; a device's live slots come first, and some device has no empty slot. `pool_owner`: among the rows of one device no member is named more than 256 times.
All inputs are finite; a program needn't handle non-finite values.
Results may differ from a plain program's by a relative error of at most 0.015.
Values may be sent and summed in bfloat16 or wider, within the bound.
A program may use at most 64 MiB of HBM per device.

v0:
```python
import math

import jax
import jax.numpy as jnp
from jax import lax
from jax.sharding import PartitionSpec as P


def passed_along(block, axis, distance):
    devices = range(lax.axis_size(axis))
    route = [(i - distance, i) for i in devices if i - distance in devices]
    return lax.ppermute(block, axis, route)


def in_blocks(value, dim, devices):
    lengths = value.shape
    pieces = value.reshape(*lengths[:dim], devices, lengths[dim] // devices, *lengths[dim + 1 :])
    return jnp.moveaxis(pieces, dim, 0)


def sum_at_owner(value, axis, dim):
    pieces = in_blocks(value, dim, lax.axis_size(axis))
    arrived = lax.all_to_all(pieces, axis, split_axis=0, concat_axis=0, tiled=True)
    return arrived.astype(jnp.float32).sum(axis=0)


def in_one_piece(arrays, axis, dim, along):
    columns = [a.reshape(*a.shape[:along], -1) for a in arrays]
    both = jnp.concatenate(columns, axis=along)
    whole, at, outs = (sum_at_owner(both, axis, dim), 0, [])
    for a, column in zip(arrays, columns):
        share = whole[..., at : at + column.shape[along]]
        outs.append(share.reshape(*share.shape[:along], *a.shape[along:]))
        at += column.shape[along]
    return tuple(outs)


def total_of_pieces(value, axis):
    pieces = lax.all_gather(value, axis).astype(jnp.float32)
    return pieces.sum(axis=0)


def copy_for_each(value, axis):
    copies = jnp.broadcast_to(value, (lax.axis_size(axis), *value.shape))
    return lax.all_to_all(copies, axis, split_axis=0, concat_axis=0, tiled=True)


def in_order(pieces, dim):
    pieces = jnp.moveaxis(pieces, 0, dim)
    lengths = pieces.shape
    return pieces.reshape(*lengths[:dim], lengths[dim] * lengths[dim + 1], *lengths[dim + 2 :])


def gather_directly(value, axis, dim):
    pieces = copy_for_each(value, axis)
    return in_order(pieces, dim)


def project(states, weights):
    sender_term = jnp.dot(states, weights[0], preferred_element_type=jnp.float32).astype(
        jnp.bfloat16
    )
    receiver_term = jnp.dot(states, weights[1], preferred_element_type=jnp.float32).astype(
        jnp.bfloat16
    )
    return (sender_term, receiver_term)


def gather_messages(fetch, receiver_term, receivers, weight_out, count, most):
    edges = receivers.shape[0]
    block = math.gcd(edges, most)
    width = receiver_term.shape[1]

    def advance(summed, turn):
        begin = turn * block
        targets = lax.dynamic_slice_in_dim(receivers, begin, block)
        before = fetch(begin, block) + jnp.take(
            receiver_term, jnp.minimum(targets, count - 1), axis=0
        ).astype(jnp.float32)
        hidden = jax.nn.silu(before).astype(jnp.bfloat16)
        message = jnp.dot(hidden, weight_out, preferred_element_type=jnp.float32)
        return (summed.at[targets].add(message, mode="drop"), None)

    turns = jnp.arange(edges // block, dtype=jnp.int32)
    summed, unused = lax.scan(advance, jnp.zeros((count, width), jnp.float32), turns)
    return summed


def update_nodes(states, aggregate, weights, gain):
    merged = jnp.dot(states, weights[3], preferred_element_type=jnp.float32)
    merged = merged + jnp.dot(
        aggregate.astype(jnp.bfloat16), weights[4], preferred_element_type=jnp.float32
    )
    inner = jax.nn.silu(merged).astype(jnp.bfloat16)
    output = jnp.dot(inner, weights[5], preferred_element_type=jnp.float32)
    centred = output - jnp.mean(output, axis=1, keepdims=True)
    spread = jnp.mean(centred * centred, axis=1, keepdims=True)
    return (states.astype(jnp.float32) + gain * centred * lax.rsqrt(spread + 1e-05)).astype(
        jnp.bfloat16
    )


def table_fetch(table, senders):

    def fetch(begin, rows):
        picked = lax.dynamic_slice_in_dim(senders, begin, rows)
        return jnp.take(table, picked, axis=0).astype(jnp.float32)

    return fetch


def body(
    fine_nodes,
    fine_weights,
    coarse_weights,
    top_weights,
    gains,
    send_list,
    fine_sender,
    fine_receiver,
    pool_owner,
    pool_local,
    coarse_sender,
    coarse_receiver,
    top_parent,
    top_sender,
    top_receiver,
):
    nodes = fine_nodes.shape[0]
    width = fine_nodes.shape[1]
    members = lax.axis_size("gx")
    coarse_rows = nodes // 8
    top_rows = coarse_rows * members // 8
    lists = send_list.reshape(4, -1)
    fine_send, fine_recv = project(fine_nodes, fine_weights)
    pieces = [fine_send]
    for slot, offset in ((0, 1), (1, -1)):
        pieces.append(passed_along(jnp.take(fine_send, lists[slot], axis=0), "gx", offset))
    for slot, offset in ((2, 1), (3, -1)):
        pieces.append(passed_along(jnp.take(fine_send, lists[slot], axis=0), "gy", offset))
    table = jnp.concatenate(pieces, axis=0)
    fine_aggregate = gather_messages(
        table_fetch(table, fine_sender.reshape(-1)),
        fine_recv,
        fine_receiver.reshape(-1),
        fine_weights[2],
        nodes,
        4096,
    )
    fine_one = update_nodes(fine_nodes, fine_aggregate, fine_weights, gains[0])
    owner = pool_owner.reshape(-1)
    parent = owner * coarse_rows + pool_local
    partial_value = (
        jnp.zeros((members * coarse_rows, width), jnp.float32)
        .at[parent]
        .add(fine_one.astype(jnp.float32))
    )
    partial_count = jnp.zeros((members * coarse_rows,), jnp.float32).at[parent].add(1.0)
    coarse_sum, child_count = in_one_piece(
        (partial_value.astype(jnp.bfloat16), partial_count.astype(jnp.bfloat16)), "gx", 0, 1
    )
    coarse_zero = (coarse_sum / jnp.maximum(child_count, 1.0)[:, None]).astype(jnp.bfloat16)
    coarse_send, coarse_recv = project(coarse_zero, coarse_weights)
    coarse_senders = coarse_sender.reshape(-1)
    piece = lax.all_gather(coarse_send, "gx", axis=0, tiled=True)
    inside = (coarse_senders >= 0) & (coarse_senders < piece.shape[0])
    picked = jnp.take(piece, jnp.clip(coarse_senders, 0, piece.shape[0] - 1), axis=0).astype(
        jnp.float32
    )
    gathered = jnp.where(inside[:, None], picked, 0.0)

    def slice_gathered(begin, rows):
        return gathered

    coarse_aggregate = gather_messages(
        slice_gathered,
        coarse_recv,
        coarse_receiver.reshape(-1),
        coarse_weights[2],
        coarse_rows,
        4096,
    )
    coarse_one = update_nodes(coarse_zero, coarse_aggregate, coarse_weights, gains[1])
    parents = top_parent.reshape(-1)
    partial_top = (
        jnp.zeros((top_rows, width), jnp.float32).at[parents].add(coarse_one.astype(jnp.float32))
    )
    partial_top_count = jnp.zeros((top_rows,), jnp.float32).at[parents].add(1.0)
    top_sum, top_count = (
        total_of_pieces(partial_top.astype(jnp.bfloat16), "gx").astype(jnp.float32),
        total_of_pieces(partial_top_count.astype(jnp.bfloat16), "gx").astype(jnp.float32),
    )
    top_zero = (top_sum / jnp.maximum(top_count, 1.0)[:, None]).astype(jnp.bfloat16)
    top_send, top_recv = project(top_zero, top_weights)
    top_aggregate = gather_messages(
        table_fetch(top_send, top_sender.reshape(-1)),
        top_recv,
        top_receiver.reshape(-1),
        top_weights[2],
        top_rows,
        4096,
    )
    top_one = update_nodes(top_zero, top_aggregate, top_weights, gains[2])
    coarse_two = (
        coarse_one.astype(jnp.float32) + jnp.take(top_one, parents, axis=0).astype(jnp.float32)
    ).astype(jnp.bfloat16)
    whole = gather_directly(coarse_two, "gx", 0)
    lifted = jnp.take(whole, parent, axis=0)
    fine_state = (fine_one.astype(jnp.float32) + lifted.astype(jnp.float32)).astype(jnp.bfloat16)
    return (fine_state, coarse_two[None])


def solution(mesh):
    placed = (
        P(("gx", "gy"), None),
        P(),
        P(),
        P(),
        P(),
        P("gx", "gy", None, None),
        P("gx", "gy", None),
        P("gx", "gy", None),
        P(("gx", "gy"), None),
        P(("gx", "gy")),
        P("gy", "gx"),
        P("gy", "gx"),
        P("gy", "gx"),
        P("gy", None),
        P("gy", None),
    )
    return jax.shard_map(
        body,
        mesh=mesh,
        in_specs=placed,
        out_specs=(P(("gx", "gy"), None), P("gy", "gx", None)),
        check_vma=False,
    )
```

profile of v0, /device:TPU:96, one launch (start us, length us, event | category | flops | bytes accessed | tf_op | source)
XLA Modules:
  0.0 478.4 jit_solution(6572406727963635730)
XLA Ops:
  12.6 4.2 collective-permute-start
  28.4 3.6 collective-permute-start.3
  35.4 2.7 fusion.56
  41.5 11.4 %scatter_custom_fusion.2 = f32[4096]{0:T(1024)S(1)} fusion(s32[2048]{0:T(1024)S(1)} %get-tuple-element.113, f32[2048]{0:T(1024)S(1)} %broadcast.315, f32[]{:T(128)} %constant.135.clone.1), kind=kCustom, calls=%fused_computation.148 | custom fusion | flops 2048 | bytes 16388 | tf_op jit(solution)/shard_map/scatter-add | solution.py:158
  58.1 131.6 %while.2 = (s32[]{:T(128)}, f32[2048,256]{1,0:T(8,128)S(1)}, s32[2]{0:T(128)S(1)}, s32[8192]{0:T(1024)S(1)}, s32[8192]{0:T(1024)S(1)}, /*index=5*/bf16[4096,256]...) while((s32[]{:T(128)}, f32[2048,256]{1,0:T(8,128)S(1)}, ...), condition=%wide.region_2.4_spmd, body=%wide.region_0.3_spmd.sunk | while | flops 548507648 | bytes 30195924 | solution.py:85
  59.2 17.0 %gather_fusion = bf16[4096,256]{1,0:T(8,128)(2,1)} fusion(bf16[2048,256]{1,0:T(8,128)(2,1)S(1)} %get-tuple-element.237, s32[4096]{0:T(1024)S(1)} %get-tuple-element.203), kind=kCustom, calls=%fused_computation.2.clone.1 | custom fusion | bytes 4210688 | tf_op jit(solution)/shard_map/while/body/eval_jaxpr/jit(_take)/gather | solution.py:77
  76.3 17.8 %gather_fusion.1 = bf16[4096,256]{1,0:T(8,128)(2,1)} fusion(bf16[4096,256]{1,0:T(8,128)(2,1)} %get-tuple-element.236, s32[4096]{0:T(1024)S(1)} %get-tuple-element.204), kind=kCustom, calls=%fused_computation.1.clone.1 | custom fusion | bytes 4210688 | tf_op jit(solution)/shard_map/while/body/eval_jaxpr/jit(_take)/gather | solution.py:107
  94.1 6.1 %fusion.129 = f32[4096,256]{1,0:T(8,128)} fusion(bf16[256,256]{1,0:T(8,128)(2,1)S(1)} %copy-done.9, bf16[4096,256]{1,0:T(8,128)(2,1)} %gather_fusion, bf16[4096,256]{1,0:T(8,128)(2,1)} %gather_fusion.1, pred[4096]{0:T(1024)(128)(4,1)S(1)} %get-tuple-element.205, pred[4096]{0:T(1024)(128)(4,1)S(1)} %get-tuple-element.206), kind=kOutput, calls=%fused_computation.20.clone.1 | convolution fusion | flops 547356672 | bytes 8527872 | tf_op jit(solution)/shard_map/while/body/eval_jaxpr/dot_general | solution.py:81
  100.2 23.6 %scatter_fusion = f32[2048,256]{1,0:T(8,128)S(1)} fusion(f32[2048,256]{1,0:T(8,128)S(1)} %get-tuple-element.220, s32[4096]{0:T(1024)S(1)} %get-tuple-element.202, f32[4096,256]{1,0:T(8,128)} %fusion.129), kind=kCustom, calls=%fused_computation.12.clone.1 | custom fusion | flops 1048576 | bytes 12599296 | tf_op jit(solution)/shard_map/while/body/eval_jaxpr/scatter-add | solution.py:82
  125.1 17.0 %gather_fusion = bf16[4096,256]{1,0:T(8,128)(2,1)} fusion(bf16[2048,256]{1,0:T(8,128)(2,1)S(1)} %get-tuple-element.237, s32[4096]{0:T(1024)S(1)} %get-tuple-element.203), kind=kCustom, calls=%fused_computation.2.clone.1 | custom fusion | bytes 4210688 | tf_op jit(solution)/shard_map/while/body/eval_jaxpr/jit(_take)/gather | solution.py:77
  142.1 17.8 %gather_fusion.1 = bf16[4096,256]{1,0:T(8,128)(2,1)} fusion(bf16[4096,256]{1,0:T(8,128)(2,1)} %get-tuple-element.236, s32[4096]{0:T(1024)S(1)} %get-tuple-element.204), kind=kCustom, calls=%fused_computation.1.clone.1 | custom fusion | bytes 4210688 | tf_op jit(solution)/shard_map/while/body/eval_jaxpr/jit(_take)/gather | solution.py:107
  159.9 6.1 %fusion.129 = f32[4096,256]{1,0:T(8,128)} fusion(bf16[256,256]{1,0:T(8,128)(2,1)S(1)} %copy-done.9, bf16[4096,256]{1,0:T(8,128)(2,1)} %gather_fusion, bf16[4096,256]{1,0:T(8,128)(2,1)} %gather_fusion.1, pred[4096]{0:T(1024)(128)(4,1)S(1)} %get-tuple-element.205, pred[4096]{0:T(1024)(128)(4,1)S(1)} %get-tuple-element.206), kind=kOutput, calls=%fused_computation.20.clone.1 | convolution fusion | flops 547356672 | bytes 8527872 | tf_op jit(solution)/shard_map/while/body/eval_jaxpr/dot_general | solution.py:81
  166.1 23.6 %scatter_fusion = f32[2048,256]{1,0:T(8,128)S(1)} fusion(f32[2048,256]{1,0:T(8,128)S(1)} %get-tuple-element.220, s32[4096]{0:T(1024)S(1)} %get-tuple-element.202, f32[4096,256]{1,0:T(8,128)} %fusion.129), kind=kCustom, calls=%fused_computation.12.clone.1 | custom fusion | flops 1048576 | bytes 12599296 | tf_op jit(solution)/shard_map/while/body/eval_jaxpr/scatter-add | solution.py:82
  189.7 3.8 fusion.99
  199.5 14.1 %scatter_custom_fusion.1 = f32[4096,256]{1,0:T(8,128)} fusion(s32[2048]{0:T(1024)S(1)} %copy-done.14, f32[2048,256]{1,0:T(8,128)} %copy.63, f32[]{:T(128)} %constant.135.clone.1), kind=kCustom, calls=%fused_computation.41 | custom fusion | flops 524288 | bytes 4194816 | tf_op jit(solution)/shard_map/scatter-add | solution.py:156
  213.6 2.4 convert_element_type.140
  216.0 2.4 copy.64
  220.1 37.6 %all_to_all.10 = bf16[16,256,257]{1,2,0:T(8,128)(2,1)S(1)} all-to-all(bf16[16,256,257]{1,2,0:T(8,128)(2,1)S(1)} %pad_maximum_fusion), channel_id=1, replica_groups=mesh['gx'=16,'gy'=16] {'gx'}, dimensions={0} | all-to-all | bytes 4210688 | tf_op jit(solution)/shard_map/all_to_all | solution.py:23
  260.8 3.9 gather_fusion.3
  264.9 42.1 %all-gather.6.cloned.1.call-done = bf16[4096,256]{1,0:T(8,128)(2,1)} async-done(((bf16[256,256]{1,0:T(8,128)(2,1)}), bf16[4096,256]{1,0:T(8,128)(2,1)}) %all-gather.6.cloned.1.call-update) | async-done | bytes 2097168 | tf_op jit(solution)/shard_map/all_gather | solution.py:165
  307.0 5.3 %gather_fusion.2 = bf16[1024,256]{1,0:T(8,128)(2,1)S(1)} fusion(bf16[4096,256]{1,0:T(8,128)(2,1)} %all-gather.6.cloned.1.call-done, s32[1024]{0:T(1024)S(1)} %get-tuple-element.143), kind=kCustom, calls=%fused_computation.8 | custom fusion | bytes 1052672 | tf_op jit(solution)/shard_map/jit(_take)/gather | solution.py:167
  314.2 6.6 %scatter_custom_fusion.3 = f32[256,256]{1,0:T(8,128)S(1)} fusion(s32[1024]{0:T(1024)S(1)} %bitcast.146, f32[1024,256]{1,0:T(8,128)} %fusion.20, f32[]{:T(128)} %constant.135.clone.1), kind=kCustom, calls=%fused_computation.122 | custom fusion | flops 262144 | bytes 262656 | tf_op jit(solution)/shard_map/while/body/eval_jaxpr/scatter-add | solution.py:82
  326.8 22.9 %all-gather.2 = bf16[16,1,512]{2,1,0:T(2,128)(2,1)S(1)} all-gather(bf16[1,1,512]{2,1,0:T(2,128)(2,1)S(1)} %reshape.453), channel_id=3, replica_groups=mesh['gx'=16,'gy'=16] {'gx'}, dimensions={0}, use_global_device_ids=true | all-gather | bytes 17408 | tf_op jit(solution)/shard_map/all_gather | solution.py:39
  349.9 30.7 %all-gather.8.cloned.1.call-done = bf16[8192,256]{1,0:T(8,128)(2,1)} async-done(((bf16[512,256]{1,0:T(8,128)(2,1)}), bf16[8192,256]{1,0:T(8,128)(2,1)}) %all-gather.8.cloned.1.call-update) | async-done | bytes 4194320 | tf_op jit(solution)/shard_map/all_gather | solution.py:39
  380.6 2.9 convert_reduce_fusion
  385.4 7.5 %gather_fusion.10 = bf16[2048,256]{1,0:T(8,128)(2,1)S(1)} fusion(bf16[512,256]{1,0:T(8,128)(2,1)S(1)} %convolution_convert_fusion.3, s32[2048]{0:T(1024)S(1)} %get-tuple-element.136), kind=kCustom, calls=%fused_computation.3.clone | custom fusion | bytes 2105344 | tf_op jit(solution)/shard_map/while/body/eval_jaxpr/jit(_take)/gather | solution.py:107
  392.9 7.5 %gather_fusion.11 = bf16[2048,256]{1,0:T(8,128)(2,1)S(1)} fusion(bf16[512,256]{1,0:T(8,128)(2,1)S(1)} %convolution_convert_fusion.2, s32[2048]{0:T(1024)S(1)} %get-tuple-element.137), kind=kCustom, calls=%fused_computation.7.clone | custom fusion | bytes 2105344 | tf_op jit(solution)/shard_map/while/body/eval_jaxpr/jit(_take)/gather | solution.py:77
  400.4 4.0 fusion.15
  404.4 12.1 %scatter_custom_fusion.6 = f32[512,256]{1,0:T(8,128)S(1)} fusion(s32[2048]{0:T(1024)S(1)} %bitcast.144, f32[2048,256]{1,0:T(8,128)} %fusion.15, f32[]{:T(128)} %constant.135.clone.1), kind=kCustom, calls=%fused_computation.75 | custom fusion | flops 524288 | bytes 524800 | tf_op jit(solution)/shard_map/while/body/eval_jaxpr/scatter-add | solution.py:82
  421.4 5.3 %all-to-all-start.1 = ((bf16[16,256,256]{2,1,0:T(8,128)(2,1)}), bf16[16,256,256]{2,1,0:T(8,128)(2,1)S(1)}, u32[]{:S(2)}, u32[]{:S(2)}) async-start(bf16[16,256,256]{2,1,0:T(8,128)(2,1)} %broadcast_in_dim.154), calls=%async_computation.1 | async-start | bytes 4194304 | tf_op jit(solution)/shard_map/all_to_all | solution.py:45
  427.5 29.6 %all-to-all-done.1 = bf16[16,256,256]{2,1,0:T(8,128)(2,1)S(1)} async-done(((bf16[16,256,256]{2,1,0:T(8,128)(2,1)}), bf16[16,256,256]{2,1,0:T(8,128)(2,1)S(1)}, u32[]{:S(2)}, u32[]{:S(2)}) %all-to-all-start.1) | async-done | bytes 2097184 | tf_op jit(solution)/shard_map/all_to_all | solution.py:45
  457.1 9.0 %gather_fusion.5 = bf16[2048,256]{1,0:T(8,128)(2,1)} fusion(bf16[4096,256]{1,0:T(8,128)(2,1)S(1)} %bitcast.121, s32[2048]{0:T(1024)S(1)} %broadcast_clamp_fusion), kind=kCustom, calls=%fused_computation.11 | custom fusion | bytes 2105344 | tf_op jit(solution)/shard_map/jit(_take)/gather | solution.py:208
  (167 shorter events, 61.6 us)
Async XLA Ops:
  7.2 299.8 %all-gather.6.cloned.1.call-start = ((), (), s32[]{:S(2)}) async-start(), calls=%async_computation.2 | async-start | bytes 2228224 | tf_op jit(solution)/shard_map/all_gather | solution.py:165
  12.6 41.0 %collective-permute-start = (bf16[512,256]{1,0:T(8,128)(2,1)}, bf16[512,256]{1,0:T(8,128)(2,1)}, u32[]{:S(2)}, u32[]{:S(2)}) collective-permute-start(bf16[512,256]{1,0:T(8,128)(2,1)} %broadcast_select_fusion.3), channel_id=1, source_target_pairs={{0,16},{16,32},{32,48},{48,64},{64,80},{80,96},{96,112},{112,128},... | collective-permute-start | bytes 786440 | tf_op jit(solution)/shard_map/ppermute | solution.py:12
  19.6 35.0 %collective-permute-start.1 = (bf16[512,256]{1,0:T(8,128)(2,1)}, bf16[512,256]{1,0:T(8,128)(2,1)}, u32[]{:S(2)}, u32[]{:S(2)}) collective-permute-start(bf16[512,256]{1,0:T(8,128)(2,1)} %broadcast_select_fusion.2), channel_id=1, source_target_pairs={{16,0},{32,16},{48,32},{64,48},{80,64},{96,80},{112,96},{128,112},... | collective-permute-start | bytes 786440 | tf_op jit(solution)/shard_map/ppermute | solution.py:12
  23.7 31.8 %collective-permute-start.2 = (bf16[512,256]{1,0:T(8,128)(2,1)}, bf16[512,256]{1,0:T(8,128)(2,1)}, u32[]{:S(2)}, u32[]{:S(2)}) collective-permute-start(bf16[512,256]{1,0:T(8,128)(2,1)} %broadcast_select_fusion.1), channel_id=1, source_target_pairs={{0,1},{1,2},{2,3},{3,4},{4,5},{5,6},{6,7},{7,8},{8,9},{9,10},{10,1... | collective-permute-start | bytes 786440 | tf_op jit(solution)/shard_map/ppermute | solution.py:12
  27.6 7.8 %copy-start.3 = (bf16[2048,256]{1,0:T(8,128)(2,1)S(1)}, bf16[2048,256]{1,0:T(8,128)(2,1)}, u32[]{:S(2)}) copy-start(bf16[2048,256]{1,0:T(8,128)(2,1)} %param.21) | copy-start | bytes 3145732
  28.4 28.1 %collective-permute-start.3 = (bf16[512,256]{1,0:T(8,128)(2,1)}, bf16[512,256]{1,0:T(8,128)(2,1)S(1)}, u32[]{:S(2)}, u32[]{:S(2)}) collective-permute-start(bf16[512,256]{1,0:T(8,128)(2,1)} %broadcast_select_fusion), channel_id=1, source_target_pairs={{1,0},{2,1},{3,2},{4,3},{5,4},{6,5},{7,6},{8,7},{9,8},{10,9},{11,1... | collective-permute-start | bytes 786440 | tf_op jit(solution)/shard_map/ppermute | solution.py:12
  33.8 4.3 copy-start.18
  33.8 4.3 copy-start.19
  33.8 4.9 %copy-start.23 = (f32[3,256]{1,0:T(4,128)S(1)}, f32[3,256]{1,0:T(4,128)}, u32[]{:S(2)}) copy-start(f32[3,256]{1,0:T(4,128)} %param.25) | copy-start | bytes 9220
  38.7 2.9 copy-start.13
  53.6 4.5 copy-start.5
  53.6 4.5 copy-start.6
  76.3 17.8 %copy-start.9 = (bf16[256,256]{1,0:T(8,128)(2,1)S(1)}, bf16[256,256]{1,0:T(8,128)(2,1)}, u32[]{:S(2)}) copy-start(bf16[256,256]{1,0:T(8,128)(2,1)} %get-tuple-element.238) | copy-start | bytes 393220 | tf_op jit(solution)/shard_map/while
  142.1 17.8 %copy-start.9 = (bf16[256,256]{1,0:T(8,128)(2,1)S(1)}, bf16[256,256]{1,0:T(8,128)(2,1)}, u32[]{:S(2)}) copy-start(bf16[256,256]{1,0:T(8,128)(2,1)} %get-tuple-element.238) | copy-start | bytes 393220 | tf_op jit(solution)/shard_map/while
  193.5 2.2 copy-start.4
  193.5 2.2 copy-start.22
  197.5 2.0 copy-start.1
  197.5 2.0 copy-start.14
  216.0 2.4 copy-start.10
  257.7 1.5 copy-start.8
  257.7 2.6 copy-start.11
  257.7 2.7 copy-start.24
  257.7 2.7 copy-start.16
  260.1 120.5 %all-gather.8.cloned.1.call-start = ((), (), s32[]{:S(2)}) async-start(), calls=%async_computation.3 | async-start | bytes 4456448 | tf_op jit(solution)/shard_map/all_gather | solution.py:39
  314.2 7.1 %copy-start.20 = (f32[1,256]{1,0:T(1,128)S(1)}, f32[1,256]{1,0:T(1,128)}, u32[]{:S(2)}) copy-start(f32[1,256]{1,0:T(1,128)} %get-tuple-element.125) | copy-start | bytes 3076
  320.8 28.9 %copy-start.12 = (s32[1,2048]{1,0:T(1,128)S(1)}, s32[1,2048]{1,0:T(1,128)}, u32[]{:S(2)}) copy-start(s32[1,2048]{1,0:T(1,128)} %param.35) | copy-start | bytes 24580
  320.8 29.0 %copy-start.15 = (s32[1,2048]{1,0:T(1,128)S(1)}, s32[1,2048]{1,0:T(1,128)}, u32[]{:S(2)}) copy-start(s32[1,2048]{1,0:T(1,128)} %param.34) | copy-start | bytes 24580
  380.6 3.1 copy-start.7
  404.4 13.8 %copy-start.21 = (f32[1,256]{1,0:T(1,128)S(1)}, f32[1,256]{1,0:T(1,128)}, u32[]{:S(2)}) copy-start(f32[1,256]{1,0:T(1,128)} %get-tuple-element.123) | copy-start | bytes 3076
  421.4 35.6 %all-to-all-start.1 = ((bf16[16,256,256]{2,1,0:T(8,128)(2,1)}), bf16[16,256,256]{2,1,0:T(8,128)(2,1)S(1)}, u32[]{:S(2)}, u32[]{:S(2)}) async-start(bf16[16,256,256]{2,1,0:T(8,128)(2,1)} %broadcast_in_dim.154), calls=%async_computation.1 | async-start | bytes 4194304 | tf_op jit(solution)/shard_map/all_to_all | solution.py:45
  457.1 10.7 %copy-start.17 = (pred[2048]{0:T(1024)(128)(4,1)S(1)}, pred[2048]{0:T(1024)(128)(4,1)}, u32[]{:S(2)}) copy-start(pred[2048]{0:T(1024)(128)(4,1)} %get-tuple-element.112) | copy-start | bytes 6148
  466.1 1.9 copy-start.2
  (1 other events, 1.3 us)
Sparse Core Ops, SparseCore 0:
  260.2 46.7 all-gather.5
  324.6 55.9 all-gather.7
where the time goes:
time: 480 us; the launch traced here: 478 us
  local copies, waits for them, and re-layouts  135 us (28%)
  other arithmetic  115 us (24%)
  waiting for transfers between devices  102 us (21%)
  blocking collectives  60.5 us (13%)
  matrix products  32.9 us (7%)
  starting transfers between devices  16.5 us (3%)
  between operations  14.8 us (3%)
    scatter-add x4, other arithmetic, advance(): return (summed.at[targets].add(message, mode='drop'), None)  65.9 us
    gather x4, local copies, waits for them, and re-layouts, advance(): jnp.take(receiver_term, jnp.minimum(targets, count - 1), axis=0)  45.5 us
    gather x3, local copies, waits for them, and re-layouts, fetch(): return jnp.take(table, picked, axis=0).astype(jnp.float32)  43.1 us
    all_gather x1, waiting for transfers between devices, body(): piece = lax.all_gather(coarse_send, 'gx', axis=0, tiled=True)  42.1 us
    all_to_all x1, blocking collectives, sum_at_owner(): lax.all_to_all(pieces, axis, split_axis=0, concat_axis=0, tiled=True)  37.6 us
    all_gather x1, waiting for transfers between devices, total_of_pieces(): pieces = lax.all_gather(value, axis).astype(jnp.float32)  30.7 us
    all_to_all x1, waiting for transfers between devices, copy_for_each(): return lax.all_to_all(copies, axis, split_axis=0, concat_axis=0, tiled=True)  29.6 us
    all_gather x1, blocking collectives, total_of_pieces(): pieces = lax.all_gather(value, axis).astype(jnp.float32)  22.9 us
  transfers between devices with their start and end apart: 7, of which 3 were waited for; matrix products, arithmetic and copies ran while one was open for 8% of the time, Pallas kernels for 0%

commit v1 on v0

v1 whole, which is shorter than its diff:
```python
import functools

import jax
import jax.numpy as jnp
from jax import lax
from jax.experimental import pallas as pl
from jax.experimental.pallas import tpu as pltpu
from jax.sharding import PartitionSpec as P

F32 = jnp.float32
BF16 = jnp.bfloat16
LANES = 128
VMEM = pltpu.VMEM
SMEM = pltpu.SMEM


def silu(v):
    half = 0.5 * v
    return half + half * jnp.tanh(half)


def dot(a, b):
    return jnp.dot(a, b, preferred_element_type=F32)


def put_rows(pairs, begin, rows, value):
    pairs[pl.ds(2 * begin, rows, stride=2), :] = value[:, :LANES]
    pairs[pl.ds(2 * begin + 1, rows, stride=2), :] = value[:, LANES:]


def get_rows(pairs, begin, rows):
    left = pairs[pl.ds(2 * begin, rows, stride=2), :]
    right = pairs[pl.ds(2 * begin + 1, rows, stride=2), :]
    return left, right


def project_rows(states, weight, pairs, at, rows, block):
    @pl.loop(0, rows // block)
    def _(t):
        begin = pl.multiple_of(t * block, block)
        term = dot(states[pl.ds(begin, block), :], weight).astype(BF16).astype(F32)
        put_rows(pairs, at + begin, block, term)


def spread_rows(table, pairs, at, rows, block):
    @pl.loop(0, rows // block)
    def _(t):
        begin = pl.multiple_of(t * block, block)
        put_rows(pairs, at + begin, block, table[pl.ds(begin, block), :].astype(F32))


def pick_pairs(edges, unroll, out, pick):
    @pl.loop(0, edges // unroll)
    def _(t):
        begin = t * unroll
        found = [pick(begin + u) for u in range(unroll)]
        for u in range(unroll):
            out[pl.ds(2 * (begin + u), 2), :] = found[u]


def one_hot(targets, begin, rows):
    shape = (rows, targets.shape[1])
    return jnp.where(
        lax.broadcasted_iota(jnp.int32, shape, 0) + begin == targets, 1.0, 0.0
    ).astype(BF16)


def pass_edges(senders, receivers, target_row, table, terms, sums, hidden, total, count, chunk, tile):
    edges = receivers.shape[0]

    @pl.loop(0, count // tile)
    def _(t):
        total[pl.ds(pl.multiple_of(t * tile, tile), tile), :] = jnp.zeros((tile, 2 * LANES), F32)

    @pl.loop(0, edges // chunk)
    def _(c):
        first = c * chunk

        def pick(e):
            s = senders[first + e]
            r = receivers[first + e]
            return table[pl.ds(2 * s, 2), :] + terms[pl.ds(2 * r, 2), :]

        pick_pairs(chunk, 16, sums, pick)

        @pl.loop(0, chunk // 64)
        def _(t):
            begin = pl.multiple_of(t * 64, 64)
            left, right = get_rows(sums, begin, 64)
            hidden[pl.ds(begin, 64), :LANES] = silu(left).astype(BF16)
            hidden[pl.ds(begin, 64), LANES:] = silu(right).astype(BF16)

        targets = target_row[:, pl.ds(pl.multiple_of(first, chunk), chunk)]

        @pl.loop(0, count // tile)
        def _(t):
            begin = pl.multiple_of(t * tile, tile)
            total[pl.ds(begin, tile), :] += dot(one_hot(targets, begin, tile), hidden[...])


def update(states, total, weights, gain, begin, rows):
    h = states[pl.ds(begin, rows), :]
    aggregate = dot(total[pl.ds(begin, rows), :].astype(BF16), weights[2]).astype(BF16)
    inner = silu(dot(h, weights[3]) + dot(aggregate, weights[4])).astype(BF16)
    output = dot(inner, weights[5])
    centred = output - jnp.mean(output, axis=1, keepdims=True)
    spread = jnp.mean(centred * centred, axis=1, keepdims=True)
    return (h.astype(F32) + gain * centred * lax.rsqrt(spread + 1e-05)).astype(BF16)


def send_kernel(list_ref, nodes, weights, out, pairs, picked):
    rows = nodes.shape[0]
    project_rows(nodes, weights[0], pairs, 0, rows, 256)
    pick_pairs(list_ref.shape[0], 16, picked, lambda e: pairs[pl.ds(2 * list_ref[e], 2), :])

    @pl.loop(0, out.shape[0] // 64)
    def _(t):
        begin = pl.multiple_of(t * 64, 64)
        left, right = get_rows(picked, begin, 64)
        out[pl.ds(begin, 64), :LANES] = left.astype(BF16)
        out[pl.ds(begin, 64), LANES:] = right.astype(BF16)


def fine_kernel(
    senders, receivers, nodes, halo0, halo1, halo2, halo3, weights, gains, target_row, parent_row,
    fine_one, pooled, table, terms, sums, hidden, total,
):
    rows = nodes.shape[0]
    halo = halo0.shape[0]
    project_rows(nodes, weights[0], table, 0, rows, 256)
    project_rows(nodes, weights[1], terms, 0, rows, 256)
    terms[pl.ds(2 * rows, 8), :] = jnp.zeros((8, LANES), F32)
    for slot, part in enumerate((halo0, halo1, halo2, halo3)):
        spread_rows(part, table, rows + slot * halo, halo, 64)
    pass_edges(senders, receivers, target_row, table, terms, sums, hidden, total, rows, 1024, 256)

    @pl.loop(0, rows // 256)
    def _(t):
        begin = pl.multiple_of(t * 256, 256)
        fine_one[pl.ds(begin, 256), :] = update(nodes, total, weights, gains[0:1, :], begin, 256)

    parents = parent_row[...]

    @pl.loop(0, pooled.shape[0] // 256)
    def _(t):
        begin = pl.multiple_of(t * 256, 256)
        pooled[pl.ds(begin, 256), :] = dot(one_hot(parents, begin, 256), fine_one[...]).astype(BF16)


def coarse_kernel(
    senders, receivers, states, gathered, weights, gains, target_row,
    out, table, terms, sums, hidden, total,
):
    rows = states.shape[0]
    spread_rows(gathered, table, 0, gathered.shape[0], 64)
    project_rows(states, weights[1], terms, 0, rows, 256)
    pass_edges(senders, receivers, target_row, table, terms, sums, hidden, total, rows, 1024, 256)
    out[...] = update(states, total, weights, gains[1:2, :], 0, rows)


def top_kernel(
    senders, receivers, parents, fine_parents, place, coarse, fine_one, weights, gains, target_row,
    parent_row, top_count,
    fine_state, coarse_state, coarse_pairs, table, terms, sums, hidden, total, top_zero,
):
    count = top_zero.shape[0]
    own = coarse_state.shape[0]
    spread_rows(coarse, coarse_pairs, 0, coarse.shape[0], 64)
    above = parent_row[...]

    @pl.loop(0, count // 256)
    def _(t):
        begin = pl.multiple_of(t * 256, 256)
        summed = dot(one_hot(above, begin, 256), coarse[...])
        children = top_count[pl.ds(begin, 256), :]
        top_zero[pl.ds(begin, 256), :] = (summed / jnp.maximum(children, 1.0)).astype(BF16)

    project_rows(top_zero, weights[0], table, 0, count, 256)
    project_rows(top_zero, weights[1], terms, 0, count, 256)
    pass_edges(senders, receivers, target_row, table, terms, sums, hidden, total, count, 1024, 256)

    @pl.loop(0, count // 256)
    def _(t):
        begin = pl.multiple_of(t * 256, 256)
        result = update(top_zero, total, weights, gains[2:3, :], begin, 256).astype(F32)
        put_rows(table, begin, 256, result)

    def lift(parent):
        return coarse_pairs[pl.ds(2 * parent, 2), :] + table[pl.ds(2 * parents[parent], 2), :]

    first = place[0] * own
    pick_pairs(own, 16, sums, lambda e: lift(first + e))

    @pl.loop(0, own // 64)
    def _(t):
        begin = pl.multiple_of(t * 64, 64)
        left, right = get_rows(sums, begin, 64)
        coarse_state[pl.ds(begin, 64), :LANES] = left.astype(BF16)
        coarse_state[pl.ds(begin, 64), LANES:] = right.astype(BF16)

    chunk = sums.shape[0] // 2

    @pl.loop(0, fine_one.shape[0] // chunk)
    def _(c):
        pick_pairs(chunk, 16, sums, lambda e: lift(fine_parents[c * chunk + e]))

        @pl.loop(0, chunk // 64)
        def _(t):
            begin = pl.multiple_of(t * 64, 64)
            to = pl.multiple_of(c * chunk + begin, 64)
            left, right = get_rows(sums, begin, 64)
            for value, at in ((left, 0), (right, LANES)):
                own_part = fine_one[pl.ds(to, 64), at : at + LANES].astype(F32)
                fine_state[pl.ds(to, 64), at : at + LANES] = (
                    own_part + value.astype(BF16).astype(F32)
                ).astype(BF16)


def call(kernel, outs, scalars, arrays, scratch, name, flops=10**9):
    in_specs = [pl.BlockSpec(memory_space=SMEM)] * len(scalars)
    in_specs += [pl.BlockSpec(memory_space=VMEM)] * len(arrays)
    return pl.pallas_call(
        kernel,
        out_shape=outs,
        in_specs=in_specs,
        out_specs=jax.tree.map(lambda _: pl.BlockSpec(memory_space=VMEM), outs),
        scratch_shapes=scratch,
        compiler_params=pltpu.CompilerParams(vmem_limit_bytes=56 << 20),
        cost_estimate=pl.CostEstimate(flops=flops, bytes_accessed=1 << 20, transcendentals=0),
        name=name,
    )(*scalars, *arrays)


def passed_along(block, axis, distance):
    devices = range(lax.axis_size(axis))
    route = [(i - distance, i) for i in devices if i - distance in devices]
    return lax.ppermute(block, axis, route)


def spread_counts(high, low, highs, lows):
    by_high = (high[None, :] == jnp.arange(highs, dtype=jnp.int32)[:, None]).astype(BF16)
    by_low = (low[:, None] == jnp.arange(lows, dtype=jnp.int32)[None, :]).astype(BF16)
    return dot(by_high, by_low)


def shape(rows, width=256, dtype=BF16):
    return jax.ShapeDtypeStruct((rows, width), dtype)


def body(
    fine_nodes, fine_weights, coarse_weights, top_weights, gains, send_list, fine_sender,
    fine_receiver, pool_owner, pool_local, coarse_sender, coarse_receiver, top_parent, top_sender,
    top_receiver,
):
    nodes = fine_nodes.shape[0]
    width = fine_nodes.shape[1]
    members = lax.axis_size("gx")
    coarse_rows = nodes // 8
    coarse_all = coarse_rows * members
    top_rows = coarse_all // 8
    lists = send_list.reshape(-1)
    halo = lists.shape[0] // 4
    owner = pool_owner.reshape(-1)
    parent = owner * coarse_rows + pool_local
    parents = top_parent.reshape(-1)

    counts = spread_counts(owner, pool_local, members, coarse_rows)
    child_count = lax.psum_scatter(counts, "gx", scatter_dimension=0, tiled=True).reshape(-1)
    all_parents = lax.all_gather(parents, "gx", axis=0, tiled=True)
    top_count = spread_counts(all_parents // 32, all_parents % 32, top_rows // 32, 32)
    top_count = top_count.reshape(-1, 1)

    sent = call(
        send_kernel, shape(4 * halo), (lists,), (fine_nodes, fine_weights),
        [VMEM((2 * nodes, LANES), F32), VMEM((8 * halo, LANES), F32)], "send_rows",
    )
    halos = [
        passed_along(sent[slot * halo : (slot + 1) * halo], axis, offset)
        for slot, (axis, offset) in enumerate((("gx", 1), ("gx", -1), ("gy", 1), ("gy", -1)))
    ]
    edges = fine_sender.reshape(-1), fine_receiver.reshape(-1)
    fine_one, pooled = call(
        fine_kernel, (shape(nodes), shape(coarse_all)), edges,
        (fine_nodes, *halos, fine_weights, gains, edges[1][None, :], parent[None, :]),
        [
            VMEM((2 * (nodes + 4 * halo), LANES), F32), VMEM((2 * nodes + 8, LANES), F32),
            VMEM((2048, LANES), F32), VMEM((1024, width), BF16), VMEM((nodes, width), F32),
        ],
        "fine_layer",
    )
    arrived = lax.all_to_all(
        pooled.reshape(members, coarse_rows, width), "gx", split_axis=0, concat_axis=0, tiled=True
    )
    coarse_sum = arrived.astype(F32).sum(axis=0)
    coarse_zero = (coarse_sum / jnp.maximum(child_count, 1.0)[:, None]).astype(BF16)
    coarse_send = dot(coarse_zero, coarse_weights[0]).astype(BF16)
    gathered = lax.all_gather(coarse_send, "gx", axis=0, tiled=True)
    edges = coarse_sender.reshape(-1), coarse_receiver.reshape(-1)
    coarse_one = call(
        coarse_kernel, shape(coarse_rows), edges,
        (coarse_zero, gathered, coarse_weights, gains, edges[1][None, :]),
        [
            VMEM((2 * coarse_all, LANES), F32), VMEM((2 * coarse_rows, LANES), F32),
            VMEM((2048, LANES), F32), VMEM((1024, width), BF16), VMEM((coarse_rows, width), F32),
        ],
        "coarse_layer",
    )
    coarse_whole = lax.all_gather(coarse_one, "gx", axis=0, tiled=True)
    edges = top_sender.reshape(-1), top_receiver.reshape(-1)
    place = lax.axis_index("gx").astype(jnp.int32).reshape(1)
    fine_state, coarse_state = call(
        top_kernel, (shape(nodes), shape(coarse_rows)), (*edges, all_parents, parent, place),
        (
            coarse_whole, fine_one, top_weights, gains, edges[1][None, :], all_parents[None, :],
            top_count,
        ),
        [
            VMEM((2 * coarse_all, LANES), F32), VMEM((2 * top_rows, LANES), F32),
            VMEM((2 * top_rows, LANES), F32), VMEM((2048, LANES), F32), VMEM((1024, width), BF16),
            VMEM((top_rows, width), F32), VMEM((top_rows, width), BF16),
        ],
        "top_layer",
    )
    return (fine_state, coarse_state[None])


def solution(mesh):
    placed = (
        P(("gx", "gy"), None), P(), P(), P(), P(),
        P("gx", "gy", None, None), P("gx", "gy", None), P("gx", "gy", None),
        P(("gx", "gy"), None), P(("gx", "gy")),
        P("gy", "gx"), P("gy", "gx"), P("gy", "gx"), P("gy", None), P("gy", None),
    )
    return jax.shard_map(
        body,
        mesh=mesh,
        in_specs=placed,
        out_specs=(P(("gx", "gy"), None), P("gy", "gx", None)),
        check_vma=False,
    )
```

time: 480 us -> 331 us (0.69)
  local copies, waits for them, and re-layouts: 135 us -> 4.83 us
  other arithmetic: 115 us -> 1.66 us
  Pallas kernels: 0 us -> 97.6 us
  blocking collectives: 60.5 us -> 111 us
  matrix products: 32.9 us -> 2.52 us
  waiting for transfers between devices: 102 us -> 79.8 us
    gather x16 -> x0, local copies, waits for them, and re-layouts: 114 us -> none  [the longest x4 45.5 us: advance(): jnp.take(receiver_term, jnp.minimum(targets, count - 1), axis=0)]
    pallas_call x0 -> x4, Pallas kernels: none -> 97.6 us  [call(): pl.pallas_call(kernel, out_shape=outs, in_specs=in_specs, out_specs=jax.t...]
    scatter-add x8 -> x0, other arithmetic: 95.9 us -> none  [the longest x4 65.9 us: advance(): return (summed.at[targets].add(message, mode='drop'), None)]
    unnamed x0 -> x1, blocking collectives: none -> 87.9 us
    all_to_all x1 -> x0, blocking collectives: 37.6 us -> none  [sum_at_owner(): lax.all_to_all(pieces, axis, split_axis=0, concat_axis=0, tiled=True)]
    dot_general x16 -> x3, matrix products: 32.9 us -> 2.52 us  [dot(): return jnp.dot(a, b, preferred_element_type=F32)]
    all_to_all x1, waiting for transfers between devices: 29.6 us -> 0.01 us  [body(): lax.all_to_all(pooled.reshape(members, coarse_rows, width), 'gx', split_a...]
    unnamed x56 -> x22, local copies, waits for them, and re-layouts: 10.2 us -> 2.61 us
  transfers between devices with their start and end apart: 7 -> 7, of which waited for: 3 -> 4; matrix products, arithmetic and copies ran while one was open for 8% -> 1% of each run, Pallas kernels for 0% -> 0%
where the time goes in v1:
time: 331 us; the launch traced here: 330 us
  blocking collectives  111 us (34%)
  Pallas kernels  97.6 us (29%)
  waiting for transfers between devices  79.8 us (24%)
  starting transfers between devices  18.7 us (6%)
  between operations  14.2 us (4%)
  local copies, waits for them, and re-layouts  4.83 us (1%)
    pallas_call x4, Pallas kernels, call(): pl.pallas_call(kernel, out_shape=outs, in_specs=in_specs, out_specs=jax.t...  97.6 us
    unnamed x1, blocking collectives  87.9 us
    all_gather x1, waiting for transfers between devices, body(): gathered = lax.all_gather(coarse_send, 'gx', axis=0, tiled=True)  50.8 us
    all_gather x1, waiting for transfers between devices, body(): coarse_whole = lax.all_gather(coarse_one, 'gx', axis=0, tiled=True)  25.7 us
    all_gather x1, blocking collectives, body(): all_parents = lax.all_gather(parents, 'gx', axis=0, tiled=True)  22.6 us
    ppermute x4, starting transfers between devices, passed_along(): return lax.ppermute(block, axis, route)  10.3 us
    all_to_all x1, starting transfers between devices, body(): lax.all_to_all(pooled.reshape(members, coarse_rows, width), 'gx', split_a...  8.23 us
  transfers between devices with their start and end apart: 7, of which 4 were waited for; matrix products, arithmetic and copies ran while one was open for 1% of the time, Pallas kernels for 0%

profile of v1, /device:TPU:96, one launch (start us, length us, event | category | flops | bytes accessed | tf_op | source)
XLA Modules:
  0.0 329.8 jit_solution(8902831806407402526)
XLA Ops:
  7.2 1.3 copy.20
  8.5 7.1 %send_rows.1 = bf16[2048,256]{1,0:T(8,128)(2,1)} custom-call(s32[2048]{0:T(1024)} %bitcast.30, bf16[2048,256]{1,0:T(8,128)(2,1)} %nodes.3, bf16[6,256,256]{2,1,0:T(8,128)(2,1)} %weights.5), custom_call_target="tpu_custom_call" | custom-call | flops 1000000000 | bytes 1048576 | tf_op jit(solution)/shard_map/send_rows/pallas_call | solution.py:222
  15.6 1.3 fusion.10
  16.9 3.5 %collective-permute-start = (bf16[512,256]{1,0:T(8,128)(2,1)S(1)}, bf16[512,256]{1,0:T(8,128)(2,1)S(1)}, u32[]{:S(2)}, u32[]{:S(2)}) collective-permute-start(bf16[512,256]{1,0:T(8,128)(2,1)S(1)} %get-tuple-element.13), channel_id=1, source_target_pairs={{0,16},{16,32},{32,48},{48,64},{64,80},{80,96},{96,112},{112,128},... | collective-permute-start | bytes 786440 | tf_op jit(solution)/shard_map/ppermute | solution.py:237
  20.4 1.3 collective-permute-start.1
  21.7 1.9 collective-permute-start.2
  23.6 3.6 %collective-permute-start.3 = (bf16[512,256]{1,0:T(8,128)(2,1)S(1)}, bf16[512,256]{1,0:T(8,128)(2,1)S(1)}, u32[]{:S(2)}, u32[]{:S(2)}) collective-permute-start(bf16[512,256]{1,0:T(8,128)(2,1)S(1)} %get-tuple-element.10), channel_id=1, source_target_pairs={{1,0},{2,1},{3,2},{4,3},{5,4},{6,5},{7,6},{8,7},{9,8},{10,9},{11,1... | collective-permute-start | bytes 786440 | tf_op jit(solution)/shard_map/ppermute | solution.py:237
  27.3 0.6 multiply_add_fusion.fine_parents
  27.9 2.2 collective-permute-done.1.halo1
  30.0 1.1 collective-permute-done.3.halo3
  31.1 0.7 copy-done.8
  31.8 62.8 %fine_layer.1 = (bf16[2048,256]{1,0:T(8,128)(2,1)}, bf16[4096,256]{1,0:T(8,128)(2,1)}) custom-call(s32[8192]{0:T(1024)} %bitcast.33, s32[8192]{0:T(1024)} %bitcast.34, bf16[2048,256]{1,0:T(8,128)(2,1)} %nodes.3, bf16[512,256]{1,0:T(8,128)(2,1)} %copy-done.5, bf16[512,256]{1,0:T(8,128)(2,1)} %copy-done.6, bf16[512,256]{1,0:T(8,128)(2,1)} %copy-done.7, ...), custom_call_target="tpu_custom_call" | custom-call | flops 1000000000 | bytes 1048576 | tf_op jit(solution)/shard_map/fine_layer/pallas_call | solution.py:222
  94.6 8.2 %all-to-all-start = ((bf16[16,256,256]{2,1,0:T(8,128)(2,1)}), bf16[16,256,256]{2,1,0:T(8,128)(2,1)S(1)}, u32[]{:S(2)}, u32[]{:S(2)}) async-start(bf16[16,256,256]{2,1,0:T(8,128)(2,1)} %bitcast.21), calls=%async_computation | async-start | bytes 4194304 | tf_op jit(solution)/shard_map/all_to_all | solution.py:291
  102.9 0.0 all-gather.4.cloned.1.call-start
  102.9 0.6 dynamic-slice
  103.5 0.5 fusion
  104.0 87.9 %all-reduce = f32[16,256]{1,0:T(8,128)S(1)} all-reduce(f32[16,256]{1,0:T(8,128)S(1)} %fusion), channel_id=3, replica_groups=mesh['gx'=16,'gy'=16] {'gx'}, use_global_device_ids=true, to_apply=%region_1.2.clone | all-reduce | flops 4096 | bytes 32768
  191.9 0.7 dynamic-slice_maximum_fusion
  192.6 0.3 convert_reduce_fusion
  192.9 0.1 divide_convert_fusion.states
  193.0 0.0 copy-start
  193.0 1.8 convolution_convert_fusion
  194.8 0.0 all-gather.4.cloned.1.call-update
  194.9 0.0 all-gather.6.cloned.1.call-start
  194.9 50.8 %all-gather.4.cloned.1.call-done.gathered = bf16[4096,256]{1,0:T(8,128)(2,1)} async-done(((bf16[256,256]{1,0:T(8,128)(2,1)}), bf16[4096,256]{1,0:T(8,128)(2,1)}) %all-gather.4.cloned.1.call-update) | async-done | bytes 2097168 | tf_op jit(solution)/shard_map/all_gather | solution.py:297
  245.8 6.8 %coarse_layer.1 = bf16[256,256]{1,0:T(8,128)(2,1)} custom-call(s32[1024]{0:T(1024)} %bitcast.36, s32[1024]{0:T(1024)} %bitcast.37, bf16[256,256]{1,0:T(8,128)(2,1)} %copy-done, bf16[4096,256]{1,0:T(8,128)(2,1)} %all-gather.4.cloned.1.call-done.gathered, bf16[6,256,256]{2,1,0:T(8,128)(2,1)} %weights.6, f32[3,256]{1,0:T(4,128)} %gains.5, s32[1,1024]{1,0:T(1,128)} %target_row.2), custom_call_target="tpu_custom_call" | custom-call | flops 1000000000 | bytes 1048576 | tf_op jit(solution)/shard_map/coarse_layer/pallas_call | solution.py:222
  252.5 0.0 all-gather.6.cloned.1.call-update
  252.6 22.6 %all-gather.parent_row = s32[1,4096]{1,0:T(1,128)S(1)} all-gather(s32[1,256]{1,0:T(1,128)S(1)} %copy-done.4), channel_id=2, replica_groups=mesh['gx'=16,'gy'=16] {'gx'}, dimensions={1}, use_global_device_ids=true | all-gather | bytes 17408 | tf_op jit(solution)/shard_map/all_gather | solution.py:269
  275.2 0.2 fusion.2
  275.5 1.0 reshape.66.top_count
  276.4 25.7 %all-gather.6.cloned.1.call-done.coarse = bf16[4096,256]{1,0:T(8,128)(2,1)} async-done(((bf16[256,256]{1,0:T(8,128)(2,1)}), bf16[4096,256]{1,0:T(8,128)(2,1)}) %all-gather.6.cloned.1.call-update) | async-done | bytes 2097168 | tf_op jit(solution)/shard_map/all_gather | solution.py:308
  302.1 20.8 %top_layer.1 = (bf16[2048,256]{1,0:T(8,128)(2,1)}, bf16[256,256]{1,0:T(8,128)(2,1)}) custom-call(s32[2048]{0:T(1024)} %bitcast.26, s32[2048]{0:T(1024)} %bitcast.24, s32[4096]{0:T(1024)} %bitcast.23, s32[2048]{0:T(1024)} %multiply_add_fusion.fine_parents, s32[1]{0:T(128)} %bitcast.4.place, bf16[4096,256]{1,0:T(8,128)(2,1)} %all-gather.6.cloned.1.call-done.coarse, ...), custom_call_target="tpu_custom_call" | custom-call | flops 1000000000 | bytes 1048576 | tf_op jit(solution)/shard_map/top_layer/pallas_call | solution.py:222
  (22 shorter events, 0.1 us)
Async XLA Ops:
  8.5 18.8 %copy-start.2 = (s32[2048]{0:T(1024)S(1)}, s32[2048]{0:T(1024)}, u32[]{:S(2)}) copy-start(s32[2048]{0:T(1024)} %param.24) | copy-start | bytes 24580
  8.5 18.8 %copy-start.3 = (s32[2048,1]{0,1:T(1,128)S(1)}, s32[2048,1]{0,1:T(1,128)}, u32[]{:S(2)}) copy-start(s32[2048,1]{0,1:T(1,128)} %param.23) | copy-start | bytes 24580
  16.9 11.0 %collective-permute-start = (bf16[512,256]{1,0:T(8,128)(2,1)S(1)}, bf16[512,256]{1,0:T(8,128)(2,1)S(1)}, u32[]{:S(2)}, u32[]{:S(2)}) collective-permute-start(bf16[512,256]{1,0:T(8,128)(2,1)S(1)} %get-tuple-element.13), channel_id=1, source_target_pairs={{0,16},{16,32},{32,48},{48,64},{64,80},{80,96},{96,112},{112,128},... | collective-permute-start | bytes 786440 | tf_op jit(solution)/shard_map/ppermute | solution.py:237
  20.4 9.7 %collective-permute-start.1 = (bf16[512,256]{1,0:T(8,128)(2,1)S(1)}, bf16[512,256]{1,0:T(8,128)(2,1)S(1)}, u32[]{:S(2)}, u32[]{:S(2)}) collective-permute-start(bf16[512,256]{1,0:T(8,128)(2,1)S(1)} %get-tuple-element.12), channel_id=1, source_target_pairs={{16,0},{32,16},{48,32},{64,48},{80,64},{96,80},{112,96},{128,112},... | collective-permute-start | bytes 786440 | tf_op jit(solution)/shard_map/ppermute | solution.py:237
  21.7 8.4 %collective-permute-start.2 = (bf16[512,256]{1,0:T(8,128)(2,1)S(1)}, bf16[512,256]{1,0:T(8,128)(2,1)S(1)}, u32[]{:S(2)}, u32[]{:S(2)}) collective-permute-start(bf16[512,256]{1,0:T(8,128)(2,1)S(1)} %get-tuple-element.11), channel_id=1, source_target_pairs={{0,1},{1,2},{2,3},{3,4},{4,5},{5,6},{6,7},{7,8},{8,9},{9,10},{10,1... | collective-permute-start | bytes 786440 | tf_op jit(solution)/shard_map/ppermute | solution.py:237
  23.6 7.5 %collective-permute-start.3 = (bf16[512,256]{1,0:T(8,128)(2,1)S(1)}, bf16[512,256]{1,0:T(8,128)(2,1)S(1)}, u32[]{:S(2)}, u32[]{:S(2)}) collective-permute-start(bf16[512,256]{1,0:T(8,128)(2,1)S(1)} %get-tuple-element.10), channel_id=1, source_target_pairs={{1,0},{2,1},{3,2},{4,3},{5,4},{6,5},{7,6},{8,7},{9,8},{10,9},{11,1... | collective-permute-start | bytes 786440 | tf_op jit(solution)/shard_map/ppermute | solution.py:237
  27.9 3.3 copy-start.5
  30.0 1.1 copy-start.6
  30.0 1.1 copy-start.7
  31.1 0.7 copy-start.8
  94.6 8.3 %copy-start.9 = (u32[256]{0:T(256)S(1)}, u32[256]{0:T(256)}, u32[]{:S(2)}) copy-start(u32[256]{0:T(256)} %constant.49) | copy-start | bytes 3076
  94.6 98.0 %all-to-all-start = ((bf16[16,256,256]{2,1,0:T(8,128)(2,1)}), bf16[16,256,256]{2,1,0:T(8,128)(2,1)S(1)}, u32[]{:S(2)}, u32[]{:S(2)}) async-start(bf16[16,256,256]{2,1,0:T(8,128)(2,1)} %bitcast.21), calls=%async_computation | async-start | bytes 4194304 | tf_op jit(solution)/shard_map/all_to_all | solution.py:291
  102.9 142.9 %all-gather.4.cloned.1.call-start = ((), (), s32[]{:S(2)}) async-start(), calls=%async_computation.1 | async-start | bytes 2228224 | tf_op jit(solution)/shard_map/all_gather | solution.py:297
  193.0 52.7 %copy-start = (bf16[256,256]{1,0:T(8,128)(2,1)}, bf16[256,256]{1,0:T(8,128)(2,1)S(1)}, u32[]{:S(2)}) copy-start(bf16[256,256]{1,0:T(8,128)(2,1)S(1)} %divide_convert_fusion.states) | copy-start | bytes 393220
  193.0 59.5 %copy-start.4 = (s32[1,256]{1,0:T(1,128)S(1)}, s32[1,256]{1,0:T(1,128)}, u32[]{:S(2)}) copy-start(s32[1,256]{1,0:T(1,128)} %param.27) | copy-start | bytes 3076
  194.9 107.2 %all-gather.6.cloned.1.call-start = ((), (), s32[]{:S(2)}) async-start(), calls=%async_computation.2 | async-start | bytes 2228224 | tf_op jit(solution)/shard_map/all_gather | solution.py:308
  275.2 26.9 %copy-start.1 = (s32[1,4096]{1,0:T(1,128)}, s32[1,4096]{1,0:T(1,128)S(1)}, u32[]{:S(2)}) copy-start(s32[1,4096]{1,0:T(1,128)S(1)} %all-gather.parent_row) | copy-start | bytes 49156
Sparse Core Ops, SparseCore 0:
  195.0 50.7 all-gather.3
  252.7 49.3 all-gather.5

commit v2 on v1

--- a/solution.py
+++ b/solution.py
@@ -1,4 +1,4 @@
-import functools
+import math
 
 import jax
 import jax.numpy as jnp
@@ -122,16 +122,15 @@
 
 
 def fine_kernel(
-    senders, receivers, nodes, halo0, halo1, halo2, halo3, weights, gains, target_row, parent_row,
+    senders, receivers, nodes, halo, weights, gains, target_row, parent_row,
     fine_one, pooled, table, terms, sums, hidden, total,
 ):
     rows = nodes.shape[0]
-    halo = halo0.shape[0]
     project_rows(nodes, weights[0], table, 0, rows, 256)
     project_rows(nodes, weights[1], terms, 0, rows, 256)
     terms[pl.ds(2 * rows, 8), :] = jnp.zeros((8, LANES), F32)
-    for slot, part in enumerate((halo0, halo1, halo2, halo3)):
-        spread_rows(part, table, rows + slot * halo, halo, 64)
+    for slot in range(4):
+        spread_rows(halo.at[slot], table, rows + slot * halo.shape[1], halo.shape[1], 64)
     pass_edges(senders, receivers, target_row, table, terms, sums, hidden, total, rows, 1024, 256)
 
     @pl.loop(0, rows // 256)
@@ -141,10 +140,12 @@
 
     parents = parent_row[...]
 
-    @pl.loop(0, pooled.shape[0] // 256)
-    def _(t):
-        begin = pl.multiple_of(t * 256, 256)
-        pooled[pl.ds(begin, 256), :] = dot(one_hot(parents, begin, 256), fine_one[...]).astype(BF16)
+    across, block = pooled.shape[1], pooled.shape[2]
+
+    @pl.loop(0, pooled.shape[0] * across)
+    def _(t):
+        summed = dot(one_hot(parents, t * block, block), fine_one[...])
+        pooled[t // across, lax.rem(t, across)] = summed.astype(BF16)
 
 
 def coarse_kernel(
@@ -160,7 +161,7 @@
 
 def top_kernel(
     senders, receivers, parents, fine_parents, place, coarse, fine_one, weights, gains, target_row,
-    parent_row, top_count,
+    parent_row,
     fine_state, coarse_state, coarse_pairs, table, terms, sums, hidden, total, top_zero,
 ):
     count = top_zero.shape[0]
@@ -171,9 +172,10 @@
     @pl.loop(0, count // 256)
     def _(t):
         begin = pl.multiple_of(t * 256, 256)
-        summed = dot(one_hot(above, begin, 256), coarse[...])
-        children = top_count[pl.ds(begin, 256), :]
-        top_zero[pl.ds(begin, 256), :] = (summed / jnp.maximum(children, 1.0)).astype(BF16)
+        chosen = one_hot(above, begin, 256)
+        summed = dot(chosen, coarse[...])
+        children = jnp.maximum(dot(chosen, jnp.ones((coarse.shape[0], LANES), BF16))[:, :1], 1.0)
+        top_zero[pl.ds(begin, 256), :] = (summed / children).astype(BF16)
 
     project_rows(top_zero, weights[0], table, 0, count, 256)
     project_rows(top_zero, weights[1], terms, 0, count, 256)
@@ -216,7 +218,282 @@
                 ).astype(BF16)
 
 
-def call(kernel, outs, scalars, arrays, scratch, name, flops=10**9):
+MESH = pl.DeviceIdType.MESH
+
+
+def step(place, by, span):
+    return lax.rem(place + by + span, span)
+
+
+def remote(source, target, sems, which, device):
+    return pltpu.make_async_remote_copy(
+        src_ref=source, dst_ref=target, send_sem=sems[0].at[which], recv_sem=sems[1].at[which],
+        device_id=device, device_id_type=MESH,
+    )
+
+
+def greet(devices):
+    barrier = pltpu.get_barrier_semaphore()
+    for device in devices:
+        pl.semaphore_signal(barrier, inc=1, device_id=device, device_id_type=MESH)
+    pl.semaphore_wait(barrier, len(devices))
+
+
+class Torus:
+    def __init__(self, side):
+        self.side = side
+        me = lax.axis_index("gx")
+        self.at = me // side, lax.rem(me, side)
+
+    def near(self, axis, by):
+        x, y = self.at
+        if axis == 0:
+            return {"gx": step(x, by, self.side) * self.side + y}
+        return {"gx": x * self.side + step(y, by, self.side)}
+
+    def neighbours(self):
+        return [self.near(axis, by) for axis in (0, 1) for by in (1, -1)]
+
+    def there(self, axis, by):
+        return step(self.at[axis], by, self.side)
+
+
+def exchange_kernel(
+    sent, counts, parents, halo, all_counts, all_parents, send_halo, recv_halo, send_count,
+    recv_count, send_parent, recv_parent,
+):
+    members, across = lax.axis_size("gx"), lax.axis_size("gy")
+    me, beside = lax.axis_index("gx"), lax.axis_index("gy")
+    ahead = {"gx": step(me, 1, members)}, {"gx": step(me, -1, members)}
+    aside = {"gy": step(beside, 1, across)}, {"gy": step(beside, -1, across)}
+    peers = [{"gx": step(me, by, members)} for by in range(1, members)]
+    greet(peers + list(aside))
+    copies = [
+        remote(sent.at[slot], halo.at[slot], (send_halo, recv_halo), slot, device)
+        for slot, device in enumerate(ahead + aside)
+    ]
+    for by, device in enumerate(peers):
+        goal = step(me, by + 1, members)
+        sems = send_count, recv_count
+        copies.append(remote(counts.at[goal], all_counts.at[me], sems, by, device))
+        sems = send_parent, recv_parent
+        copies.append(remote(parents.at[0], all_parents.at[me], sems, by, device))
+    for copy in copies:
+        copy.start()
+    all_counts[me] = counts[me]
+    all_parents[me] = parents[0]
+    for copy in copies:
+        copy.wait()
+
+
+def gather_around(torus, whole, sems):
+    rows = whole.shape[2]
+    half, quarter = rows // 2, rows // 4
+    opened = []
+
+    def begin(source, which, device):
+        copy = remote(source, source, sems, which, device)
+        copy.start()
+        opened.append(copy)
+        return copy
+
+    def block(first, one, two, low, length):
+        place = (one, two) if first == 0 else (two, one)
+        return whole.at[place[0], place[1], pl.ds(low, length)]
+
+    order = (0, -1, 1, 2)
+    def number(first, phase, way, forwarded, column):
+        return (((first * 2 + phase) * 2 + way) * 2 + forwarded) * 4 + column
+
+    ways = (1, -1)
+    outer, inner, onward = {}, {}, {}
+    for first in (0, 1):
+        low = first * half
+        for way in (0, 1):
+            mine = block(first, torus.at[first], torus.at[1 - first], low, half)
+            outer[first, way] = begin(
+                mine, number(first, 0, way, 0, 0), torus.near(first, ways[way])
+            )
+
+    def second(first, column):
+        low = first * half
+        for way in (0, 1):
+            held = block(
+                first, torus.there(first, order[column]), torus.at[1 - first], low, half
+            )
+            inner[first, way, column] = begin(
+                held, number(first, 1, way, 0, column), torus.near(1 - first, ways[way])
+            )
+
+    for first in (0, 1):
+        second(first, 0)
+    for way in (0, 1):
+        for first in (0, 1):
+            outer[first, way].wait_recv()
+            low = first * half + way * quarter
+            came = block(
+                first, torus.there(first, -ways[way]), torus.at[1 - first], low, quarter
+            )
+            onward[first, way] = begin(
+                came, number(first, 0, way, 1, 0), torus.near(first, ways[way])
+            )
+            second(first, way + 1)
+    for first in (0, 1):
+        for way in (0, 1):
+            onward[first, way].wait_recv()
+        second(first, 3)
+    last = []
+    for column in range(4):
+        for way in (0, 1):
+            for first in (0, 1):
+                inner[first, way, column].wait_recv()
+                low = first * half + way * quarter
+                came = block(
+                    first, torus.there(first, order[column]),
+                    torus.there(1 - first, -ways[way]), low, quarter,
+                )
+                last.append(
+                    begin(
+                        came, number(first, 1, way, 1, column),
+                        torus.near(1 - first, ways[way]),
+                    )
+                )
+    for copy in last:
+        copy.wait_recv()
+    for copy in opened:
+        copy.wait_send()
+
+
+def collect_kernel(
+    pooled, all_counts, weights, coarse_zero, gathered,
+    passing, joined, arrived, partial, passing2, joined2, arrived2,
+    send_sum, recv_sum, send_all, recv_all,
+):
+    torus = Torus(pooled.shape[0])
+    greet(torus.neighbours())
+    rows = pooled.shape[2]
+    half, quarter = rows // 2, rows // 4
+    ways = (1, -1)
+    opened = []
+
+    def begin(source, target, which, device):
+        copy = remote(source, target, (send_sum, recv_sum), which, device)
+        copy.start()
+        opened.append(copy)
+        return copy
+
+    def share(first, goal, low):
+        if first == 0:
+            return pooled.at[goal, :, pl.ds(low, quarter)]
+        return pooled.at[:, goal, pl.ds(low, quarter)]
+
+    firsts = (1, 0)
+    far, plain, summed = {}, {}, {}
+    for way in (0, 1):
+        for part in (0, 1):
+            first = firsts[part]
+            far[part, way] = begin(
+                share(first, torus.there(first, 2), part * half + way * quarter),
+                passing.at[part, way], part * 2 + way, torus.near(first, ways[way]),
+            )
+    for way in (0, 1):
+        for part in (0, 1):
+            first = firsts[part]
+            plain[part, way] = begin(
+                share(first, torus.there(first, ways[way]), part * half + (1 - way) * quarter),
+                arrived.at[part, way, :, pl.ds((1 - way) * quarter, quarter)],
+                4 + part * 2 + way, torus.near(first, ways[way]),
+            )
+    for way in (0, 1):
+        for part in (0, 1):
+            first = firsts[part]
+            far[part, way].wait_recv()
+            mine = share(first, torus.there(first, ways[way]), part * half + way * quarter)
+            joined[part, way] = (
+                mine[...].astype(F32) + passing[part, way].astype(F32)
+            ).astype(BF16)
+            summed[part, way] = begin(
+                joined.at[part, way],
+                arrived.at[part, way, :, pl.ds(way * quarter, quarter)],
+                8 + part * 2 + way, torus.near(first, ways[way]),
+            )
+    for part in (0, 1):
+        for way in (0, 1):
+            plain[part, way].wait_recv()
+        for way in (0, 1):
+            summed[part, way].wait_recv()
+        for way in (0, 1):
+            first = firsts[part]
+            own = share(first, torus.at[first], part * half + way * quarter)
+            cut = pl.ds(way * quarter, quarter)
+            partial[part, :, cut] = (
+                own[...].astype(F32)
+                + arrived[part, 0, :, cut].astype(F32)
+                + arrived[part, 1, :, cut].astype(F32)
+            ).astype(BF16)
+        second = 1 - firsts[part]
+        for way in (0, 1):
+            cut = pl.ds(way * quarter, quarter)
+            far[part, way] = begin(
+                partial.at[part, torus.there(second, 2), cut], passing2.at[part, way],
+                12 + part * 2 + way, torus.near(second, ways[way]),
+            )
+        for way in (0, 1):
+            cut = pl.ds((1 - way) * quarter, quarter)
+            plain[part, way] = begin(
+                partial.at[part, torus.there(second, ways[way]), cut],
+                arrived2.at[part, way, cut], 16 + part * 2 + way,
+                torus.near(second, ways[way]),
+            )
+    for part in (0, 1):
+        second = 1 - firsts[part]
+        for way in (0, 1):
+            cut = pl.ds(way * quarter, quarter)
+            far[part, way].wait_recv()
+            joined2[part, way] = (
+                partial[part, torus.there(second, ways[way]), cut].astype(F32)
+                + passing2[part, way].astype(F32)
+            ).astype(BF16)
+            summed[part, way] = begin(
+                joined2.at[part, way], arrived2.at[part, way, cut], 20 + part * 2 + way,
+                torus.near(second, ways[way]),
+            )
+    total_count = jnp.sum(all_counts[...], axis=(0, 1)).reshape(1, rows)
+    square = (rows, rows)
+    diagonal = lax.broadcasted_iota(jnp.int32, square, 0) == lax.broadcasted_iota(
+        jnp.int32, square, 1
+    )
+    children = jnp.maximum(
+        jnp.sum(jnp.where(diagonal, total_count, 0.0), axis=1, keepdims=True), 1.0
+    )
+    x, y = torus.at
+    for part in (0, 1):
+        second = 1 - firsts[part]
+        for way in (0, 1):
+            plain[part, way].wait_recv()
+            summed[part, way].wait_recv()
+        whole = (
+            partial[part, torus.at[second]].astype(F32)
+            + arrived2[part, 0].astype(F32)
+            + arrived2[part, 1].astype(F32)
+        )
+        mean = (whole / children[part * half : (part + 1) * half]).astype(BF16)
+        coarse_zero[pl.ds(part * half, half), :] = mean
+        gathered[x, y, pl.ds(part * half, half)] = dot(mean, weights[0]).astype(BF16)
+    for copy in opened:
+        copy.wait_send()
+    gather_around(torus, gathered, (send_all, recv_all))
+
+
+def share_kernel(block, whole, send_all, recv_all):
+    torus = Torus(whole.shape[0])
+    x, y = torus.at
+    whole[x, y] = block[...]
+    greet(torus.neighbours())
+    gather_around(torus, whole, (send_all, recv_all))
+
+
+def call(kernel, outs, scalars, arrays, scratch, name, collective=None):
     in_specs = [pl.BlockSpec(memory_space=SMEM)] * len(scalars)
     in_specs += [pl.BlockSpec(memory_space=VMEM)] * len(arrays)
     return pl.pallas_call(
@@ -225,16 +502,13 @@
         in_specs=in_specs,
         out_specs=jax.tree.map(lambda _: pl.BlockSpec(memory_space=VMEM), outs),
         scratch_shapes=scratch,
-        compiler_params=pltpu.CompilerParams(vmem_limit_bytes=56 << 20),
-        cost_estimate=pl.CostEstimate(flops=flops, bytes_accessed=1 << 20, transcendentals=0),
+        compiler_params=pltpu.CompilerParams(
+            vmem_limit_bytes=56 << 20, collective_id=collective,
+            has_side_effects=collective is not None,
+        ),
+        cost_estimate=pl.CostEstimate(flops=10**9, bytes_accessed=1 << 20, transcendentals=0),
         name=name,
     )(*scalars, *arrays)
-
-
-def passed_along(block, axis, distance):
-    devices = range(lax.axis_size(axis))
-    route = [(i - distance, i) for i in devices if i - distance in devices]
-    return lax.ppermute(block, axis, route)
 
 
 def spread_counts(high, low, highs, lows):
@@ -264,56 +538,76 @@
     parent = owner * coarse_rows + pool_local
     parents = top_parent.reshape(-1)
 
+    side = math.isqrt(members)
     counts = spread_counts(owner, pool_local, members, coarse_rows)
-    child_count = lax.psum_scatter(counts, "gx", scatter_dimension=0, tiled=True).reshape(-1)
-    all_parents = lax.all_gather(parents, "gx", axis=0, tiled=True)
-    top_count = spread_counts(all_parents // 32, all_parents % 32, top_rows // 32, 32)
-    top_count = top_count.reshape(-1, 1)
+    dma = pltpu.SemaphoreType.DMA
 
     sent = call(
         send_kernel, shape(4 * halo), (lists,), (fine_nodes, fine_weights),
         [VMEM((2 * nodes, LANES), F32), VMEM((8 * halo, LANES), F32)], "send_rows",
     )
-    halos = [
-        passed_along(sent[slot * halo : (slot + 1) * halo], axis, offset)
-        for slot, (axis, offset) in enumerate((("gx", 1), ("gx", -1), ("gy", 1), ("gy", -1)))
-    ]
+    halos, all_counts, all_parents = call(
+        exchange_kernel,
+        (
+            jax.ShapeDtypeStruct((4, halo, width), BF16),
+            jax.ShapeDtypeStruct((members, 1, coarse_rows), F32),
+            jax.ShapeDtypeStruct((members, 1, coarse_rows), jnp.int32),
+        ),
+        (),
+        (
+            sent.reshape(4, halo, width), counts.reshape(members, 1, coarse_rows),
+            parents.reshape(1, 1, coarse_rows),
+        ),
+        [dma((4,))] * 2 + [dma((members - 1,))] * 4, "exchange", 0,
+    )
+    all_parents = all_parents.reshape(-1)
     edges = fine_sender.reshape(-1), fine_receiver.reshape(-1)
     fine_one, pooled = call(
-        fine_kernel, (shape(nodes), shape(coarse_all)), edges,
-        (fine_nodes, *halos, fine_weights, gains, edges[1][None, :], parent[None, :]),
+        fine_kernel,
+        (shape(nodes), jax.ShapeDtypeStruct((side, side, coarse_rows, width), BF16)), edges,
+        (fine_nodes, halos, fine_weights, gains, edges[1][None, :], parent[None, :]),
         [
             VMEM((2 * (nodes + 4 * halo), LANES), F32), VMEM((2 * nodes + 8, LANES), F32),
             VMEM((2048, LANES), F32), VMEM((1024, width), BF16), VMEM((nodes, width), F32),
         ],
         "fine_layer",
     )
-    arrived = lax.all_to_all(
-        pooled.reshape(members, coarse_rows, width), "gx", split_axis=0, concat_axis=0, tiled=True
-    )
-    coarse_sum = arrived.astype(F32).sum(axis=0)
-    coarse_zero = (coarse_sum / jnp.maximum(child_count, 1.0)[:, None]).astype(BF16)
-    coarse_send = dot(coarse_zero, coarse_weights[0]).astype(BF16)
-    gathered = lax.all_gather(coarse_send, "gx", axis=0, tiled=True)
+    half, quarter = coarse_rows // 2, coarse_rows // 4
+    coarse_zero, gathered = call(
+        collect_kernel,
+        (shape(coarse_rows), jax.ShapeDtypeStruct((side, side, coarse_rows, width), BF16)), (),
+        (pooled, all_counts, coarse_weights),
+        [
+            VMEM((2, 2, side, quarter, width), BF16), VMEM((2, 2, side, quarter, width), BF16),
+            VMEM((2, 2, side, half, width), BF16), VMEM((2, side, half, width), BF16),
+            VMEM((2, 2, quarter, width), BF16), VMEM((2, 2, quarter, width), BF16),
+            VMEM((2, 2, half, width), BF16),
+            dma((24,)), dma((24,)), dma((64,)), dma((64,)),
+        ],
+        "collect", 1,
+    )
     edges = coarse_sender.reshape(-1), coarse_receiver.reshape(-1)
     coarse_one = call(
         coarse_kernel, shape(coarse_rows), edges,
-        (coarse_zero, gathered, coarse_weights, gains, edges[1][None, :]),
+        (
+            coarse_zero, gathered.reshape(coarse_all, width), coarse_weights, gains,
+            edges[1][None, :],
+        ),
         [
             VMEM((2 * coarse_all, LANES), F32), VMEM((2 * coarse_rows, LANES), F32),
             VMEM((2048, LANES), F32), VMEM((1024, width), BF16), VMEM((coarse_rows, width), F32),
         ],
         "coarse_layer",
     )
-    coarse_whole = lax.all_gather(coarse_one, "gx", axis=0, tiled=True)
+    coarse_whole = call(
+        share_kernel, jax.ShapeDtypeStruct((side, side, coarse_rows, width), BF16), (),
+        (coarse_one,), [dma((64,)), dma((64,))], "share", 2,
+    ).reshape(coarse_all, width)
     edges = top_sender.reshape(-1), top_receiver.reshape(-1)
     place = lax.axis_index("gx").astype(jnp.int32).reshape(1)
     fine_state, coarse_state = call(
         top_kernel, (shape(nodes), shape(coarse_rows)), (*edges, all_parents, parent, place),
-        (
-            coarse_whole, fine_one, top_weights, gains, edges[1][None, :], all_parents[None, :],
-            top_count,
-        ),
+        (coarse_whole, fine_one, top_weights, gains, edges[1][None, :], all_parents[None, :]),
         [
             VMEM((2 * coarse_all, LANES), F32), VMEM((2 * top_rows, LANES), F32),
             VMEM((2 * top_rows, LANES), F32), VMEM((2048, LANES), F32), VMEM((1024, width), BF16),

time: 331 us -> 184 us (0.56)
  blocking collectives: 111 us -> 0 us
  Pallas kernels: 97.6 us -> 179 us
  waiting for transfers between devices: 79.8 us -> 0 us
  starting transfers between devices: 18.7 us -> 0 us
  between operations: 14.2 us -> 0.68 us
    unnamed x1 -> x0, blocking collectives: 87.9 us -> none
    pallas_call x4 -> x7, Pallas kernels: 97.6 us -> 179 us  [call(): pl.pallas_call(kernel, out_shape=outs, in_specs=in_specs, out_specs=jax.t...]
    all_gather x2 -> x0, waiting for transfers between devices: 76.5 us -> none  [the longest x1 50.8 us: body(): gathered = lax.all_gather(coarse_send, 'gx', axis=0, tiled=True)]
    all_gather x1 -> x0, blocking collectives: 22.6 us -> none  [body(): all_parents = lax.all_gather(parents, 'gx', axis=0, tiled=True)]
    ppermute x4 -> x0, starting transfers between devices: 10.3 us -> none  [passed_along(): return lax.ppermute(block, axis, route)]
    all_to_all x1 -> x0, starting transfers between devices: 8.23 us -> none  [body(): lax.all_to_all(pooled.reshape(members, coarse_rows, width), 'gx', split_a...]
  transfers between devices with their start and end apart: 7 -> 0, of which waited for: 4 -> 0; matrix products, arithmetic and copies ran while one was open for 1% -> 0% of each run, Pallas kernels for 0% -> 0%
where the time goes in v2:
time: 184 us
  Pallas kernels  179 us (97%)
  local copies, waits for them, and re-layouts  1.93 us (1%)
    pallas_call x7, Pallas kernels, call(): pl.pallas_call(kernel, out_shape=outs, in_specs=in_specs, out_specs=jax.t...  179 us

profile of v2, /device:TPU:96, one launch (start us, length us, event | category | flops | bytes accessed | tf_op | source)
XLA Modules:
  0.0 183.7 jit_solution(17135814747940741443)
XLA Ops:
  0.6 1.2 fusion
  1.8 0.6 reshape.50.counts
  2.5 1.3 copy.17
  3.8 7.1 %send_rows.1 = bf16[2048,256]{1,0:T(8,128)(2,1)} custom-call(s32[2048]{0:T(1024)} %bitcast.28, bf16[2048,256]{1,0:T(8,128)(2,1)} %nodes.3, bf16[6,256,256]{2,1,0:T(8,128)(2,1)} %weights.6), custom_call_target="tpu_custom_call" | custom-call | flops 1000000000 | bytes 1048576 | tf_op jit(solution)/shard_map/send_rows/pallas_call | solution.py:499
  10.9 0.0 copy-start
  10.9 0.0 copy-start.1
  10.9 17.3 %exchange.1 = (bf16[4,512,256]{2,1,0:T(8,128)(2,1)}, f32[16,1,256]{2,1,0:T(1,128)}, s32[16,1,256]{2,1,0:T(1,128)}) custom-call(bf16[4,512,256]{2,1,0:T(8,128)(2,1)} %bitcast.37, f32[16,1,256]{2,1,0:T(1,128)} %reshape.50.counts, s32[1,1,256]{2,1,0:T(1,128)} %bitcast.35), custom_call_target="tpu_custom_call" | custom-call | flops 1000000000 | bytes 1048576 | tf_op jit(solution)/shard_map/exchange/pallas_call | solution.py:499
  28.2 0.0 copy-done
  28.2 0.0 copy-done.1
  28.2 0.6 multiply_add_fusion.fine_parents
  28.8 62.8 %fine_layer.1 = (bf16[2048,256]{1,0:T(8,128)(2,1)}, bf16[4,4,256,256]{3,2,1,0:T(8,128)(2,1)}) custom-call(s32[8192]{0:T(1024)} %bitcast.30, s32[8192]{0:T(1024)} %bitcast.31, bf16[2048,256]{1,0:T(8,128)(2,1)} %nodes.3, bf16[4,512,256]{2,1,0:T(8,128)(2,1)} %get-tuple-element.12.halo, bf16[6,256,256]{2,1,0:T(8,128)(2,1)} %weights.6, f32[3,256]{1,0:T(4,128)} %gains.5, ...), custom_call_target="tpu_custom_call" | custom-call | flops 1000000000 | bytes 1048576 | tf_op jit(solution)/shard_map/fine_layer/pallas_call | solution.py:499
  91.6 41.2 %collect.1 = (bf16[256,256]{1,0:T(8,128)(2,1)}, bf16[4,4,256,256]{3,2,1,0:T(8,128)(2,1)}) custom-call(bf16[4,4,256,256]{3,2,1,0:T(8,128)(2,1)} %get-tuple-element.13.pooled, f32[16,1,256]{2,1,0:T(1,128)} %get-tuple-element.14.all_counts, bf16[6,256,256]{2,1,0:T(8,128)(2,1)} %weights.8), custom_call_target="tpu_custom_call" | custom-call | flops 1000000000 | bytes 1048576 | tf_op jit(solution)/shard_map/collect/pallas_call | solution.py:499
  132.8 6.8 %coarse_layer.1.block = bf16[256,256]{1,0:T(8,128)(2,1)} custom-call(s32[1024]{0:T(1024)} %bitcast.33, s32[1024]{0:T(1024)} %bitcast.34, bf16[256,256]{1,0:T(8,128)(2,1)} %get-tuple-element.15.states, bf16[4096,256]{1,0:T(8,128)(2,1)} %bitcast.36, bf16[6,256,256]{2,1,0:T(8,128)(2,1)} %weights.8, f32[3,256]{1,0:T(4,128)} %gains.5, s32[1,1024]{1,0:T(1,128)} %target_row.2), custom_call_target="tpu_custom_call" | custom-call | flops 1000000000 | bytes 1048576 | tf_op jit(solution)/shard_map/coarse_layer/pallas_call | solution.py:499
  139.6 22.1 %share.1 = bf16[4,4,256,256]{3,2,1,0:T(8,128)(2,1)} custom-call(bf16[256,256]{1,0:T(8,128)(2,1)} %coarse_layer.1.block), custom_call_target="tpu_custom_call" | custom-call | flops 1000000000 | bytes 1048576 | tf_op jit(solution)/shard_map/share/pallas_call | solution.py:499
  161.8 22.0 %top_layer.1 = (bf16[2048,256]{1,0:T(8,128)(2,1)}, bf16[256,256]{1,0:T(8,128)(2,1)}) custom-call(s32[2048]{0:T(1024)} %bitcast.24, s32[2048]{0:T(1024)} %bitcast.22, s32[4096]{0:T(1024)} %bitcast.20, s32[2048]{0:T(1024)} %multiply_add_fusion.fine_parents, s32[1]{0:T(128)} %bitcast.6.place, bf16[4096,256]{1,0:T(8,128)(2,1)} %bitcast.19, ...), custom_call_target="tpu_custom_call" | custom-call | flops 1000000000 | bytes 1048576 | tf_op jit(solution)/shard_map/top_layer/pallas_call | solution.py:499
Async XLA Ops:
  10.9 17.3 %copy-start = (s32[2048]{0:T(1024)S(1)}, s32[2048]{0:T(1024)}, u32[]{:S(2)}) copy-start(s32[2048]{0:T(1024)} %param.24) | copy-start | bytes 24580
  10.9 17.3 %copy-start.1 = (s32[2048,1]{0,1:T(1,128)S(1)}, s32[2048,1]{0,1:T(1,128)}, u32[]{:S(2)}) copy-start(s32[2048,1]{0,1:T(1,128)} %param.23) | copy-start | bytes 24580

commit v3 on v1

v3 whole, which is shorter than its diff:
```python
import math

import jax
import jax.numpy as jnp
from jax import lax
from jax.experimental import pallas as pl
from jax.experimental.pallas import tpu as pltpu
from jax.sharding import PartitionSpec as P

F32 = jnp.float32
BF16 = jnp.bfloat16
LANES = 128
VMEM = pltpu.VMEM
SMEM = pltpu.SMEM


def silu(v):
    half = 0.5 * v
    return half + half * jnp.tanh(half)


def dot(a, b):
    return jnp.dot(a, b, preferred_element_type=F32)


def put_rows(pairs, begin, rows, value):
    pairs[pl.ds(2 * begin, rows, stride=2), :] = value[:, :LANES]
    pairs[pl.ds(2 * begin + 1, rows, stride=2), :] = value[:, LANES:]


def get_rows(pairs, begin, rows):
    left = pairs[pl.ds(2 * begin, rows, stride=2), :]
    right = pairs[pl.ds(2 * begin + 1, rows, stride=2), :]
    return left, right


def project_rows(states, weight, pairs, at, rows, block):
    @pl.loop(0, rows // block)
    def _(t):
        begin = pl.multiple_of(t * block, block)
        term = dot(states[pl.ds(begin, block), :], weight).astype(BF16).astype(F32)
        put_rows(pairs, at + begin, block, term)


def spread_rows(table, pairs, at, rows, block):
    @pl.loop(0, rows // block)
    def _(t):
        begin = pl.multiple_of(t * block, block)
        put_rows(pairs, at + begin, block, table[pl.ds(begin, block), :].astype(F32))


def pick_some(at, edges, group, out, pick):
    for begin in range(0, edges, group):
        found = [pick(begin + u) for u in range(group)]
        for u in range(0, group, 4):
            to = pl.multiple_of(2 * (at + begin + u), 8)
            out[pl.ds(to, 8), :] = jnp.concatenate(found[u : u + 4], axis=0)


def pick_pairs(edges, unroll, out, pick):
    @pl.loop(0, edges // unroll)
    def _(t):
        begin = t * unroll
        pick_some(begin, unroll, 16, out, lambda u: pick(begin + u))


def pair(table, twice):
    return table[pl.ds(pl.multiple_of(twice, 2), 2), :]


def one_hot(targets, begin, rows):
    shape = (rows, targets.shape[1])
    return jnp.where(
        lax.broadcasted_iota(jnp.int32, shape, 0) + begin == targets, 1.0, 0.0
    ).astype(BF16)


def activate(sums, hidden, begin, rows):
    left, right = get_rows(sums, begin, rows)
    hidden[pl.ds(begin, rows), :LANES] = silu(left).astype(BF16)
    hidden[pl.ds(begin, rows), LANES:] = silu(right).astype(BF16)


def pass_edges(pick, target_row, sums, hidden, total, edges, chunk):
    count = total.shape[0]
    chunks = edges // chunk

    def ready(c, slot):
        pick_some(0, chunk, 16, sums, lambda u: pick(c * chunk + u))
        activate(sums, hidden.at[slot], 0, chunk)

    def summed(c, slot):
        targets = target_row[:, pl.ds(pl.multiple_of(c * chunk, chunk), chunk)]
        return dot(one_hot(targets, 0, count), hidden[slot])

    ready(0, 0)
    total[...] = jnp.zeros_like(total)

    if chunks > 1:
        @pl.loop(1, chunks)
        def _(c):
            slot = lax.rem(c, 2)
            total[...] += summed(c - 1, 1 - slot)
            ready(c, slot)

    total[...] += summed(chunks - 1, (chunks - 1) % 2)


def update(states, total, weights, gain, begin, rows):
    h = states[pl.ds(begin, rows), :]
    aggregate = dot(total[pl.ds(begin, rows), :].astype(BF16), weights[2]).astype(BF16)
    inner = silu(dot(h, weights[3]) + dot(aggregate, weights[4])).astype(BF16)
    output = dot(inner, weights[5])
    centred = output - jnp.mean(output, axis=1, keepdims=True)
    spread = jnp.mean(centred * centred, axis=1, keepdims=True)
    return (h.astype(F32) + gain * centred * lax.rsqrt(spread + 1e-05)).astype(BF16)


def fine_kernel(
    senders, receivers, nodes, halo, weights, gains, target_row,
    fine_one, table, terms, sums, hidden, total,
):
    rows = nodes.shape[0]
    project_rows(nodes, weights[0], table, 0, rows, rows)
    project_rows(nodes, weights[1], terms, 0, rows, rows)
    terms[pl.ds(2 * rows, 8), :] = jnp.zeros((8, LANES), F32)
    for slot in range(4):
        spread_rows(halo.at[slot], table, rows + slot * halo.shape[1], halo.shape[1], 64)
    pass_edges(
        lambda e: pair(table, senders[0, e]) + pair(terms, receivers[0, e]),
        target_row, sums, hidden, total, target_row.shape[1], 1024,
    )
    fine_one[...] = update(nodes, total, weights, gains[0:1, :], 0, rows)


def coarse_kernel(
    senders, receivers, states, gathered, weights, gains, target_row,
    out, table, terms, sums, hidden, total,
):
    rows = states.shape[0]
    spread_rows(gathered, table, 0, gathered.shape[0], 64)
    project_rows(states, weights[1], terms, 0, rows, 256)
    pass_edges(
        lambda e: pair(table, 2 * senders[e]) + pair(terms, 2 * receivers[e]),
        target_row, sums, hidden, total, target_row.shape[1], 1024,
    )
    out[...] = update(states, total, weights, gains[1:2, :], 0, rows)


def top_kernel(
    senders, receivers, parents, fine_parents, place, coarse, fine_one, weights, gains, target_row,
    parent_row,
    fine_state, coarse_state, coarse_pairs, table, terms, sums, hidden, total, top_zero,
):
    count = top_zero.shape[0]
    own = coarse_state.shape[0]
    spread_rows(coarse, coarse_pairs, 0, coarse.shape[0], 64)
    above = parent_row[...]

    @pl.loop(0, count // 256)
    def _(t):
        begin = pl.multiple_of(t * 256, 256)
        chosen = one_hot(above, begin, 256)
        summed = dot(chosen, coarse[...])
        children = jnp.maximum(dot(chosen, jnp.ones((coarse.shape[0], LANES), BF16))[:, :1], 1.0)
        top_zero[pl.ds(begin, 256), :] = (summed / children).astype(BF16)

    project_rows(top_zero, weights[0], table, 0, count, 512)
    project_rows(top_zero, weights[1], terms, 0, count, 512)
    pass_edges(
        lambda e: pair(table, 2 * senders[e]) + pair(terms, 2 * receivers[e]),
        target_row, sums, hidden, total, target_row.shape[1], 1024,
    )
    put_rows(table, 0, count, update(top_zero, total, weights, gains[2:3, :], 0, count).astype(F32))

    def lift(parent):
        return pair(coarse_pairs, 2 * parent) + pair(table, 2 * parents[parent])

    first = place[0] * own
    pick_pairs(own, 32, sums, lambda e: lift(first + e))
    left, right = get_rows(sums, 0, own)
    coarse_state[:, :LANES] = left.astype(BF16)
    coarse_state[:, LANES:] = right.astype(BF16)
    chunk = sums.shape[0] // 2

    @pl.loop(0, fine_one.shape[0] // chunk)
    def _(c):
        pick_pairs(chunk, 64, sums, lambda e: lift(fine_parents[c * chunk + e]))

        @pl.loop(0, chunk // 256)
        def _(t):
            begin = pl.multiple_of(t * 256, 256)
            to = pl.multiple_of(c * chunk + begin, 256)
            left, right = get_rows(sums, begin, 256)
            for value, at in ((left, 0), (right, LANES)):
                own_part = fine_one[pl.ds(to, 256), at : at + LANES].astype(F32)
                fine_state[pl.ds(to, 256), at : at + LANES] = (
                    own_part + value.astype(BF16).astype(F32)
                ).astype(BF16)


MESH = pl.DeviceIdType.MESH


def step(place, by, span):
    return lax.rem(place + by + span, span)


def remote(source, target, sems, which, device):
    return pltpu.make_async_remote_copy(
        src_ref=source, dst_ref=target, send_sem=sems[0].at[which], recv_sem=sems[1].at[which],
        device_id=device, device_id_type=MESH,
    )


WAYS = (1, -1, 2)


def greet_first(devices):
    barrier = pltpu.get_barrier_semaphore()
    for device in devices:
        pl.semaphore_signal(barrier, inc=1, device_id=device, device_id_type=MESH)


def greet_last(devices):
    pl.semaphore_wait(pltpu.get_barrier_semaphore(), len(devices))


class Torus:
    def __init__(self, side):
        self.side = side
        me = lax.axis_index("gx")
        self.at = me // side, lax.rem(me, side)

    def near(self, axis, by):
        x, y = self.at
        if axis == 0:
            return {"gx": step(x, by, self.side) * self.side + y}
        return {"gx": x * self.side + step(y, by, self.side)}

    def ring(self):
        return [self.near(axis, by) for axis in (0, 1) for by in WAYS]

    def there(self, axis, by):
        return step(self.at[axis], by, self.side)


def send_kernel(
    lists, nodes, weights, owners, locals_, senders, receivers,
    sent, counts, twice_senders, twice_receivers, pairs, picked,
):
    by_owner = one_hot(owners[...], 0, counts.shape[0])
    by_local = one_hot(locals_[...], 0, counts.shape[2])
    found = lax.dot_general(
        by_owner, by_local, (((1,), (1,)), ((), ())), preferred_element_type=F32
    )
    for member in range(counts.shape[0]):
        counts[member] = found[member : member + 1]
    rows = nodes.shape[0]
    project_rows(nodes, weights[0], pairs, 0, rows, rows)
    twice_senders[...] = 2 * senders[...]
    twice_receivers[...] = 2 * receivers[...]
    length = lists.shape[1]
    for slot in range(lists.shape[0]):
        pick_pairs(length, 64, picked.at[slot], lambda e: pair(pairs, 2 * lists[slot, e]))
        left, right = get_rows(picked.at[slot], 0, length)
        sent[slot, :, :LANES] = left.astype(BF16)
        sent[slot, :, LANES:] = right.astype(BF16)


def exchange_kernel(
    sent, counts, parents,
    halo, all_counts, all_parents,
    send_halo, recv_halo, send_count, recv_count, send_parent, recv_parent,
):
    members, across = lax.axis_size("gx"), lax.axis_size("gy")
    me, beside = lax.axis_index("gx"), lax.axis_index("gy")
    ahead = {"gx": step(me, 1, members)}, {"gx": step(me, -1, members)}
    aside = {"gy": step(beside, 1, across)}, {"gy": step(beside, -1, across)}
    peers = [{"gx": step(me, by, members)} for by in range(1, members)]
    greet_first(peers + list(aside))
    greet_last(peers + list(aside))
    copies = [
        remote(sent.at[slot], halo.at[slot], (send_halo, recv_halo), slot, device)
        for slot, device in enumerate(ahead + aside)
    ]
    for by, device in enumerate(peers):
        goal = step(me, by + 1, members)
        sems = send_count, recv_count
        copies.append(remote(counts.at[goal], all_counts.at[me], sems, by, device))
        sems = send_parent, recv_parent
        copies.append(remote(parents.at[0], all_parents.at[me], sems, by, device))
    for copy in copies:
        copy.start()
    all_counts[me] = counts[me]
    all_parents[me] = parents[0]
    for copy in copies:
        copy.wait()


class Gathering:
    def __init__(self, torus, whole, sems):
        self.torus, self.whole, self.sems = torus, whole, sems
        self.half = whole.shape[2] // 2
        self.opened, self.outer, self.inner = [], {}, {}

    def block(self, first, one, two):
        x, y = (one, two) if first == 0 else (two, one)
        return self.whole.at[x, y, pl.ds(first * self.half, self.half)]

    def send(self, first, axis, held, which, way):
        copy = remote(
            held, held, self.sems, (first * 5 + which) * 3 + way,
            self.torus.near(axis, WAYS[way]),
        )
        copy.start()
        self.opened.append(copy)
        return copy

    def begin(self, first):
        torus = self.torus
        held = self.block(first, torus.at[first], torus.at[1 - first])
        for way in range(3):
            self.outer[first, way] = self.send(first, first, held, 0, way)
        self.pass_on(first, 0)

    def pass_on(self, first, column):
        torus = self.torus
        one = torus.at[first] if column == 0 else torus.there(first, -WAYS[column - 1])
        held = self.block(first, one, torus.at[1 - first])
        for way in range(3):
            self.inner[first, column, way] = self.send(first, 1 - first, held, 1 + column, way)

    def finish(self):
        for way in range(3):
            for first in (0, 1):
                self.outer[first, way].wait_recv()
                self.pass_on(first, 1 + way)
        for column in range(4):
            for way in range(3):
                for first in (0, 1):
                    self.inner[first, column, way].wait_recv()
        for copy in self.opened:
            copy.wait_send()


def collect_kernel(
    fine_one, parent_row, all_counts, weights, coarse_zero, gathered,
    pooled, kept, arrived, partial, arrived2, send_sum, recv_sum, send_all, recv_all,
):
    torus = Torus(gathered.shape[0])
    side, rows = torus.side, gathered.shape[2]
    half = rows // 2
    greet_first(torus.ring())
    parents = parent_row[...]
    opened, first_hop, second_hop = [], {}, {}

    def share(part, goal):
        begins = [
            (k * side + goal if part == 0 else goal * side + k) * rows + part * half
            for k in range(side)
        ]
        chosen = jnp.concatenate([one_hot(parents, begin, half) for begin in begins], axis=0)
        return dot(chosen, fine_one[...]).reshape(side, half, 2 * LANES)

    for way in (2, 0, 1):
        for part in (0, 1):
            axis = 1 - part
            pooled[part, way] = share(part, torus.there(axis, WAYS[way])).astype(BF16)
            if (way, part) == (2, 0):
                greet_last(torus.ring())
            copy = remote(
                pooled.at[part, way], arrived.at[part, way], (send_sum, recv_sum),
                part * 3 + way, torus.near(axis, WAYS[way]),
            )
            copy.start()
            opened.append(copy)
            first_hop[part, way] = copy
    for part in (0, 1):
        kept[part] = share(part, torus.at[1 - part])
    for part in (0, 1):
        for way in range(3):
            first_hop[part, way].wait_recv()
        partial[part] = (
            kept[part]
            + arrived[part, 0].astype(F32)
            + arrived[part, 1].astype(F32)
            + arrived[part, 2].astype(F32)
        ).astype(BF16)
        for way in range(3):
            copy = remote(
                partial.at[part, torus.there(part, WAYS[way])], arrived2.at[part, way],
                (send_sum, recv_sum), 6 + part * 3 + way, torus.near(part, WAYS[way]),
            )
            copy.start()
            opened.append(copy)
            second_hop[part, way] = copy
    total_count = jnp.sum(all_counts[...], axis=(0, 1)).reshape(1, rows)
    square = (rows, rows)
    diagonal = lax.broadcasted_iota(jnp.int32, square, 0) == lax.broadcasted_iota(
        jnp.int32, square, 1
    )
    children = jnp.maximum(
        jnp.sum(jnp.where(diagonal, total_count, 0.0), axis=1, keepdims=True), 1.0
    )
    x, y = torus.at
    gathering = Gathering(torus, gathered, (send_all, recv_all))
    for part in (0, 1):
        for way in range(3):
            second_hop[part, way].wait_recv()
        whole = (
            partial[part, torus.at[part]].astype(F32)
            + arrived2[part, 0].astype(F32)
            + arrived2[part, 1].astype(F32)
            + arrived2[part, 2].astype(F32)
        )
        mean = (whole / children[part * half : (part + 1) * half]).astype(BF16)
        coarse_zero[pl.ds(part * half, half), :] = mean
        gathered[x, y, pl.ds(part * half, half)] = dot(mean, weights[0]).astype(BF16)
        gathering.begin(part)
    gathering.finish()
    for copy in opened:
        copy.wait_send()


def share_kernel(block, whole, send_all, recv_all):
    torus = Torus(whole.shape[0])
    x, y = torus.at
    greet_first(torus.ring())
    whole[x, y] = block[...]
    greet_last(torus.ring())
    gathering = Gathering(torus, whole, (send_all, recv_all))
    gathering.begin(0)
    gathering.begin(1)
    gathering.finish()


def call(kernel, outs, scalars, arrays, scratch, name, collective=None):
    in_specs = [pl.BlockSpec(memory_space=SMEM)] * len(scalars)
    in_specs += [pl.BlockSpec(memory_space=VMEM)] * len(arrays)
    return pl.pallas_call(
        kernel,
        out_shape=outs,
        in_specs=in_specs,
        out_specs=jax.tree.map(lambda _: pl.BlockSpec(memory_space=VMEM), outs),
        scratch_shapes=scratch,
        compiler_params=pltpu.CompilerParams(
            vmem_limit_bytes=56 << 20, collective_id=collective,
            has_side_effects=collective is not None,
        ),
        cost_estimate=pl.CostEstimate(flops=10**9, bytes_accessed=1 << 20, transcendentals=0),
        name=name,
    )(*scalars, *arrays)


def shape(rows, width=256, dtype=BF16):
    return jax.ShapeDtypeStruct((rows, width), dtype)


def body(
    fine_nodes, fine_weights, coarse_weights, top_weights, gains, send_list, fine_sender,
    fine_receiver, pool_owner, pool_local, coarse_sender, coarse_receiver, top_parent, top_sender,
    top_receiver,
):
    nodes = fine_nodes.shape[0]
    width = fine_nodes.shape[1]
    members = lax.axis_size("gx")
    coarse_rows = nodes // 8
    coarse_all = coarse_rows * members
    top_rows = coarse_all // 8
    lists = send_list.reshape(4, -1)
    halo = lists.shape[1]
    owner = pool_owner.reshape(1, -1)
    local = pool_local.reshape(1, -1)
    parent = owner * coarse_rows + local
    parents = top_parent.reshape(1, 1, -1)
    senders = fine_sender.reshape(1, -1)
    receivers = fine_receiver.reshape(1, -1)
    side = math.isqrt(members)
    dma = pltpu.SemaphoreType.DMA
    whole = jax.ShapeDtypeStruct((side, side, coarse_rows, width), BF16)
    gather_sems = [dma((30,)), dma((30,))]
    ints = jnp.int32

    rows16 = jax.ShapeDtypeStruct((members, 1, coarse_rows), F32)
    halo_shape = jax.ShapeDtypeStruct((4, halo, width), BF16)
    doubled = shape(1, senders.shape[1], ints)
    sent, counts, twice_senders, twice_receivers = call(
        send_kernel, (halo_shape, rows16, doubled, doubled), (lists,),
        (fine_nodes, fine_weights, owner, local, senders, receivers),
        [VMEM((2 * nodes, LANES), F32), VMEM((4, 2 * halo, LANES), F32)],
        "send_rows",
    )
    halos, all_counts, all_parents = call(
        exchange_kernel,
        (halo_shape, rows16, jax.ShapeDtypeStruct((members, 1, coarse_rows), ints)),
        (), (sent, counts, parents),
        [dma((4,))] * 2 + [dma((members - 1,))] * 4,
        "exchange", 0,
    )
    all_parents = all_parents.reshape(-1)
    fine_one = call(
        fine_kernel, shape(nodes), (twice_senders, twice_receivers),
        (fine_nodes, halos, fine_weights, gains, receivers),
        [
            VMEM((2 * (nodes + 4 * halo), LANES), F32), VMEM((2 * nodes + 8, LANES), F32),
            VMEM((2048, LANES), F32), VMEM((2, 1024, width), BF16), VMEM((nodes, width), F32),
        ],
        "fine_layer",
    )
    half = coarse_rows // 2
    coarse_zero, gathered = call(
        collect_kernel, (shape(coarse_rows), whole), (),
        (fine_one, parent, all_counts, coarse_weights),
        [
            VMEM((2, 3, side, half, width), BF16), VMEM((2, side, half, width), F32),
            VMEM((2, 3, side, half, width), BF16), VMEM((2, side, half, width), BF16),
            VMEM((2, 3, half, width), BF16),
            dma((12,)), dma((12,)), *gather_sems,
        ],
        "collect", 1,
    )
    edges = coarse_sender.reshape(-1), coarse_receiver.reshape(-1)
    coarse_one = call(
        coarse_kernel, shape(coarse_rows), edges,
        (
            coarse_zero, gathered.reshape(coarse_all, width), coarse_weights, gains,
            edges[1][None, :],
        ),
        [
            VMEM((2 * coarse_all, LANES), F32), VMEM((2 * coarse_rows, LANES), F32),
            VMEM((2048, LANES), F32), VMEM((2, 1024, width), BF16), VMEM((coarse_rows, width), F32),
        ],
        "coarse_layer",
    )
    coarse_whole = call(
        share_kernel, whole, (), (coarse_one,), gather_sems, "share", 2,
    ).reshape(coarse_all, width)
    edges = top_sender.reshape(-1), top_receiver.reshape(-1)
    place = lax.axis_index("gx").astype(jnp.int32).reshape(1)
    fine_state, coarse_state = call(
        top_kernel, (shape(nodes), shape(coarse_rows)), (*edges, all_parents, parent.reshape(-1), place),
        (coarse_whole, fine_one, top_weights, gains, edges[1][None, :], all_parents[None, :]),
        [
            VMEM((2 * coarse_all, LANES), F32), VMEM((2 * top_rows, LANES), F32),
            VMEM((2 * top_rows, LANES), F32), VMEM((2048, LANES), F32), VMEM((2, 1024, width), BF16),
            VMEM((top_rows, width), F32), VMEM((top_rows, width), BF16),
        ],
        "top_layer",
    )
    return (fine_state, coarse_state[None])


def solution(mesh):
    placed = (
        P(("gx", "gy"), None), P(), P(), P(), P(),
        P("gx", "gy", None, None), P("gx", "gy", None), P("gx", "gy", None),
        P(("gx", "gy"), None), P(("gx", "gy")),
        P("gy", "gx"), P("gy", "gx"), P("gy", "gx"), P("gy", None), P("gy", None),
    )
    return jax.shard_map(
        body,
        mesh=mesh,
        in_specs=placed,
        out_specs=(P(("gx", "gy"), None), P("gy", "gx", None)),
        check_vma=False,
    )
```

time: 331 us -> 137 us (0.41)
  blocking collectives: 111 us -> 0 us
  waiting for transfers between devices: 79.8 us -> 0 us
  Pallas kernels: 97.6 us -> 134 us
  starting transfers between devices: 18.7 us -> 0 us
  between operations: 14.2 us -> 0.66 us
  local copies, waits for them, and re-layouts: 4.83 us -> 0 us
    unnamed x1 -> x0, blocking collectives: 87.9 us -> none
    all_gather x2 -> x0, waiting for transfers between devices: 76.5 us -> none  [the longest x1 50.8 us: body(): gathered = lax.all_gather(coarse_send, 'gx', axis=0, tiled=True)]
    pallas_call x4 -> x7, Pallas kernels: 97.6 us -> 134 us  [call(): pl.pallas_call(kernel, out_shape=outs, in_specs=in_specs, out_specs=jax.t...]
    all_gather x1 -> x0, blocking collectives: 22.6 us -> none  [body(): all_parents = lax.all_gather(parents, 'gx', axis=0, tiled=True)]
    ppermute x4 -> x0, starting transfers between devices: 10.3 us -> none  [passed_along(): return lax.ppermute(block, axis, route)]
    all_to_all x1 -> x0, starting transfers between devices: 8.23 us -> none  [body(): lax.all_to_all(pooled.reshape(members, coarse_rows, width), 'gx', split_a...]
  transfers between devices with their start and end apart: 7 -> 0, of which waited for: 4 -> 0; matrix products, arithmetic and copies ran while one was open for 1% -> 0% of each run, Pallas kernels for 0% -> 0%
where the time goes in v3:
time: 137 us; the launch traced here: 136 us
  Pallas kernels  134 us (98%)
  other arithmetic  2 us (1%)
    pallas_call x7, Pallas kernels, call(): pl.pallas_call(kernel, out_shape=outs, in_specs=in_specs, out_specs=jax.t...  134 us

profile of v3, /device:TPU:96, one launch (start us, length us, event | category | flops | bytes accessed | tf_op | source)
XLA Modules:
  0.0 136.3 jit_solution(6398745801537469294)
XLA Ops:
  0.6 0.7 broadcast_multiply_fusion
  1.3 1.3 add.5.fine_parents
  2.6 8.3 %send_rows.1 = (bf16[4,512,256]{2,1,0:T(8,128)(2,1)}, f32[16,1,256]{2,1,0:T(1,128)}, s32[1,8192]{1,0:T(1,128)}, s32[1,8192]{1,0:T(1,128)}) custom-call(s32[4,512]{1,0:T(4,128)} %bitcast.31, bf16[2048,256]{1,0:T(8,128)(2,1)} %nodes.3, bf16[6,256,256]{2,1,0:T(8,128)(2,1)} %weights.6, s32[1,2048]{1,0:T(1,128)} %bitcast.28, s32[1,2048]{1,0:T(1,128)} %bitcast.27, ...), custom_call_target="tpu_custom_call" | custom-call | flops 1000000000 | bytes 1048576 | tf_op jit(solution)/shard_map/send_rows/pallas_call | solution.py:441
  10.9 17.3 %exchange.1 = (bf16[4,512,256]{2,1,0:T(8,128)(2,1)}, f32[16,1,256]{2,1,0:T(1,128)}, s32[16,1,256]{2,1,0:T(1,128)}) custom-call(bf16[4,512,256]{2,1,0:T(8,128)(2,1)} %get-tuple-element.13.sent, f32[16,1,256]{2,1,0:T(1,128)} %get-tuple-element.14.counts, s32[1,1,256]{2,1,0:T(1,128)} %bitcast.34), custom_call_target="tpu_custom_call" | custom-call | flops 1000000000 | bytes 1048576 | tf_op jit(solution)/shard_map/exchange/pallas_call | solution.py:441
  28.2 23.1 %fine_layer.1.fine_one = bf16[2048,256]{1,0:T(8,128)(2,1)} custom-call(s32[1,8192]{1,0:T(1,128)} %get-tuple-element.16.senders, s32[1,8192]{1,0:T(1,128)} %get-tuple-element.17.receivers, bf16[2048,256]{1,0:T(8,128)(2,1)} %nodes.3, bf16[4,512,256]{2,1,0:T(8,128)(2,1)} %get-tuple-element.18.halo, bf16[6,256,256]{2,1,0:T(8,128)(2,1)} %weights.6, ...), custom_call_target="tpu_custom_call" | custom-call | flops 1000000000 | bytes 1048576 | tf_op jit(solution)/shard_map/fine_layer/pallas_call | solution.py:441
  51.3 41.5 %collect.1 = (bf16[256,256]{1,0:T(8,128)(2,1)}, bf16[4,4,256,256]{3,2,1,0:T(8,128)(2,1)}) custom-call(bf16[2048,256]{1,0:T(8,128)(2,1)} %fine_layer.1.fine_one, s32[1,2048]{1,0:T(1,128)} %bitcast.24, f32[16,1,256]{2,1,0:T(1,128)} %get-tuple-element.19.all_counts, bf16[6,256,256]{2,1,0:T(8,128)(2,1)} %weights.8), custom_call_target="tpu_custom_call" | custom-call | flops 1000000000 | bytes 1048576 | tf_op jit(solution)/shard_map/collect/pallas_call | solution.py:441
  92.8 6.1 %coarse_layer.1.block = bf16[256,256]{1,0:T(8,128)(2,1)} custom-call(s32[1024]{0:T(1024)} %bitcast.32, s32[1024]{0:T(1024)} %bitcast.33, bf16[256,256]{1,0:T(8,128)(2,1)} %get-tuple-element.20.states, bf16[4096,256]{1,0:T(8,128)(2,1)} %bitcast.35, bf16[6,256,256]{2,1,0:T(8,128)(2,1)} %weights.8, f32[3,256]{1,0:T(4,128)} %gains.5, s32[1,1024]{1,0:T(1,128)} %target_row.2), custom_call_target="tpu_custom_call" | custom-call | flops 1000000000 | bytes 1048576 | tf_op jit(solution)/shard_map/coarse_layer/pallas_call | solution.py:441
  98.9 20.4 %share.1 = bf16[4,4,256,256]{3,2,1,0:T(8,128)(2,1)} custom-call(bf16[256,256]{1,0:T(8,128)(2,1)} %coarse_layer.1.block), custom_call_target="tpu_custom_call" | custom-call | flops 1000000000 | bytes 1048576 | tf_op jit(solution)/shard_map/share/pallas_call | solution.py:441
  119.3 17.0 %top_layer.1 = (bf16[2048,256]{1,0:T(8,128)(2,1)}, bf16[256,256]{1,0:T(8,128)(2,1)}) custom-call(s32[2048]{0:T(1024)} %bitcast.26, s32[2048]{0:T(1024)} %bitcast.23, s32[4096]{0:T(1024)} %bitcast.19, s32[2048]{0:T(1024)} %add.5.fine_parents, s32[1]{0:T(128)} %bitcast.10.place, bf16[4096,256]{1,0:T(8,128)(2,1)} %bitcast.18, ...), custom_call_target="tpu_custom_call" | custom-call | flops 1000000000 | bytes 1048576 | tf_op jit(solution)/shard_map/top_layer/pallas_call | solution.py:441

commit v4 on v3

--- a/solution.py
+++ b/solution.py
@@ -125,7 +125,7 @@
     project_rows(nodes, weights[1], terms, 0, rows, rows)
     terms[pl.ds(2 * rows, 8), :] = jnp.zeros((8, LANES), F32)
     for slot in range(4):
-        spread_rows(halo.at[slot], table, rows + slot * halo.shape[1], halo.shape[1], 64)
+        spread_rows(halo.at[slot], table, rows + slot * halo.shape[1], halo.shape[1], 512)
     pass_edges(
         lambda e: pair(table, senders[0, e]) + pair(terms, receivers[0, e]),
         target_row, sums, hidden, total, target_row.shape[1], 1024,
@@ -134,11 +134,10 @@
 
 
 def coarse_kernel(
-    senders, receivers, states, gathered, weights, gains, target_row,
-    out, table, terms, sums, hidden, total,
+    senders, receivers, states, table, weights, gains, target_row,
+    out, terms, sums, hidden, total,
 ):
     rows = states.shape[0]
-    spread_rows(gathered, table, 0, gathered.shape[0], 64)
     project_rows(states, weights[1], terms, 0, rows, 256)
     pass_edges(
         lambda e: pair(table, 2 * senders[e]) + pair(terms, 2 * receivers[e]),
@@ -148,23 +147,12 @@
 
 
 def top_kernel(
-    senders, receivers, parents, fine_parents, place, coarse, fine_one, weights, gains, target_row,
-    parent_row,
-    fine_state, coarse_state, coarse_pairs, table, terms, sums, hidden, total, top_zero,
+    senders, receivers, twice_parents, fine_parents, place, coarse_pairs, top_zero, fine_one,
+    weights, gains, target_row,
+    fine_state, coarse_state, table, terms, sums, hidden, total,
 ):
     count = top_zero.shape[0]
     own = coarse_state.shape[0]
-    spread_rows(coarse, coarse_pairs, 0, coarse.shape[0], 64)
-    above = parent_row[...]
-
-    @pl.loop(0, count // 256)
-    def _(t):
-        begin = pl.multiple_of(t * 256, 256)
-        chosen = one_hot(above, begin, 256)
-        summed = dot(chosen, coarse[...])
-        children = jnp.maximum(dot(chosen, jnp.ones((coarse.shape[0], LANES), BF16))[:, :1], 1.0)
-        top_zero[pl.ds(begin, 256), :] = (summed / children).astype(BF16)
-
     project_rows(top_zero, weights[0], table, 0, count, 512)
     project_rows(top_zero, weights[1], terms, 0, count, 512)
     pass_edges(
@@ -174,7 +162,7 @@
     put_rows(table, 0, count, update(top_zero, total, weights, gains[2:3, :], 0, count).astype(F32))
 
     def lift(parent):
-        return pair(coarse_pairs, 2 * parent) + pair(table, 2 * parents[parent])
+        return pair(coarse_pairs, 2 * parent) + pair(table, twice_parents[parent])
 
     first = place[0] * own
     pick_pairs(own, 32, sums, lambda e: lift(first + e))
@@ -245,32 +233,10 @@
         return step(self.at[axis], by, self.side)
 
 
-def send_kernel(
-    lists, nodes, weights, owners, locals_, senders, receivers,
-    sent, counts, twice_senders, twice_receivers, pairs, picked,
-):
-    by_owner = one_hot(owners[...], 0, counts.shape[0])
-    by_local = one_hot(locals_[...], 0, counts.shape[2])
-    found = lax.dot_general(
-        by_owner, by_local, (((1,), (1,)), ((), ())), preferred_element_type=F32
-    )
-    for member in range(counts.shape[0]):
-        counts[member] = found[member : member + 1]
-    rows = nodes.shape[0]
-    project_rows(nodes, weights[0], pairs, 0, rows, rows)
-    twice_senders[...] = 2 * senders[...]
-    twice_receivers[...] = 2 * receivers[...]
-    length = lists.shape[1]
-    for slot in range(lists.shape[0]):
-        pick_pairs(length, 64, picked.at[slot], lambda e: pair(pairs, 2 * lists[slot, e]))
-        left, right = get_rows(picked.at[slot], 0, length)
-        sent[slot, :, :LANES] = left.astype(BF16)
-        sent[slot, :, LANES:] = right.astype(BF16)
-
-
 def exchange_kernel(
-    sent, counts, parents,
-    halo, all_counts, all_parents,
+    lists, nodes, weights, owners, locals_, parents, senders, receivers,
+    halo, all_counts, all_parents, twice_parents, twice_senders, twice_receivers, fine_parents,
+    rows3, picked, sent, counts,
     send_halo, recv_halo, send_count, recv_count, send_parent, recv_parent,
 ):
     members, across = lax.axis_size("gx"), lax.axis_size("gy")
@@ -279,23 +245,51 @@
     aside = {"gy": step(beside, 1, across)}, {"gy": step(beside, -1, across)}
     peers = [{"gx": step(me, by, members)} for by in range(1, members)]
     greet_first(peers + list(aside))
-    greet_last(peers + list(aside))
-    copies = [
-        remote(sent.at[slot], halo.at[slot], (send_halo, recv_halo), slot, device)
-        for slot, device in enumerate(ahead + aside)
-    ]
+    term = dot(nodes[...], weights[0]).astype(BF16).astype(F32)
+    rows3[:, 0, :] = term[:, :LANES]
+    rows3[:, 1, :] = term[:, LANES:]
+    length = lists.shape[1]
+    copies = []
+    for slot, device in enumerate(ahead + aside):
+
+        @pl.loop(0, length // 32)
+        def _(t):
+            begin = t * 32
+            found = [rows3[lists[slot, begin + u]] for u in range(32)]
+            for u in range(32):
+                picked[slot, begin + u] = found[u]
+
+        sent[slot, :, :LANES] = picked[slot, :, 0, :].astype(BF16)
+        sent[slot, :, LANES:] = picked[slot, :, 1, :].astype(BF16)
+        if slot == 0:
+            greet_last(peers + list(aside))
+        copy = remote(sent.at[slot], halo.at[slot], (send_halo, recv_halo), slot, device)
+        copy.start()
+        copies.append(copy)
+    for by, device in enumerate(peers):
+        sems = send_parent, recv_parent
+        copies.append(remote(parents.at[0], all_parents.at[me], sems, by, device))
+        copies[-1].start()
+    by_owner = one_hot(owners[...], 0, members)
+    by_local = one_hot(locals_[...], 0, counts.shape[2])
+    found = lax.dot_general(
+        by_owner, by_local, (((1,), (1,)), ((), ())), preferred_element_type=F32
+    )
+    for member in range(members):
+        counts[member] = found[member : member + 1]
     for by, device in enumerate(peers):
         goal = step(me, by + 1, members)
         sems = send_count, recv_count
         copies.append(remote(counts.at[goal], all_counts.at[me], sems, by, device))
-        sems = send_parent, recv_parent
-        copies.append(remote(parents.at[0], all_parents.at[me], sems, by, device))
-    for copy in copies:
-        copy.start()
+        copies[-1].start()
     all_counts[me] = counts[me]
     all_parents[me] = parents[0]
+    twice_senders[...] = 2 * senders[...]
+    twice_receivers[...] = 2 * receivers[...]
+    fine_parents[...] = owners[...] * counts.shape[2] + locals_[...]
     for copy in copies:
         copy.wait()
+    twice_parents[...] = 2 * all_parents[...]
 
 
 class Gathering:
@@ -317,6 +311,13 @@
         self.opened.append(copy)
         return copy
 
+    def widen(self, pairs, first, one, two):
+        x, y = (one, two) if first == 0 else (two, one)
+        side, rows = self.torus.side, self.whole.shape[2]
+        begin = (x * side + y) * rows + first * self.half
+        value = self.whole[x, y, pl.ds(first * self.half, self.half)].astype(F32)
+        put_rows(pairs, begin, self.half, value)
+
     def begin(self, first):
         torus = self.torus
         held = self.block(first, torus.at[first], torus.at[1 - first])
@@ -324,29 +325,40 @@
             self.outer[first, way] = self.send(first, first, held, 0, way)
         self.pass_on(first, 0)
 
+    def place(self, first, column):
+        torus = self.torus
+        return torus.at[first] if column == 0 else torus.there(first, -WAYS[column - 1])
+
     def pass_on(self, first, column):
-        torus = self.torus
-        one = torus.at[first] if column == 0 else torus.there(first, -WAYS[column - 1])
-        held = self.block(first, one, torus.at[1 - first])
+        held = self.block(first, self.place(first, column), self.torus.at[1 - first])
         for way in range(3):
             self.inner[first, column, way] = self.send(first, 1 - first, held, 1 + column, way)
 
-    def finish(self):
+    def finish(self, pairs, after=lambda column: None):
+        torus = self.torus
         for way in range(3):
             for first in (0, 1):
                 self.outer[first, way].wait_recv()
                 self.pass_on(first, 1 + way)
         for column in range(4):
+            for first in (0, 1):
+                self.widen(pairs, first, self.place(first, column), torus.at[1 - first])
             for way in range(3):
                 for first in (0, 1):
                     self.inner[first, column, way].wait_recv()
+                    self.widen(
+                        pairs, first, self.place(first, column),
+                        torus.there(1 - first, -WAYS[way]),
+                    )
+            after(column)
         for copy in self.opened:
             copy.wait_send()
 
 
 def collect_kernel(
-    fine_one, parent_row, all_counts, weights, coarse_zero, gathered,
-    pooled, kept, arrived, partial, arrived2, send_sum, recv_sum, send_all, recv_all,
+    fine_one, parent_row, all_counts, all_parents, weights,
+    coarse_zero, pairs, top_count,
+    gathered, pooled, kept, arrived, partial, arrived2, send_sum, recv_sum, send_all, recv_all,
 ):
     torus = Torus(gathered.shape[0])
     side, rows = torus.side, gathered.shape[2]
@@ -378,6 +390,14 @@
             first_hop[part, way] = copy
     for part in (0, 1):
         kept[part] = share(part, torus.at[1 - part])
+    ones = jnp.ones((side * rows, LANES), BF16)
+    top_count[...] = jnp.zeros_like(top_count)
+
+    @pl.loop(0, side)
+    def _(k):
+        above = jnp.concatenate([all_parents[k * side + q] for q in range(side)], axis=1)
+        top_count[...] += dot(one_hot(above, 0, top_count.shape[0]), ones)
+
     for part in (0, 1):
         for way in range(3):
             first_hop[part, way].wait_recv()
@@ -418,13 +438,16 @@
         coarse_zero[pl.ds(part * half, half), :] = mean
         gathered[x, y, pl.ds(part * half, half)] = dot(mean, weights[0]).astype(BF16)
         gathering.begin(part)
-    gathering.finish()
+    gathering.finish(pairs)
     for copy in opened:
         copy.wait_send()
 
 
-def share_kernel(block, whole, send_all, recv_all):
+def share_kernel(
+    block, all_parents, top_count, pairs, top_zero, whole, total, send_all, recv_all
+):
     torus = Torus(whole.shape[0])
+    side, half = torus.side, whole.shape[2] // 2
     x, y = torus.at
     greet_first(torus.ring())
     whole[x, y] = block[...]
@@ -432,7 +455,22 @@
     gathering = Gathering(torus, whole, (send_all, recv_all))
     gathering.begin(0)
     gathering.begin(1)
-    gathering.finish()
+    total[...] = jnp.zeros_like(total)
+
+    def after(column):
+        at_x, at_y = gathering.place(0, column), gathering.place(1, column)
+        low, high = slice(0, half), slice(half, 2 * half)
+        above = [all_parents[at_x * side + k, :, low] for k in range(side)]
+        above += [all_parents[k * side + at_y, :, high] for k in range(side)]
+        states = [whole[at_x, k, low] for k in range(side)]
+        states += [whole[k, at_y, high] for k in range(side)]
+        chosen = one_hot(jnp.concatenate(above, axis=1), 0, total.shape[0])
+        total[...] += dot(chosen, jnp.concatenate(states, axis=0))
+
+    gathering.finish(pairs, after)
+    children = jnp.maximum(top_count[...], 1.0)
+    top_zero[:, :LANES] = (total[:, :LANES] / children).astype(BF16)
+    top_zero[:, LANES:] = (total[:, LANES:] / children).astype(BF16)
 
 
 def call(kernel, outs, scalars, arrays, scratch, name, collective=None):
@@ -445,7 +483,7 @@
         out_specs=jax.tree.map(lambda _: pl.BlockSpec(memory_space=VMEM), outs),
         scratch_shapes=scratch,
         compiler_params=pltpu.CompilerParams(
-            vmem_limit_bytes=56 << 20, collective_id=collective,
+            vmem_limit_bytes=40 << 20, collective_id=collective,
             has_side_effects=collective is not None,
         ),
         cost_estimate=pl.CostEstimate(flops=10**9, bytes_accessed=1 << 20, transcendentals=0),
@@ -472,33 +510,32 @@
     halo = lists.shape[1]
     owner = pool_owner.reshape(1, -1)
     local = pool_local.reshape(1, -1)
-    parent = owner * coarse_rows + local
     parents = top_parent.reshape(1, 1, -1)
     senders = fine_sender.reshape(1, -1)
     receivers = fine_receiver.reshape(1, -1)
     side = math.isqrt(members)
     dma = pltpu.SemaphoreType.DMA
-    whole = jax.ShapeDtypeStruct((side, side, coarse_rows, width), BF16)
     gather_sems = [dma((30,)), dma((30,))]
     ints = jnp.int32
-
     rows16 = jax.ShapeDtypeStruct((members, 1, coarse_rows), F32)
-    halo_shape = jax.ShapeDtypeStruct((4, halo, width), BF16)
+    ints16 = jax.ShapeDtypeStruct((members, 1, coarse_rows), ints)
     doubled = shape(1, senders.shape[1], ints)
-    sent, counts, twice_senders, twice_receivers = call(
-        send_kernel, (halo_shape, rows16, doubled, doubled), (lists,),
-        (fine_nodes, fine_weights, owner, local, senders, receivers),
-        [VMEM((2 * nodes, LANES), F32), VMEM((4, 2 * halo, LANES), F32)],
-        "send_rows",
-    )
-    halos, all_counts, all_parents = call(
+    pairs_shape = shape(2 * coarse_all, LANES, F32)
+
+    halos, all_counts, all_parents, twice_parents, twice_senders, twice_receivers, parent = call(
         exchange_kernel,
-        (halo_shape, rows16, jax.ShapeDtypeStruct((members, 1, coarse_rows), ints)),
-        (), (sent, counts, parents),
-        [dma((4,))] * 2 + [dma((members - 1,))] * 4,
+        (
+            jax.ShapeDtypeStruct((4, halo, width), BF16), rows16, ints16, ints16,
+            doubled, doubled, shape(1, nodes, ints),
+        ),
+        (lists,), (fine_nodes, fine_weights, owner, local, parents, senders, receivers),
+        [
+            VMEM((nodes, 2, LANES), F32), VMEM((4, halo, 2, LANES), F32),
+            VMEM((4, halo, width), BF16), VMEM((members, 1, coarse_rows), F32),
+        ]
+        + [dma((4,))] * 2 + [dma((members - 1,))] * 4,
         "exchange", 0,
     )
-    all_parents = all_parents.reshape(-1)
     fine_one = call(
         fine_kernel, shape(nodes), (twice_senders, twice_receivers),
         (fine_nodes, halos, fine_weights, gains, receivers),
@@ -509,10 +546,12 @@
         "fine_layer",
     )
     half = coarse_rows // 2
-    coarse_zero, gathered = call(
-        collect_kernel, (shape(coarse_rows), whole), (),
-        (fine_one, parent, all_counts, coarse_weights),
+    gathered = VMEM((side, side, coarse_rows, width), BF16)
+    coarse_zero, pairs, top_count = call(
+        collect_kernel, (shape(coarse_rows), pairs_shape, shape(top_rows, LANES, F32)), (),
+        (fine_one, parent, all_counts, all_parents, coarse_weights),
         [
+            gathered,
             VMEM((2, 3, side, half, width), BF16), VMEM((2, side, half, width), F32),
             VMEM((2, 3, side, half, width), BF16), VMEM((2, side, half, width), BF16),
             VMEM((2, 3, half, width), BF16),
@@ -523,28 +562,26 @@
     edges = coarse_sender.reshape(-1), coarse_receiver.reshape(-1)
     coarse_one = call(
         coarse_kernel, shape(coarse_rows), edges,
-        (
-            coarse_zero, gathered.reshape(coarse_all, width), coarse_weights, gains,
-            edges[1][None, :],
-        ),
+        (coarse_zero, pairs, coarse_weights, gains, edges[1][None, :]),
         [
-            VMEM((2 * coarse_all, LANES), F32), VMEM((2 * coarse_rows, LANES), F32),
-            VMEM((2048, LANES), F32), VMEM((2, 1024, width), BF16), VMEM((coarse_rows, width), F32),
+            VMEM((2 * coarse_rows, LANES), F32), VMEM((2048, LANES), F32),
+            VMEM((2, 1024, width), BF16), VMEM((coarse_rows, width), F32),
         ],
         "coarse_layer",
     )
-    coarse_whole = call(
-        share_kernel, whole, (), (coarse_one,), gather_sems, "share", 2,
-    ).reshape(coarse_all, width)
+    pairs, top_zero = call(
+        share_kernel, (pairs_shape, shape(top_rows)), (), (coarse_one, all_parents, top_count),
+        [gathered, VMEM((top_rows, width), F32), *gather_sems], "share", 2,
+    )
     edges = top_sender.reshape(-1), top_receiver.reshape(-1)
-    place = lax.axis_index("gx").astype(jnp.int32).reshape(1)
+    place = lax.axis_index("gx").astype(ints).reshape(1)
     fine_state, coarse_state = call(
-        top_kernel, (shape(nodes), shape(coarse_rows)), (*edges, all_parents, parent.reshape(-1), place),
-        (coarse_whole, fine_one, top_weights, gains, edges[1][None, :], all_parents[None, :]),
+        top_kernel, (shape(nodes), shape(coarse_rows)),
+        (*edges, twice_parents.reshape(-1), parent.reshape(-1), place),
+        (pairs, top_zero, fine_one, top_weights, gains, edges[1][None, :]),
         [
-            VMEM((2 * coarse_all, LANES), F32), VMEM((2 * top_rows, LANES), F32),
-            VMEM((2 * top_rows, LANES), F32), VMEM((2048, LANES), F32), VMEM((2, 1024, width), BF16),
-            VMEM((top_rows, width), F32), VMEM((top_rows, width), BF16),
+            VMEM((2 * top_rows, LANES), F32), VMEM((2 * top_rows, LANES), F32),
+            VMEM((2048, LANES), F32), VMEM((2, 1024, width), BF16), VMEM((top_rows, width), F32),
         ],
         "top_layer",
     )

time: 137 us -> 127 us (0.927)
  Pallas kernels: 134 us -> 116 us
  local copies, waits for them, and re-layouts: 0 us -> 9.72 us
  other arithmetic: 2 us -> 0 us
    pallas_call x7 -> x6, Pallas kernels: 134 us -> 116 us  [call(): pl.pallas_call(kernel, out_shape=outs, in_specs=in_specs, out_specs=jax.t...]
    unnamed x0 -> x34, local copies, waits for them, and re-layouts: none -> 9.72 us
where the time goes in v4:
time: 127 us; the launch traced here: 126 us
  Pallas kernels  116 us (91%)
  local copies, waits for them, and re-layouts  9.72 us (8%)
    pallas_call x6, Pallas kernels, call(): pl.pallas_call(kernel, out_shape=outs, in_specs=in_specs, out_specs=jax.t...  116 us
    unnamed x34, local copies, waits for them, and re-layouts  9.72 us

profile of v4, /device:TPU:96, one launch (start us, length us, event | category | flops | bytes accessed | tf_op | source)
XLA Modules:
  0.0 126.2 jit_solution(13461915150981219576)
XLA Ops:
  0.6 0.0 copy-start
  0.6 1.2 copy-done
  1.9 0.0 copy-start.3
  1.9 1.1 copy-done.3
  3.0 0.0 copy-start.7
  3.0 0.8 copy-done.7
  3.8 0.8 copy-done.12
  4.5 0.7 copy-done.13
  5.2 0.7 copy-done.14
  5.9 0.7 copy-done.15
  6.6 0.7 copy-done.16
  7.3 18.2 %exchange.1 = (bf16[4,512,256]{2,1,0:T(8,128)(2,1)S(1)}, f32[16,1,256]{2,1,0:T(1,128)S(1)}, s32[16,1,256]{2,1,0:T(1,128)S(1)}, s32[16,1,256]{2,1,0:T(1,128)S(1)}...) custom-call(s32[4,512]{1,0:T(4,128)S(1)} %bitcast.23, bf16[2048,256]{1,0:T(8,128)(2,1)S(1)} %copy-done, ...), custom_call_target="tpu_custom_call" | custom-call | flops 1000000000 | bytes 1048576 | tf_op jit(solution)/shard_map/exchange/pallas_call | solution.py:479
  25.5 0.0 copy-start.9
  25.5 0.0 copy-start.11
  25.5 0.0 copy-start.1
  25.5 1.2 copy-done.1
  26.7 1.1 copy-done.4
  27.9 0.7 copy-done.6
  28.6 21.7 %fine_layer.1.fine_one = bf16[2048,256]{1,0:T(8,128)(2,1)S(1)} custom-call(s32[1,8192]{1,0:T(1,128)S(1)} %get-tuple-element.18.senders, s32[1,8192]{1,0:T(1,128)S(1)} %get-tuple-element.19.receivers, bf16[2048,256]{1,0:T(8,128)(2,1)S(1)} %copy-done.1, bf16[4,512,256]{2,1,0:T(8,128)(2,1)S(1)} %get-tuple-element.20.halo, bf16[6,256,256]{2,1,0:T(8,128)(2,1)S(1)} %copy-done.4, ...), custom_call_target="tpu_custom_call" | custom-call | flops 1000000000 | bytes 1048576 | tf_op jit(solution)/shard_map/fine_layer/pallas_call | solution.py:479
  50.3 0.0 copy-done.2
  50.3 40.2 %collect.1 = (bf16[256,256]{1,0:T(8,128)(2,1)S(1)}, f32[8192,128]{1,0:T(8,128)S(1)}, f32[512,128]{1,0:T(8,128)S(1)}) custom-call(bf16[2048,256]{1,0:T(8,128)(2,1)S(1)} %fine_layer.1.fine_one, s32[1,2048]{1,0:T(1,128)S(1)} %get-tuple-element.17.parent_row, f32[16,1,256]{2,1,0:T(1,128)S(1)} %get-tuple-element.21.all_counts, ...), custom_call_target="tpu_custom_call" | custom-call | flops 1000000000 | bytes 1048576 | tf_op jit(solution)/shard_map/collect/pallas_call | solution.py:479
  90.5 0.0 copy-done.9
  90.5 0.0 copy-done.11
  90.5 0.0 copy-start.5
  90.5 0.0 copy-start.8
  90.6 0.0 copy-start.10
  90.6 3.5 %coarse_layer.1.block = bf16[256,256]{1,0:T(8,128)(2,1)S(1)} custom-call(s32[1024]{0:T(1024)S(1)} %bitcast.21, s32[1024]{0:T(1024)S(1)} %bitcast.18, bf16[256,256]{1,0:T(8,128)(2,1)S(1)} %get-tuple-element.23.states, f32[8192,128]{1,0:T(8,128)S(1)} %get-tuple-element.24.table, bf16[6,256,256]{2,1,0:T(8,128)(2,1)S(1)} %copy-done.2, f32[3,256]{1,0:T(4,128)S(1)} %copy-done.6, ...), custom_call_target="tpu_custom_call" | custom-call | flops 1000000000 | bytes 1048576 | tf_op jit(solution)/shard_map/coarse_layer/pallas_call | solution.py:479
  94.1 19.7 %share.1 = (f32[8192,128]{1,0:T(8,128)S(1)}, bf16[512,256]{1,0:T(8,128)(2,1)S(1)}) custom-call(bf16[256,256]{1,0:T(8,128)(2,1)S(1)} %coarse_layer.1.block, s32[16,1,256]{2,1,0:T(1,128)S(1)} %get-tuple-element.22.all_parents, f32[512,128]{1,0:T(8,128)S(1)} %get-tuple-element.25.top_count), custom_call_target="tpu_custom_call" | custom-call | flops 1000000000 | bytes 1048576 | tf_op jit(solution)/shard_map/share/pallas_call | solution.py:479
  113.7 0.0 copy-done.5
  113.8 0.0 copy-done.8
  113.8 0.0 copy-done.10
  113.8 12.5 %top_layer.1 = (bf16[2048,256]{1,0:T(8,128)(2,1)}, bf16[256,256]{1,0:T(8,128)(2,1)}) custom-call(s32[2048]{0:T(1024)S(1)} %bitcast.19, s32[2048]{0:T(1024)S(1)} %bitcast.16, s32[4096]{0:T(1024)S(1)} %bitcast.17, s32[2048]{0:T(1024)S(1)} %bitcast.20, s32[1]{0:T(128)} %bitcast.10.place, f32[8192,128]{1,0:T(8,128)S(1)} %get-tuple-element.26.coarse_pairs, ...), custom_call_target="tpu_custom_call" | custom-call | flops 1000000000 | bytes 1048576 | tf_op jit(solution)/shard_map/top_layer/pallas_call | solution.py:479
  (8 shorter events, 0.0 us)
Async XLA Ops:
  0.6 1.2 copy-start
  1.9 1.1 copy-start.3
  3.0 0.8 copy-start.7
  3.8 0.8 copy-start.12
  4.5 0.7 copy-start.13
  5.2 0.7 copy-start.14
  5.9 0.7 copy-start.15
  6.6 0.7 copy-start.16
  7.3 43.0 %copy-start.2 = (bf16[6,256,256]{2,1,0:T(8,128)(2,1)S(1)}, bf16[6,256,256]{2,1,0:T(8,128)(2,1)}, u32[]{:S(2)}) copy-start(bf16[6,256,256]{2,1,0:T(8,128)(2,1)} %weights.8) | copy-start | bytes 2359300
  25.5 65.0 %copy-start.9 = (s32[1,1024]{1,0:T(1,128)S(1)}, s32[1,1024]{1,0:T(1,128)}, u32[]{:S(2)}) copy-start(s32[1,1024]{1,0:T(1,128)} %target_row.2) | copy-start | bytes 12292
  25.5 65.0 %copy-start.11 = (s32[1,1024]{1,0:T(1,128)S(1)}, s32[1,1024]{1,0:T(1,128)}, u32[]{:S(2)}) copy-start(s32[1,1024]{1,0:T(1,128)} %param.25) | copy-start | bytes 12292
  25.5 1.2 copy-start.1
  26.7 1.1 copy-start.4
  27.9 0.7 copy-start.6
  90.5 23.2 %copy-start.5 = (bf16[6,256,256]{2,1,0:T(8,128)(2,1)S(1)}, bf16[6,256,256]{2,1,0:T(8,128)(2,1)}, u32[]{:S(2)}) copy-start(bf16[6,256,256]{2,1,0:T(8,128)(2,1)} %weights.9) | copy-start | bytes 2359300
  90.5 23.2 %copy-start.8 = (s32[1,2048]{1,0:T(1,128)S(1)}, s32[1,2048]{1,0:T(1,128)}, u32[]{:S(2)}) copy-start(s32[1,2048]{1,0:T(1,128)} %target_row.3) | copy-start | bytes 24580
  90.6 23.2 %copy-start.10 = (s32[1,2048]{1,0:T(1,128)S(1)}, s32[1,2048]{1,0:T(1,128)}, u32[]{:S(2)}) copy-start(s32[1,2048]{1,0:T(1,128)} %param.28) | copy-start | bytes 24580

commit v5 on v4

--- a/solution.py
+++ b/solution.py
@@ -117,33 +117,14 @@
 
 
 def fine_kernel(
-    senders, receivers, nodes, halo, weights, gains, target_row,
-    fine_one, table, terms, sums, hidden, total,
+    senders, receivers, table, terms, nodes, weights, gains, target_row,
+    fine_one, sums, hidden, total,
 ):
-    rows = nodes.shape[0]
-    project_rows(nodes, weights[0], table, 0, rows, rows)
-    project_rows(nodes, weights[1], terms, 0, rows, rows)
-    terms[pl.ds(2 * rows, 8), :] = jnp.zeros((8, LANES), F32)
-    for slot in range(4):
-        spread_rows(halo.at[slot], table, rows + slot * halo.shape[1], halo.shape[1], 512)
     pass_edges(
         lambda e: pair(table, senders[0, e]) + pair(terms, receivers[0, e]),
         target_row, sums, hidden, total, target_row.shape[1], 1024,
     )
-    fine_one[...] = update(nodes, total, weights, gains[0:1, :], 0, rows)
-
-
-def coarse_kernel(
-    senders, receivers, states, table, weights, gains, target_row,
-    out, terms, sums, hidden, total,
-):
-    rows = states.shape[0]
-    project_rows(states, weights[1], terms, 0, rows, 256)
-    pass_edges(
-        lambda e: pair(table, 2 * senders[e]) + pair(terms, 2 * receivers[e]),
-        target_row, sums, hidden, total, target_row.shape[1], 1024,
-    )
-    out[...] = update(states, total, weights, gains[1:2, :], 0, rows)
+    fine_one[...] = update(nodes, total, weights, gains[0:1, :], 0, nodes.shape[0])
 
 
 def top_kernel(
@@ -234,9 +215,11 @@
 
 
 def exchange_kernel(
-    lists, nodes, weights, owners, locals_, parents, senders, receivers,
-    halo, all_counts, all_parents, twice_parents, twice_senders, twice_receivers, fine_parents,
-    rows3, picked, sent, counts,
+    lists_far, nodes_far, weights_far, coarse_weights_far, top_weights_far, gains_far, owners_far, locals_far,
+    parents_far, senders_far, receivers_far, coarse_row_far, top_row_far,
+    table, terms, nodes, weights, coarse_weights, top_weights, gains, receivers, coarse_row,
+    top_row, all_counts, all_parents, twice_parents, twice_senders, twice_receivers, fine_parents,
+    lists, owners, locals_, parents, senders, rows3, picked, sent, halo, counts, fetched,
     send_halo, recv_halo, send_count, recv_count, send_parent, recv_parent,
 ):
     members, across = lax.axis_size("gx"), lax.axis_size("gy")
@@ -245,11 +228,28 @@
     aside = {"gy": step(beside, 1, across)}, {"gy": step(beside, -1, across)}
     peers = [{"gx": step(me, by, members)} for by in range(1, members)]
     greet_first(peers + list(aside))
+    wanted = (
+        (weights_far.at[0], weights.at[0]), (nodes_far, nodes), (parents_far, parents),
+        (owners_far, owners), (locals_far, locals_), (senders_far, senders),
+        (receivers_far, receivers), (weights_far.at[pl.ds(1, 5)], weights.at[pl.ds(1, 5)]),
+        (coarse_weights_far, coarse_weights), (top_weights_far, top_weights),
+        (gains_far, gains), (coarse_row_far, coarse_row), (top_row_far, top_row),
+        (lists_far, lists),
+    )
+    fetches = [
+        pltpu.make_async_copy(source, target, fetched.at[k])
+        for k, (source, target) in enumerate(wanted)
+    ]
+    for fetch in fetches:
+        fetch.start()
+    for k in (0, 1, 13):
+        fetches[k].wait()
+    rows = nodes.shape[0]
     term = dot(nodes[...], weights[0]).astype(BF16).astype(F32)
     rows3[:, 0, :] = term[:, :LANES]
     rows3[:, 1, :] = term[:, LANES:]
     length = lists.shape[1]
-    copies = []
+    halos, copies = [], []
     for slot, device in enumerate(ahead + aside):
 
         @pl.loop(0, length // 32)
@@ -265,11 +265,14 @@
             greet_last(peers + list(aside))
         copy = remote(sent.at[slot], halo.at[slot], (send_halo, recv_halo), slot, device)
         copy.start()
-        copies.append(copy)
+        halos.append(copy)
+    fetches[2].wait()
     for by, device in enumerate(peers):
         sems = send_parent, recv_parent
         copies.append(remote(parents.at[0], all_parents.at[me], sems, by, device))
         copies[-1].start()
+    fetches[3].wait()
+    fetches[4].wait()
     by_owner = one_hot(owners[...], 0, members)
     by_local = one_hot(locals_[...], 0, counts.shape[2])
     found = lax.dot_general(
@@ -284,9 +287,17 @@
         copies[-1].start()
     all_counts[me] = counts[me]
     all_parents[me] = parents[0]
+    fine_parents[...] = owners[...] * counts.shape[2] + locals_[...]
+    for fetch in fetches[5:13]:
+        fetch.wait()
+    put_rows(table, 0, rows, dot(nodes[...], weights[0]).astype(BF16).astype(F32))
+    project_rows(nodes, weights[1], terms, 0, rows, rows)
+    terms[pl.ds(2 * rows, 8), :] = jnp.zeros((8, LANES), F32)
     twice_senders[...] = 2 * senders[...]
     twice_receivers[...] = 2 * receivers[...]
-    fine_parents[...] = owners[...] * counts.shape[2] + locals_[...]
+    for slot, copy in enumerate(halos):
+        copy.wait()
+        put_rows(table, rows + slot * length, length, halo[slot].astype(F32))
     for copy in copies:
         copy.wait()
     twice_parents[...] = 2 * all_parents[...]
@@ -316,7 +327,11 @@
         side, rows = self.torus.side, self.whole.shape[2]
         begin = (x * side + y) * rows + first * self.half
         value = self.whole[x, y, pl.ds(first * self.half, self.half)].astype(F32)
-        put_rows(pairs, begin, self.half, value)
+        if len(pairs.shape) == 2:
+            put_rows(pairs, begin, self.half, value)
+        else:
+            pairs[pl.ds(begin, self.half), 0, :] = value[:, :LANES]
+            pairs[pl.ds(begin, self.half), 1, :] = value[:, LANES:]
 
     def begin(self, first):
         torus = self.torus
@@ -355,10 +370,12 @@
             copy.wait_send()
 
 
-def collect_kernel(
-    fine_one, parent_row, all_counts, all_parents, weights,
-    coarse_zero, pairs, top_count,
+def coarse_kernel(
+    senders, receivers, fine_one, parent_row, all_counts, all_parents, weights, gains, target_row,
+    pairs, top_zero,
+    coarse_zero, top_count, table3, terms3, sums, hidden, total, top_total, whole_one,
     gathered, pooled, kept, arrived, partial, arrived2, send_sum, recv_sum, send_all, recv_all,
+    send_one, recv_one,
 ):
     torus = Torus(gathered.shape[0])
     side, rows = torus.side, gathered.shape[2]
@@ -438,44 +455,45 @@
         coarse_zero[pl.ds(part * half, half), :] = mean
         gathered[x, y, pl.ds(part * half, half)] = dot(mean, weights[0]).astype(BF16)
         gathering.begin(part)
-    gathering.finish(pairs)
+    term = dot(coarse_zero[...], weights[1]).astype(BF16).astype(F32)
+    terms3[:, 0, :] = term[:, :LANES]
+    terms3[:, 1, :] = term[:, LANES:]
+    gathering.finish(table3)
     for copy in opened:
         copy.wait_send()
 
-
-def share_kernel(
-    block, all_parents, top_count, pairs, top_zero, whole, total, send_all, recv_all
-):
-    torus = Torus(whole.shape[0])
-    side, half = torus.side, whole.shape[2] // 2
-    x, y = torus.at
-    greet_first(torus.ring())
-    whole[x, y] = block[...]
-    greet_last(torus.ring())
-    gathering = Gathering(torus, whole, (send_all, recv_all))
-    gathering.begin(0)
-    gathering.begin(1)
-    total[...] = jnp.zeros_like(total)
+    edges = target_row.shape[1]
+    pick_pairs(edges, 32, sums, lambda e: table3[senders[e]] + terms3[receivers[e]])
+    activate(sums, hidden, 0, edges)
+    total[...] = dot(one_hot(target_row[...], 0, rows), hidden[...])
+    whole_one[x, y] = update(coarse_zero, total, weights, gains[1:2, :], 0, rows)
+
+    sharing = Gathering(torus, whole_one, (send_one, recv_one))
+    sharing.begin(0)
+    sharing.begin(1)
+    top_total[...] = jnp.zeros_like(top_total)
 
     def after(column):
-        at_x, at_y = gathering.place(0, column), gathering.place(1, column)
+        at_x, at_y = sharing.place(0, column), sharing.place(1, column)
         low, high = slice(0, half), slice(half, 2 * half)
         above = [all_parents[at_x * side + k, :, low] for k in range(side)]
         above += [all_parents[k * side + at_y, :, high] for k in range(side)]
-        states = [whole[at_x, k, low] for k in range(side)]
-        states += [whole[k, at_y, high] for k in range(side)]
-        chosen = one_hot(jnp.concatenate(above, axis=1), 0, total.shape[0])
-        total[...] += dot(chosen, jnp.concatenate(states, axis=0))
-
-    gathering.finish(pairs, after)
-    children = jnp.maximum(top_count[...], 1.0)
-    top_zero[:, :LANES] = (total[:, :LANES] / children).astype(BF16)
-    top_zero[:, LANES:] = (total[:, LANES:] / children).astype(BF16)
-
-
-def call(kernel, outs, scalars, arrays, scratch, name, collective=None):
+        states = [whole_one[at_x, k, low] for k in range(side)]
+        states += [whole_one[k, at_y, high] for k in range(side)]
+        chosen = one_hot(jnp.concatenate(above, axis=1), 0, top_total.shape[0])
+        top_total[...] += dot(chosen, jnp.concatenate(states, axis=0))
+
+    sharing.finish(pairs, after)
+    above = jnp.maximum(top_count[...], 1.0)
+    top_zero[:, :LANES] = (top_total[:, :LANES] / above).astype(BF16)
+    top_zero[:, LANES:] = (top_total[:, LANES:] / above).astype(BF16)
+
+
+def call(kernel, outs, scalars, arrays, scratch, name, collective=None, space=VMEM):
+    if space is not VMEM:
+        arrays = [pltpu.with_memory_space_constraint(a, space) for a in arrays]
     in_specs = [pl.BlockSpec(memory_space=SMEM)] * len(scalars)
-    in_specs += [pl.BlockSpec(memory_space=VMEM)] * len(arrays)
+    in_specs += [pl.BlockSpec(memory_space=space)] * len(arrays)
     return pl.pallas_call(
         kernel,
         out_shape=outs,
@@ -522,63 +540,66 @@
     doubled = shape(1, senders.shape[1], ints)
     pairs_shape = shape(2 * coarse_all, LANES, F32)
 
-    halos, all_counts, all_parents, twice_parents, twice_senders, twice_receivers, parent = call(
+    coarse_row = coarse_receiver.reshape(1, -1)
+    top_row = top_receiver.reshape(1, -1)
+    (
+        table, terms, near_nodes, weights, near_coarse, near_top, near_gains, near_receivers,
+        near_coarse_row, near_top_row, all_counts, all_parents, twice_parents, twice_senders,
+        twice_receivers, parent,
+    ) = call(
         exchange_kernel,
         (
-            jax.ShapeDtypeStruct((4, halo, width), BF16), rows16, ints16, ints16,
+            shape(2 * (nodes + 4 * halo), LANES, F32), shape(2 * nodes + 8, LANES, F32),
+            shape(nodes), *[jax.ShapeDtypeStruct(fine_weights.shape, BF16)] * 3,
+            shape(3, width, F32), doubled, shape(1, coarse_row.shape[1], ints),
+            shape(1, top_row.shape[1], ints), rows16, ints16, ints16,
             doubled, doubled, shape(1, nodes, ints),
         ),
-        (lists,), (fine_nodes, fine_weights, owner, local, parents, senders, receivers),
+        (),
+        (
+            lists, fine_nodes, fine_weights, coarse_weights, top_weights, gains, owner, local, parents,
+            senders, receivers, coarse_row, top_row,
+        ),
         [
-            VMEM((nodes, 2, LANES), F32), VMEM((4, halo, 2, LANES), F32),
-            VMEM((4, halo, width), BF16), VMEM((members, 1, coarse_rows), F32),
+            SMEM(lists.shape, ints), VMEM((1, nodes), ints), VMEM((1, nodes), ints), VMEM((1, 1, coarse_rows), ints),
+            VMEM(senders.shape, ints), VMEM((nodes, 2, LANES), F32),
+            VMEM((4, halo, 2, LANES), F32), VMEM((4, halo, width), BF16),
+            VMEM((4, halo, width), BF16), VMEM((members, 1, coarse_rows), F32), dma((14,)),
         ]
         + [dma((4,))] * 2 + [dma((members - 1,))] * 4,
-        "exchange", 0,
+        "exchange", 0, pltpu.MemorySpace.HBM,
     )
     fine_one = call(
         fine_kernel, shape(nodes), (twice_senders, twice_receivers),
-        (fine_nodes, halos, fine_weights, gains, receivers),
-        [
-            VMEM((2 * (nodes + 4 * halo), LANES), F32), VMEM((2 * nodes + 8, LANES), F32),
-            VMEM((2048, LANES), F32), VMEM((2, 1024, width), BF16), VMEM((nodes, width), F32),
-        ],
+        (table, terms, near_nodes, weights, near_gains, near_receivers),
+        [VMEM((2048, LANES), F32), VMEM((2, 1024, width), BF16), VMEM((nodes, width), F32)],
         "fine_layer",
     )
     half = coarse_rows // 2
     gathered = VMEM((side, side, coarse_rows, width), BF16)
-    coarse_zero, pairs, top_count = call(
-        collect_kernel, (shape(coarse_rows), pairs_shape, shape(top_rows, LANES, F32)), (),
-        (fine_one, parent, all_counts, all_parents, coarse_weights),
+    edges = coarse_sender.reshape(-1), coarse_receiver.reshape(-1)
+    pairs, top_zero = call(
+        coarse_kernel, (pairs_shape, shape(top_rows)), edges,
+        (fine_one, parent, all_counts, all_parents, near_coarse, near_gains, near_coarse_row),
         [
-            gathered,
+            VMEM((coarse_rows, width), BF16), VMEM((top_rows, LANES), F32),
+            VMEM((coarse_all, 2, LANES), F32), VMEM((coarse_rows, 2, LANES), F32),
+            VMEM((2048, LANES), F32), VMEM((1024, width), BF16), VMEM((coarse_rows, width), F32),
+            VMEM((top_rows, width), F32), gathered, gathered,
             VMEM((2, 3, side, half, width), BF16), VMEM((2, side, half, width), F32),
             VMEM((2, 3, side, half, width), BF16), VMEM((2, side, half, width), BF16),
             VMEM((2, 3, half, width), BF16),
-            dma((12,)), dma((12,)), *gather_sems,
+            dma((12,)), dma((12,)), *gather_sems, *gather_sems,
         ],
-        "collect", 1,
-    )
-    edges = coarse_sender.reshape(-1), coarse_receiver.reshape(-1)
-    coarse_one = call(
-        coarse_kernel, shape(coarse_rows), edges,
-        (coarse_zero, pairs, coarse_weights, gains, edges[1][None, :]),
-        [
-            VMEM((2 * coarse_rows, LANES), F32), VMEM((2048, LANES), F32),
-            VMEM((2, 1024, width), BF16), VMEM((coarse_rows, width), F32),
-        ],
-        "coarse_layer",
-    )
-    pairs, top_zero = call(
-        share_kernel, (pairs_shape, shape(top_rows)), (), (coarse_one, all_parents, top_count),
-        [gathered, VMEM((top_rows, width), F32), *gather_sems], "share", 2,
-    )
+        "coarse_levels", 1,
+    )
+    pairs = pltpu.with_memory_space_constraint(pairs, VMEM)
     edges = top_sender.reshape(-1), top_receiver.reshape(-1)
     place = lax.axis_index("gx").astype(ints).reshape(1)
     fine_state, coarse_state = call(
         top_kernel, (shape(nodes), shape(coarse_rows)),
         (*edges, twice_parents.reshape(-1), parent.reshape(-1), place),
-        (pairs, top_zero, fine_one, top_weights, gains, edges[1][None, :]),
+        (pairs, top_zero, fine_one, near_top, near_gains, near_top_row),
         [
             VMEM((2 * top_rows, LANES), F32), VMEM((2 * top_rows, LANES), F32),
             VMEM((2048, LANES), F32), VMEM((2, 1024, width), BF16), VMEM((top_rows, width), F32),

time: 127 us -> 118 us (0.929)
  local copies, waits for them, and re-layouts: 9.72 us -> 4.14 us
  Pallas kernels: 116 us -> 113 us
    unnamed x34 -> x12, local copies, waits for them, and re-layouts: 9.72 us -> 4.14 us
    pallas_call x6 -> x4, Pallas kernels: 116 us -> 113 us  [call(): pl.pallas_call(kernel, out_shape=outs, in_specs=in_specs, out_specs=jax.t...]
where the time goes in v5:
time: 118 us
  Pallas kernels  113 us (96%)
  local copies, waits for them, and re-layouts  4.14 us (4%)
    pallas_call x4, Pallas kernels, call(): pl.pallas_call(kernel, out_shape=outs, in_specs=in_specs, out_specs=jax.t...  113 us
    unnamed x12, local copies, waits for them, and re-layouts  4.14 us

profile of v5, /device:TPU:96, one launch (start us, length us, event | category | flops | bytes accessed | tf_op | source)
XLA Modules:
  0.0 118.3 jit_solution(13818588717245845691)
XLA Ops:
  0.6 19.0 %exchange.1 = (f32[8192,128]{1,0:T(8,128)S(1)}, f32[4104,128]{1,0:T(8,128)S(1)}, bf16[2048,256]{1,0:T(8,128)(2,1)S(1)}, bf16[6,256,256]{2,1,0:T(8,128)(2,1)S(1)}...) custom-call(s32[4,512]{1,0:T(4,128)} %bitcast.23, ...), custom_call_target="tpu_custom_call" | custom-call | flops 1000000000 | bytes 1048576 | tf_op jit(solution)/shard_map/exchange/pallas_call | solution.py:497
  19.6 0.0 copy-start.4
  19.6 0.0 copy-start.5
  19.6 0.0 copy-start.2
  19.6 0.0 copy-start.3
  19.6 20.6 %fine_layer.1.fine_one = bf16[2048,256]{1,0:T(8,128)(2,1)S(1)} custom-call(s32[1,8192]{1,0:T(1,128)S(1)} %get-tuple-element.24.senders, s32[1,8192]{1,0:T(1,128)S(1)} %get-tuple-element.25.receivers, f32[8192,128]{1,0:T(8,128)S(1)} %get-tuple-element.26.table, f32[4104,128]{1,0:T(8,128)S(1)} %get-tuple-element.27.terms, ...), custom_call_target="tpu_custom_call" | custom-call | flops 1000000000 | bytes 1048576 | tf_op jit(solution)/shard_map/fine_layer/pallas_call | solution.py:497
  40.3 0.0 copy-done.4
  40.3 0.0 copy-done.5
  40.3 61.4 %coarse_levels.1 = (f32[8192,128]{1,0:T(8,128)S(1)}, bf16[512,256]{1,0:T(8,128)(2,1)S(1)}) custom-call(s32[1024]{0:T(1024)S(1)} %bitcast.19, s32[1024]{0:T(1024)S(1)} %bitcast.18, bf16[2048,256]{1,0:T(8,128)(2,1)S(1)} %fine_layer.1.fine_one, s32[1,2048]{1,0:T(1,128)S(1)} %get-tuple-element.23.parent_row, f32[16,1,256]{2,1,0:T(1,128)S(1)} %get-tuple-element.32.all_counts, ...), custom_call_target="tpu_custom_call" | custom-call | flops 1000000000 | bytes 1048576 | tf_op jit(solution)/shard_map/coarse_levels/pallas_call | solution.py:497
  101.7 0.0 copy-start
  101.7 1.9 %copy-done = f32[8192,128]{1,0:T(8,128)} copy-done((f32[8192,128]{1,0:T(8,128)}, f32[8192,128]{1,0:T(8,128)S(1)}, u32[]{:S(2)}) %copy-start) | copy-done | bytes 4194328
  103.7 0.0 copy-done.2
  103.7 0.0 copy-done.3
  103.7 0.0 copy-start.1
  103.7 2.2 %copy-done.1 = f32[8192,128]{1,0:T(8,128)S(1)} copy-done((f32[8192,128]{1,0:T(8,128)S(1)}, f32[8192,128]{1,0:T(8,128)}, u32[]{:S(2)}) %copy-start.1) | copy-done | bytes 4194328
  105.9 12.4 %top_layer.1 = (bf16[2048,256]{1,0:T(8,128)(2,1)}, bf16[256,256]{1,0:T(8,128)(2,1)}) custom-call(s32[2048]{0:T(1024)S(1)} %bitcast.15, s32[2048]{0:T(1024)S(1)} %bitcast.16, s32[4096]{0:T(1024)S(1)} %bitcast.14, s32[2048]{0:T(1024)S(1)} %bitcast.17, s32[1]{0:T(128)} %bitcast.10.place, f32[8192,128]{1,0:T(8,128)S(1)} %copy-done.1, ...), custom_call_target="tpu_custom_call" | custom-call | flops 1000000000 | bytes 1048576 | tf_op jit(solution)/shard_map/top_layer/pallas_call | solution.py:497
Async XLA Ops:
  19.6 20.7 %copy-start.4 = (s32[1,1024]{1,0:T(1,128)S(1)}, s32[1,1024]{1,0:T(1,128)}, u32[]{:S(2)}) copy-start(s32[1,1024]{1,0:T(1,128)} %coarse_row_far.1) | copy-start | bytes 12292
  19.6 20.7 %copy-start.5 = (s32[1,1024]{1,0:T(1,128)S(1)}, s32[1,1024]{1,0:T(1,128)}, u32[]{:S(2)}) copy-start(s32[1,1024]{1,0:T(1,128)} %param.25) | copy-start | bytes 12292
  19.6 84.0 %copy-start.2 = (s32[1,2048]{1,0:T(1,128)S(1)}, s32[1,2048]{1,0:T(1,128)}, u32[]{:S(2)}) copy-start(s32[1,2048]{1,0:T(1,128)} %param.28) | copy-start | bytes 24580
  19.6 84.0 %copy-start.3 = (s32[1,2048]{1,0:T(1,128)S(1)}, s32[1,2048]{1,0:T(1,128)}, u32[]{:S(2)}) copy-start(s32[1,2048]{1,0:T(1,128)} %top_row_far.1) | copy-start | bytes 24580
  101.7 1.9 %copy-start = (f32[8192,128]{1,0:T(8,128)}, f32[8192,128]{1,0:T(8,128)S(1)}, u32[]{:S(2)}) copy-start(f32[8192,128]{1,0:T(8,128)S(1)} %get-tuple-element.36.coarse_pairs) | copy-start | bytes 12582916
  103.7 2.2 %copy-start.1 = (f32[8192,128]{1,0:T(8,128)S(1)}, f32[8192,128]{1,0:T(8,128)}, u32[]{:S(2)}) copy-start(f32[8192,128]{1,0:T(8,128)} %copy-done) | copy-start | bytes 12582916

commit v6 on v5

--- a/solution.py
+++ b/solution.py
@@ -128,25 +128,29 @@
 
 
 def top_kernel(
-    senders, receivers, twice_parents, fine_parents, place, coarse_pairs, top_zero, fine_one,
-    weights, gains, target_row,
-    fine_state, coarse_state, table, terms, sums, hidden, total,
+    senders, receivers, twice_parents, fine_parents, fine_tops, place, coarse, top_zero, fine_one,
+    weights_far, gains, target_row,
+    fine_state, coarse_state, weights, fetched, coarse_pairs, table, terms, sums, hidden, total,
 ):
     count = top_zero.shape[0]
     own = coarse_state.shape[0]
+    fetch = pltpu.make_async_copy(weights_far, weights, fetched)
+    fetch.start()
+    spread_rows(coarse, coarse_pairs, 0, coarse.shape[0], 1024)
+    fetch.wait()
     project_rows(top_zero, weights[0], table, 0, count, 512)
     project_rows(top_zero, weights[1], terms, 0, count, 512)
     pass_edges(
-        lambda e: pair(table, 2 * senders[e]) + pair(terms, 2 * receivers[e]),
+        lambda e: pair(table, senders[0, e]) + pair(terms, receivers[0, e]),
         target_row, sums, hidden, total, target_row.shape[1], 1024,
     )
     put_rows(table, 0, count, update(top_zero, total, weights, gains[2:3, :], 0, count).astype(F32))
 
-    def lift(parent):
-        return pair(coarse_pairs, 2 * parent) + pair(table, twice_parents[parent])
+    def lift(parent, above):
+        return pair(coarse_pairs, 2 * parent) + pair(table, above)
 
     first = place[0] * own
-    pick_pairs(own, 32, sums, lambda e: lift(first + e))
+    pick_pairs(own, 32, sums, lambda e: lift(first + e, twice_parents[first + e]))
     left, right = get_rows(sums, 0, own)
     coarse_state[:, :LANES] = left.astype(BF16)
     coarse_state[:, LANES:] = right.astype(BF16)
@@ -154,7 +158,10 @@
 
     @pl.loop(0, fine_one.shape[0] // chunk)
     def _(c):
-        pick_pairs(chunk, 64, sums, lambda e: lift(fine_parents[c * chunk + e]))
+        pick_pairs(
+            chunk, 64, sums,
+            lambda e: lift(fine_parents[c * chunk + e], fine_tops[c * chunk + e]),
+        )
 
         @pl.loop(0, chunk // 256)
         def _(t):
@@ -215,11 +222,13 @@
 
 
 def exchange_kernel(
-    lists_far, nodes_far, weights_far, coarse_weights_far, top_weights_far, gains_far, owners_far, locals_far,
+    lists_far, nodes_far, weights_far, coarse_weights_far, gains_far, owners_far, locals_far,
     parents_far, senders_far, receivers_far, coarse_row_far, top_row_far,
-    table, terms, nodes, weights, coarse_weights, top_weights, gains, receivers, coarse_row,
+    top_senders_far,
+    table, terms, nodes, weights, coarse_weights, gains, receivers, coarse_row,
     top_row, all_counts, all_parents, twice_parents, twice_senders, twice_receivers, fine_parents,
-    lists, owners, locals_, parents, senders, rows3, picked, sent, halo, counts, fetched,
+    twice_top_senders, twice_top_receivers,
+    lists, owners, locals_, parents, senders, top_senders, rows3, picked, sent, halo, counts, fetched,
     send_halo, recv_halo, send_count, recv_count, send_parent, recv_parent,
 ):
     members, across = lax.axis_size("gx"), lax.axis_size("gy")
@@ -232,9 +241,9 @@
         (weights_far.at[0], weights.at[0]), (nodes_far, nodes), (parents_far, parents),
         (owners_far, owners), (locals_far, locals_), (senders_far, senders),
         (receivers_far, receivers), (weights_far.at[pl.ds(1, 5)], weights.at[pl.ds(1, 5)]),
-        (coarse_weights_far, coarse_weights), (top_weights_far, top_weights),
+        (coarse_weights_far, coarse_weights),
         (gains_far, gains), (coarse_row_far, coarse_row), (top_row_far, top_row),
-        (lists_far, lists),
+        (top_senders_far, top_senders), (lists_far, lists),
     )
     fetches = [
         pltpu.make_async_copy(source, target, fetched.at[k])
@@ -295,6 +304,8 @@
     terms[pl.ds(2 * rows, 8), :] = jnp.zeros((8, LANES), F32)
     twice_senders[...] = 2 * senders[...]
     twice_receivers[...] = 2 * receivers[...]
+    twice_top_senders[...] = 2 * top_senders[...]
+    twice_top_receivers[...] = 2 * top_row[...]
     for slot, copy in enumerate(halos):
         copy.wait()
         put_rows(table, rows + slot * length, length, halo[slot].astype(F32))
@@ -323,6 +334,8 @@
         return copy
 
     def widen(self, pairs, first, one, two):
+        if pairs is None:
+            return
         x, y = (one, two) if first == 0 else (two, one)
         side, rows = self.torus.side, self.whole.shape[2]
         begin = (x * side + y) * rows + first * self.half
@@ -371,9 +384,9 @@
 
 
 def coarse_kernel(
-    senders, receivers, fine_one, parent_row, all_counts, all_parents, weights, gains, target_row,
-    pairs, top_zero,
-    coarse_zero, top_count, table3, terms3, sums, hidden, total, top_total, whole_one,
+    senders, receivers, twice_parents, fine_parents, fine_one, parent_row, all_counts, all_parents, weights, gains, target_row,
+    whole_one, top_zero, fine_tops,
+    coarse_zero, top_count, table3, terms3, sums, hidden, total, top_total,
     gathered, pooled, kept, arrived, partial, arrived2, send_sum, recv_sum, send_all, recv_all,
     send_one, recv_one,
 ):
@@ -432,6 +445,14 @@
             copy.start()
             opened.append(copy)
             second_hop[part, way] = copy
+
+    @pl.loop(0, fine_tops.shape[0] // 32)
+    def _(t):
+        begin = t * 32
+        found = [twice_parents[fine_parents[begin + u]] for u in range(32)]
+        for u in range(32):
+            fine_tops[begin + u] = found[u]
+
     total_count = jnp.sum(all_counts[...], axis=(0, 1)).reshape(1, rows)
     square = (rows, rows)
     diagonal = lax.broadcasted_iota(jnp.int32, square, 0) == lax.broadcasted_iota(
@@ -483,22 +504,29 @@
         chosen = one_hot(jnp.concatenate(above, axis=1), 0, top_total.shape[0])
         top_total[...] += dot(chosen, jnp.concatenate(states, axis=0))
 
-    sharing.finish(pairs, after)
+    sharing.finish(None, after)
     above = jnp.maximum(top_count[...], 1.0)
     top_zero[:, :LANES] = (top_total[:, :LANES] / above).astype(BF16)
     top_zero[:, LANES:] = (top_total[:, LANES:] / above).astype(BF16)
 
 
-def call(kernel, outs, scalars, arrays, scratch, name, collective=None, space=VMEM):
-    if space is not VMEM:
-        arrays = [pltpu.with_memory_space_constraint(a, space) for a in arrays]
+def call(kernel, outs, scalars, arrays, scratch, name, collective=None, far=(), out_spaces=None):
+    hbm = pltpu.MemorySpace.HBM
+    arrays = [
+        pltpu.with_memory_space_constraint(array, hbm) if k in far else array
+        for k, array in enumerate(arrays)
+    ]
     in_specs = [pl.BlockSpec(memory_space=SMEM)] * len(scalars)
-    in_specs += [pl.BlockSpec(memory_space=space)] * len(arrays)
+    in_specs += [pl.BlockSpec(memory_space=hbm if k in far else VMEM) for k in range(len(arrays))]
     return pl.pallas_call(
         kernel,
         out_shape=outs,
         in_specs=in_specs,
-        out_specs=jax.tree.map(lambda _: pl.BlockSpec(memory_space=VMEM), outs),
+        out_specs=(
+            jax.tree.map(lambda _: pl.BlockSpec(memory_space=VMEM), outs)
+            if out_spaces is None
+            else tuple(pl.BlockSpec(memory_space=place) for place in out_spaces)
+        ),
         scratch_shapes=scratch,
         compiler_params=pltpu.CompilerParams(
             vmem_limit_bytes=40 << 20, collective_id=collective,
@@ -538,36 +566,36 @@
     rows16 = jax.ShapeDtypeStruct((members, 1, coarse_rows), F32)
     ints16 = jax.ShapeDtypeStruct((members, 1, coarse_rows), ints)
     doubled = shape(1, senders.shape[1], ints)
-    pairs_shape = shape(2 * coarse_all, LANES, F32)
 
     coarse_row = coarse_receiver.reshape(1, -1)
     top_row = top_receiver.reshape(1, -1)
     (
-        table, terms, near_nodes, weights, near_coarse, near_top, near_gains, near_receivers,
+        table, terms, near_nodes, weights, near_coarse, near_gains, near_receivers,
         near_coarse_row, near_top_row, all_counts, all_parents, twice_parents, twice_senders,
-        twice_receivers, parent,
+        twice_receivers, parent, twice_top_senders, twice_top_receivers,
     ) = call(
         exchange_kernel,
         (
             shape(2 * (nodes + 4 * halo), LANES, F32), shape(2 * nodes + 8, LANES, F32),
-            shape(nodes), *[jax.ShapeDtypeStruct(fine_weights.shape, BF16)] * 3,
+            shape(nodes), *[jax.ShapeDtypeStruct(fine_weights.shape, BF16)] * 2,
             shape(3, width, F32), doubled, shape(1, coarse_row.shape[1], ints),
             shape(1, top_row.shape[1], ints), rows16, ints16, ints16,
             doubled, doubled, shape(1, nodes, ints),
+            *[shape(1, top_row.shape[1], ints)] * 2,
         ),
         (),
         (
-            lists, fine_nodes, fine_weights, coarse_weights, top_weights, gains, owner, local, parents,
-            senders, receivers, coarse_row, top_row,
+            lists, fine_nodes, fine_weights, coarse_weights, gains, owner, local, parents,
+            senders, receivers, coarse_row, top_row, top_sender.reshape(1, -1),
         ),
         [
             SMEM(lists.shape, ints), VMEM((1, nodes), ints), VMEM((1, nodes), ints), VMEM((1, 1, coarse_rows), ints),
-            VMEM(senders.shape, ints), VMEM((nodes, 2, LANES), F32),
+            VMEM(senders.shape, ints), VMEM(top_row.shape, ints), VMEM((nodes, 2, LANES), F32),
             VMEM((4, halo, 2, LANES), F32), VMEM((4, halo, width), BF16),
             VMEM((4, halo, width), BF16), VMEM((members, 1, coarse_rows), F32), dma((14,)),
         ]
         + [dma((4,))] * 2 + [dma((members - 1,))] * 4,
-        "exchange", 0, pltpu.MemorySpace.HBM,
+        "exchange", 0, far=range(13),
     )
     fine_one = call(
         fine_kernel, shape(nodes), (twice_senders, twice_receivers),
@@ -578,33 +606,40 @@
     half = coarse_rows // 2
     gathered = VMEM((side, side, coarse_rows, width), BF16)
     edges = coarse_sender.reshape(-1), coarse_receiver.reshape(-1)
-    pairs, top_zero = call(
-        coarse_kernel, (pairs_shape, shape(top_rows)), edges,
+    gathered_one, top_zero, fine_tops = call(
+        coarse_kernel,
+        (
+            jax.ShapeDtypeStruct((side, side, coarse_rows, width), BF16), shape(top_rows),
+            jax.ShapeDtypeStruct((nodes,), ints),
+        ),
+        (*edges, twice_parents.reshape(-1), parent.reshape(-1)),
         (fine_one, parent, all_counts, all_parents, near_coarse, near_gains, near_coarse_row),
         [
             VMEM((coarse_rows, width), BF16), VMEM((top_rows, LANES), F32),
             VMEM((coarse_all, 2, LANES), F32), VMEM((coarse_rows, 2, LANES), F32),
             VMEM((2048, LANES), F32), VMEM((1024, width), BF16), VMEM((coarse_rows, width), F32),
-            VMEM((top_rows, width), F32), gathered, gathered,
+            VMEM((top_rows, width), F32), gathered,
             VMEM((2, 3, side, half, width), BF16), VMEM((2, side, half, width), F32),
             VMEM((2, 3, side, half, width), BF16), VMEM((2, side, half, width), BF16),
             VMEM((2, 3, half, width), BF16),
             dma((12,)), dma((12,)), *gather_sems, *gather_sems,
         ],
-        "coarse_levels", 1,
-    )
-    pairs = pltpu.with_memory_space_constraint(pairs, VMEM)
-    edges = top_sender.reshape(-1), top_receiver.reshape(-1)
+        "coarse_levels", 1, out_spaces=(VMEM, VMEM, SMEM),
+    )
     place = lax.axis_index("gx").astype(ints).reshape(1)
     fine_state, coarse_state = call(
         top_kernel, (shape(nodes), shape(coarse_rows)),
-        (*edges, twice_parents.reshape(-1), parent.reshape(-1), place),
-        (pairs, top_zero, fine_one, near_top, near_gains, near_top_row),
+        (
+            twice_top_senders, twice_top_receivers, twice_parents.reshape(-1), parent.reshape(-1),
+            fine_tops, place,
+        ),
+        (gathered_one.reshape(coarse_all, width), top_zero, fine_one, top_weights, near_gains, near_top_row),
         [
-            VMEM((2 * top_rows, LANES), F32), VMEM((2 * top_rows, LANES), F32),
-            VMEM((2048, LANES), F32), VMEM((2, 1024, width), BF16), VMEM((top_rows, width), F32),
+            VMEM(top_weights.shape, BF16), dma(()),
+            VMEM((2 * coarse_all, LANES), F32), VMEM((2 * top_rows, LANES), F32),
+            VMEM((2 * top_rows, LANES), F32), VMEM((2048, LANES), F32), VMEM((2, 1024, width), BF16), VMEM((top_rows, width), F32),
         ],
-        "top_layer",
+        "top_layer", far=(3,),
     )
     return (fine_state, coarse_state[None])
 

time: 118 us -> 117 us (level)
  local copies, waits for them, and re-layouts: 4.14 us -> 0.01 us
  Pallas kernels: 113 us -> 116 us
    unnamed x12 -> x4, local copies, waits for them, and re-layouts: 4.14 us -> 0.01 us
    pallas_call x4, Pallas kernels: 113 us -> 116 us  [call(): pl.pallas_call(kernel, out_shape=outs, in_specs=in_specs, out_specs=jax.t...]
where the time goes in v6:
time: 117 us
  Pallas kernels  116 us (99%)
    pallas_call x4, Pallas kernels, call(): pl.pallas_call(kernel, out_shape=outs, in_specs=in_specs, out_specs=jax.t...  116 us

profile of v6, /device:TPU:96, one launch (start us, length us, event | category | flops | bytes accessed | tf_op | source)
XLA Modules:
  0.0 116.7 jit_solution(10281559781528178359)
XLA Ops:
  0.6 19.0 %exchange.1 = (f32[8192,128]{1,0:T(8,128)S(1)}, f32[4104,128]{1,0:T(8,128)S(1)}, bf16[2048,256]{1,0:T(8,128)(2,1)S(1)}, bf16[6,256,256]{2,1,0:T(8,128)(2,1)S(1)}...) custom-call(s32[4,512]{1,0:T(4,128)} %bitcast.23, ...), custom_call_target="tpu_custom_call" | custom-call | flops 1000000000 | bytes 1048576 | tf_op jit(solution)/shard_map/exchange/pallas_call | solution.py:521
  19.6 0.0 copy-start
  19.7 0.0 copy-start.1
  19.7 20.6 %fine_layer.1.fine_one = bf16[2048,256]{1,0:T(8,128)(2,1)S(1)} custom-call(s32[1,8192]{1,0:T(1,128)S(1)} %get-tuple-element.28.senders, s32[1,8192]{1,0:T(1,128)S(1)} %get-tuple-element.29.receivers, f32[8192,128]{1,0:T(8,128)S(1)} %get-tuple-element.30.table, f32[4104,128]{1,0:T(8,128)S(1)} %get-tuple-element.31.terms, ...), custom_call_target="tpu_custom_call" | custom-call | flops 1000000000 | bytes 1048576 | tf_op jit(solution)/shard_map/fine_layer/pallas_call | solution.py:521
  40.2 0.0 copy-done
  40.2 0.0 copy-done.1
  40.3 63.6 %coarse_levels.1 = (bf16[4,4,256,256]{3,2,1,0:T(8,128)(2,1)S(1)}, bf16[512,256]{1,0:T(8,128)(2,1)S(1)}, s32[2048]{0:T(1024)S(1)}) custom-call(s32[1024]{0:T(1024)S(1)} %bitcast.19, s32[1024]{0:T(1024)S(1)} %bitcast.18, s32[4096]{0:T(1024)S(1)} %bitcast.14, s32[2048]{0:T(1024)S(1)} %bitcast.16, bf16[2048,256]{1,0:T(8,128)(2,1)S(1)} %fine_layer.1.fine_one, ...), custom_call_target="tpu_custom_call" | custom-call | flops 1000000000 | bytes 1048576 | tf_op jit(solution)/shard_map/coarse_levels/pallas_call | solution.py:521
  103.9 12.7 %top_layer.1 = (bf16[2048,256]{1,0:T(8,128)(2,1)}, bf16[256,256]{1,0:T(8,128)(2,1)}) custom-call(s32[1,2048]{1,0:T(1,128)S(1)} %get-tuple-element.24.senders, s32[1,2048]{1,0:T(1,128)S(1)} %get-tuple-element.25.receivers, s32[4096]{0:T(1024)S(1)} %bitcast.15, s32[2048]{0:T(1024)S(1)} %bitcast.17, s32[2048]{0:T(1024)S(1)} %get-tuple-element.40.fine_tops, ...), custom_call_target="tpu_custom_call" | custom-call | flops 1000000000 | bytes 1048576 | tf_op jit(solution)/shard_map/top_layer/pallas_call | solution.py:521
Async XLA Ops:
  19.6 20.6 %copy-start = (s32[1,1024]{1,0:T(1,128)S(1)}, s32[1,1024]{1,0:T(1,128)}, u32[]{:S(2)}) copy-start(s32[1,1024]{1,0:T(1,128)} %coarse_row_far.1) | copy-start | bytes 12292
  19.7 20.6 %copy-start.1 = (s32[1,1024]{1,0:T(1,128)S(1)}, s32[1,1024]{1,0:T(1,128)}, u32[]{:S(2)}) copy-start(s32[1,1024]{1,0:T(1,128)} %param.25) | copy-start | bytes 12292

commit v7 on v6

--- a/solution.py
+++ b/solution.py
@@ -420,14 +420,6 @@
             first_hop[part, way] = copy
     for part in (0, 1):
         kept[part] = share(part, torus.at[1 - part])
-    ones = jnp.ones((side * rows, LANES), BF16)
-    top_count[...] = jnp.zeros_like(top_count)
-
-    @pl.loop(0, side)
-    def _(k):
-        above = jnp.concatenate([all_parents[k * side + q] for q in range(side)], axis=1)
-        top_count[...] += dot(one_hot(above, 0, top_count.shape[0]), ones)
-
     for part in (0, 1):
         for way in range(3):
             first_hop[part, way].wait_recv()
@@ -445,14 +437,6 @@
             copy.start()
             opened.append(copy)
             second_hop[part, way] = copy
-
-    @pl.loop(0, fine_tops.shape[0] // 32)
-    def _(t):
-        begin = t * 32
-        found = [twice_parents[fine_parents[begin + u]] for u in range(32)]
-        for u in range(32):
-            fine_tops[begin + u] = found[u]
-
     total_count = jnp.sum(all_counts[...], axis=(0, 1)).reshape(1, rows)
     square = (rows, rows)
     diagonal = lax.broadcasted_iota(jnp.int32, square, 0) == lax.broadcasted_iota(
@@ -479,6 +463,14 @@
     term = dot(coarse_zero[...], weights[1]).astype(BF16).astype(F32)
     terms3[:, 0, :] = term[:, :LANES]
     terms3[:, 1, :] = term[:, LANES:]
+    ones = jnp.ones((side * rows, LANES), BF16)
+    top_count[...] = jnp.zeros_like(top_count)
+
+    @pl.loop(0, side)
+    def _(k):
+        above = jnp.concatenate([all_parents[k * side + q] for q in range(side)], axis=1)
+        top_count[...] += dot(one_hot(above, 0, top_count.shape[0]), ones)
+
     gathering.finish(table3)
     for copy in opened:
         copy.wait_send()
@@ -492,6 +484,14 @@
     sharing = Gathering(torus, whole_one, (send_one, recv_one))
     sharing.begin(0)
     sharing.begin(1)
+
+    @pl.loop(0, fine_tops.shape[0] // 32)
+    def _(t):
+        begin = t * 32
+        found = [twice_parents[fine_parents[begin + u]] for u in range(32)]
+        for u in range(32):
+            fine_tops[begin + u] = found[u]
+
     top_total[...] = jnp.zeros_like(top_total)
 
     def after(column):

time: 117 us -> 115 us (0.983)
  Pallas kernels: 116 us -> 114 us
    pallas_call x4, Pallas kernels: 116 us -> 114 us  [call(): pl.pallas_call(kernel, out_shape=outs, in_specs=in_specs, out_specs=jax.t...]
where the time goes in v7:
time: 115 us
  Pallas kernels  114 us (99%)
    pallas_call x4, Pallas kernels, call(): pl.pallas_call(kernel, out_shape=outs, in_specs=in_specs, out_specs=jax.t...  114 us

profile of v7, /device:TPU:96, one launch (start us, length us, event | category | flops | bytes accessed | tf_op | source)
XLA Modules:
  0.0 115.2 jit_solution(13938453064425063689)
XLA Ops:
  0.6 19.0 %exchange.1 = (f32[8192,128]{1,0:T(8,128)S(1)}, f32[4104,128]{1,0:T(8,128)S(1)}, bf16[2048,256]{1,0:T(8,128)(2,1)S(1)}, bf16[6,256,256]{2,1,0:T(8,128)(2,1)S(1)}...) custom-call(s32[4,512]{1,0:T(4,128)} %bitcast.23, ...), custom_call_target="tpu_custom_call" | custom-call | flops 1000000000 | bytes 1048576 | tf_op jit(solution)/shard_map/exchange/pallas_call | solution.py:521
  19.6 0.0 copy-start
  19.7 0.0 copy-start.1
  19.7 20.6 %fine_layer.1.fine_one = bf16[2048,256]{1,0:T(8,128)(2,1)S(1)} custom-call(s32[1,8192]{1,0:T(1,128)S(1)} %get-tuple-element.28.senders, s32[1,8192]{1,0:T(1,128)S(1)} %get-tuple-element.29.receivers, f32[8192,128]{1,0:T(8,128)S(1)} %get-tuple-element.30.table, f32[4104,128]{1,0:T(8,128)S(1)} %get-tuple-element.31.terms, ...), custom_call_target="tpu_custom_call" | custom-call | flops 1000000000 | bytes 1048576 | tf_op jit(solution)/shard_map/fine_layer/pallas_call | solution.py:521
  40.3 0.0 copy-done
  40.3 0.0 copy-done.1
  40.3 62.0 %coarse_levels.1 = (bf16[4,4,256,256]{3,2,1,0:T(8,128)(2,1)S(1)}, bf16[512,256]{1,0:T(8,128)(2,1)S(1)}, s32[2048]{0:T(1024)S(1)}) custom-call(s32[1024]{0:T(1024)S(1)} %bitcast.19, s32[1024]{0:T(1024)S(1)} %bitcast.18, s32[4096]{0:T(1024)S(1)} %bitcast.14, s32[2048]{0:T(1024)S(1)} %bitcast.16, bf16[2048,256]{1,0:T(8,128)(2,1)S(1)} %fine_layer.1.fine_one, ...), custom_call_target="tpu_custom_call" | custom-call | flops 1000000000 | bytes 1048576 | tf_op jit(solution)/shard_map/coarse_levels/pallas_call | solution.py:521
  102.3 12.7 %top_layer.1 = (bf16[2048,256]{1,0:T(8,128)(2,1)}, bf16[256,256]{1,0:T(8,128)(2,1)}) custom-call(s32[1,2048]{1,0:T(1,128)S(1)} %get-tuple-element.24.senders, s32[1,2048]{1,0:T(1,128)S(1)} %get-tuple-element.25.receivers, s32[4096]{0:T(1024)S(1)} %bitcast.15, s32[2048]{0:T(1024)S(1)} %bitcast.17, s32[2048]{0:T(1024)S(1)} %get-tuple-element.40.fine_tops, ...), custom_call_target="tpu_custom_call" | custom-call | flops 1000000000 | bytes 1048576 | tf_op jit(solution)/shard_map/top_layer/pallas_call | solution.py:521
Async XLA Ops:
  19.6 20.6 %copy-start = (s32[1,1024]{1,0:T(1,128)S(1)}, s32[1,1024]{1,0:T(1,128)}, u32[]{:S(2)}) copy-start(s32[1,1024]{1,0:T(1,128)} %coarse_row_far.1) | copy-start | bytes 12292
  19.7 20.6 %copy-start.1 = (s32[1,1024]{1,0:T(1,128)S(1)}, s32[1,1024]{1,0:T(1,128)}, u32[]{:S(2)}) copy-start(s32[1,1024]{1,0:T(1,128)} %param.25) | copy-start | bytes 12292

commit v8 on v7

--- a/solution.py
+++ b/solution.py
@@ -362,12 +362,13 @@
         for way in range(3):
             self.inner[first, column, way] = self.send(first, 1 - first, held, 1 + column, way)
 
-    def finish(self, pairs, after=lambda column: None):
+    def finish(self, pairs, after=lambda column: None, during=lambda: None):
         torus = self.torus
         for way in range(3):
             for first in (0, 1):
                 self.outer[first, way].wait_recv()
                 self.pass_on(first, 1 + way)
+        during()
         for column in range(4):
             for first in (0, 1):
                 self.widen(pairs, first, self.place(first, column), torus.at[1 - first])
@@ -386,7 +387,7 @@
 def coarse_kernel(
     senders, receivers, twice_parents, fine_parents, fine_one, parent_row, all_counts, all_parents, weights, gains, target_row,
     whole_one, top_zero, fine_tops,
-    coarse_zero, top_count, table3, terms3, sums, hidden, total, top_total,
+    coarse_zero, top_count, table3, terms3, sums, ahead, hidden, total, top_total,
     gathered, pooled, kept, arrived, partial, arrived2, send_sum, recv_sum, send_all, recv_all,
     send_one, recv_one,
 ):
@@ -420,15 +421,13 @@
             first_hop[part, way] = copy
     for part in (0, 1):
         kept[part] = share(part, torus.at[1 - part])
+    for way in (2, 0):
+        for part in (0, 1):
+            first_hop[part, way].wait_recv()
+            kept[part] += arrived[part, way].astype(F32)
     for part in (0, 1):
-        for way in range(3):
-            first_hop[part, way].wait_recv()
-        partial[part] = (
-            kept[part]
-            + arrived[part, 0].astype(F32)
-            + arrived[part, 1].astype(F32)
-            + arrived[part, 2].astype(F32)
-        ).astype(BF16)
+        first_hop[part, 1].wait_recv()
+        partial[part] = (kept[part] + arrived[part, 1].astype(F32)).astype(BF16)
         for way in range(3):
             copy = remote(
                 partial.at[part, torus.there(part, WAYS[way])], arrived2.at[part, way],
@@ -471,12 +470,15 @@
         above = jnp.concatenate([all_parents[k * side + q] for q in range(side)], axis=1)
         top_count[...] += dot(one_hot(above, 0, top_count.shape[0]), ones)
 
-    gathering.finish(table3)
+    edges = target_row.shape[1]
+
+    def during():
+        pick_pairs(edges, 32, ahead, lambda e: terms3[receivers[e]])
+
+    gathering.finish(table3, during=during)
     for copy in opened:
         copy.wait_send()
-
-    edges = target_row.shape[1]
-    pick_pairs(edges, 32, sums, lambda e: table3[senders[e]] + terms3[receivers[e]])
+    pick_pairs(edges, 32, sums, lambda e: table3[senders[e]] + pair(ahead, 2 * e))
     activate(sums, hidden, 0, edges)
     total[...] = dot(one_hot(target_row[...], 0, rows), hidden[...])
     whole_one[x, y] = update(coarse_zero, total, weights, gains[1:2, :], 0, rows)
@@ -617,7 +619,8 @@
         [
             VMEM((coarse_rows, width), BF16), VMEM((top_rows, LANES), F32),
             VMEM((coarse_all, 2, LANES), F32), VMEM((coarse_rows, 2, LANES), F32),
-            VMEM((2048, LANES), F32), VMEM((1024, width), BF16), VMEM((coarse_rows, width), F32),
+            VMEM((2048, LANES), F32), VMEM((2048, LANES), F32),
+            VMEM((1024, width), BF16), VMEM((coarse_rows, width), F32),
             VMEM((top_rows, width), F32), gathered,
             VMEM((2, 3, side, half, width), BF16), VMEM((2, side, half, width), F32),
             VMEM((2, 3, side, half, width), BF16), VMEM((2, side, half, width), BF16),

time: 115 us -> 116 us (level); the launches traced: 115 us -> 115 us
  no operation moved by 1% of the time
where the time goes in v8:
time: 116 us; the launch traced here: 115 us
  Pallas kernels  114 us (98%)
    pallas_call x4, Pallas kernels, call(): pl.pallas_call(kernel, out_shape=outs, in_specs=in_specs, out_specs=jax.t...  114 us

profile of v8, /device:TPU:96, one launch (start us, length us, event | category | flops | bytes accessed | tf_op | source)
XLA Modules:
  0.0 114.8 jit_solution(17209389440539151996)
XLA Ops:
  0.6 19.0 %exchange.1 = (f32[8192,128]{1,0:T(8,128)S(1)}, f32[4104,128]{1,0:T(8,128)S(1)}, bf16[2048,256]{1,0:T(8,128)(2,1)S(1)}, bf16[6,256,256]{2,1,0:T(8,128)(2,1)S(1)}...) custom-call(s32[4,512]{1,0:T(4,128)} %bitcast.23, ...), custom_call_target="tpu_custom_call" | custom-call | flops 1000000000 | bytes 1048576 | tf_op jit(solution)/shard_map/exchange/pallas_call | solution.py:523
  19.6 0.0 copy-start
  19.7 0.0 copy-start.1
  19.7 20.6 %fine_layer.1.fine_one = bf16[2048,256]{1,0:T(8,128)(2,1)S(1)} custom-call(s32[1,8192]{1,0:T(1,128)S(1)} %get-tuple-element.28.senders, s32[1,8192]{1,0:T(1,128)S(1)} %get-tuple-element.29.receivers, f32[8192,128]{1,0:T(8,128)S(1)} %get-tuple-element.30.table, f32[4104,128]{1,0:T(8,128)S(1)} %get-tuple-element.31.terms, ...), custom_call_target="tpu_custom_call" | custom-call | flops 1000000000 | bytes 1048576 | tf_op jit(solution)/shard_map/fine_layer/pallas_call | solution.py:523
  40.3 0.0 copy-done
  40.3 0.0 copy-done.1
  40.3 61.5 %coarse_levels.1 = (bf16[4,4,256,256]{3,2,1,0:T(8,128)(2,1)S(1)}, bf16[512,256]{1,0:T(8,128)(2,1)S(1)}, s32[2048]{0:T(1024)S(1)}) custom-call(s32[1024]{0:T(1024)S(1)} %bitcast.19, s32[1024]{0:T(1024)S(1)} %bitcast.18, s32[4096]{0:T(1024)S(1)} %bitcast.14, s32[2048]{0:T(1024)S(1)} %bitcast.16, bf16[2048,256]{1,0:T(8,128)(2,1)S(1)} %fine_layer.1.fine_one, ...), custom_call_target="tpu_custom_call" | custom-call | flops 1000000000 | bytes 1048576 | tf_op jit(solution)/shard_map/coarse_levels/pallas_call | solution.py:523
  101.9 12.7 %top_layer.1 = (bf16[2048,256]{1,0:T(8,128)(2,1)}, bf16[256,256]{1,0:T(8,128)(2,1)}) custom-call(s32[1,2048]{1,0:T(1,128)S(1)} %get-tuple-element.24.senders, s32[1,2048]{1,0:T(1,128)S(1)} %get-tuple-element.25.receivers, s32[4096]{0:T(1024)S(1)} %bitcast.15, s32[2048]{0:T(1024)S(1)} %bitcast.17, s32[2048]{0:T(1024)S(1)} %get-tuple-element.40.fine_tops, ...), custom_call_target="tpu_custom_call" | custom-call | flops 1000000000 | bytes 1048576 | tf_op jit(solution)/shard_map/top_layer/pallas_call | solution.py:523
Async XLA Ops:
  19.6 20.7 %copy-start = (s32[1,1024]{1,0:T(1,128)S(1)}, s32[1,1024]{1,0:T(1,128)}, u32[]{:S(2)}) copy-start(s32[1,1024]{1,0:T(1,128)} %coarse_row_far.1) | copy-start | bytes 12292
  19.7 20.7 %copy-start.1 = (s32[1,1024]{1,0:T(1,128)S(1)}, s32[1,1024]{1,0:T(1,128)}, u32[]{:S(2)}) copy-start(s32[1,1024]{1,0:T(1,128)} %param.25) | copy-start | bytes 12292

commit v9 on v7

--- a/solution.py
+++ b/solution.py
@@ -189,7 +189,7 @@
     )
 
 
-WAYS = (1, -1, 2)
+WAYS = (2, 1, -1)
 
 
 def greet_first(devices):
@@ -364,14 +364,14 @@
 
     def finish(self, pairs, after=lambda column: None):
         torus = self.torus
-        for way in range(3):
+        for way in (1, 2, 0):
             for first in (0, 1):
                 self.outer[first, way].wait_recv()
                 self.pass_on(first, 1 + way)
-        for column in range(4):
+        for column in (0, 2, 3, 1):
             for first in (0, 1):
                 self.widen(pairs, first, self.place(first, column), torus.at[1 - first])
-            for way in range(3):
+            for way in (1, 2, 0):
                 for first in (0, 1):
                     self.inner[first, column, way].wait_recv()
                     self.widen(
@@ -405,11 +405,11 @@
         chosen = jnp.concatenate([one_hot(parents, begin, half) for begin in begins], axis=0)
         return dot(chosen, fine_one[...]).reshape(side, half, 2 * LANES)
 
-    for way in (2, 0, 1):
+    for way in range(3):
         for part in (0, 1):
             axis = 1 - part
             pooled[part, way] = share(part, torus.there(axis, WAYS[way])).astype(BF16)
-            if (way, part) == (2, 0):
+            if (way, part) == (0, 0):
                 greet_last(torus.ring())
             copy = remote(
                 pooled.at[part, way], arrived.at[part, way], (send_sum, recv_sum),

time: 115 us -> 118 us (1.026)
  Pallas kernels: 114 us -> 116 us
    pallas_call x4, Pallas kernels: 114 us -> 116 us  [call(): pl.pallas_call(kernel, out_shape=outs, in_specs=in_specs, out_specs=jax.t...]
where the time goes in v9:
time: 118 us; the launch traced here: 117 us
  Pallas kernels  116 us (98%)
    pallas_call x4, Pallas kernels, call(): pl.pallas_call(kernel, out_shape=outs, in_specs=in_specs, out_specs=jax.t...  116 us

profile of v9, /device:TPU:96, one launch (start us, length us, event | category | flops | bytes accessed | tf_op | source)
XLA Modules:
  0.0 117.1 jit_solution(18046686736812426739)
XLA Ops:
  0.6 19.0 %exchange.1 = (f32[8192,128]{1,0:T(8,128)S(1)}, f32[4104,128]{1,0:T(8,128)S(1)}, bf16[2048,256]{1,0:T(8,128)(2,1)S(1)}, bf16[6,256,256]{2,1,0:T(8,128)(2,1)S(1)}...) custom-call(s32[4,512]{1,0:T(4,128)} %bitcast.23, ...), custom_call_target="tpu_custom_call" | custom-call | flops 1000000000 | bytes 1048576 | tf_op jit(solution)/shard_map/exchange/pallas_call | solution.py:521
  19.6 0.0 copy-start
  19.7 0.0 copy-start.1
  19.7 20.6 %fine_layer.1.fine_one = bf16[2048,256]{1,0:T(8,128)(2,1)S(1)} custom-call(s32[1,8192]{1,0:T(1,128)S(1)} %get-tuple-element.28.senders, s32[1,8192]{1,0:T(1,128)S(1)} %get-tuple-element.29.receivers, f32[8192,128]{1,0:T(8,128)S(1)} %get-tuple-element.30.table, f32[4104,128]{1,0:T(8,128)S(1)} %get-tuple-element.31.terms, ...), custom_call_target="tpu_custom_call" | custom-call | flops 1000000000 | bytes 1048576 | tf_op jit(solution)/shard_map/fine_layer/pallas_call | solution.py:521
  40.3 0.0 copy-done
  40.3 0.0 copy-done.1
  40.3 63.9 %coarse_levels.1 = (bf16[4,4,256,256]{3,2,1,0:T(8,128)(2,1)S(1)}, bf16[512,256]{1,0:T(8,128)(2,1)S(1)}, s32[2048]{0:T(1024)S(1)}) custom-call(s32[1024]{0:T(1024)S(1)} %bitcast.19, s32[1024]{0:T(1024)S(1)} %bitcast.18, s32[4096]{0:T(1024)S(1)} %bitcast.14, s32[2048]{0:T(1024)S(1)} %bitcast.16, bf16[2048,256]{1,0:T(8,128)(2,1)S(1)} %fine_layer.1.fine_one, ...), custom_call_target="tpu_custom_call" | custom-call | flops 1000000000 | bytes 1048576 | tf_op jit(solution)/shard_map/coarse_levels/pallas_call | solution.py:521
  104.2 12.7 %top_layer.1 = (bf16[2048,256]{1,0:T(8,128)(2,1)}, bf16[256,256]{1,0:T(8,128)(2,1)}) custom-call(s32[1,2048]{1,0:T(1,128)S(1)} %get-tuple-element.24.senders, s32[1,2048]{1,0:T(1,128)S(1)} %get-tuple-element.25.receivers, s32[4096]{0:T(1024)S(1)} %bitcast.15, s32[2048]{0:T(1024)S(1)} %bitcast.17, s32[2048]{0:T(1024)S(1)} %get-tuple-element.40.fine_tops, ...), custom_call_target="tpu_custom_call" | custom-call | flops 1000000000 | bytes 1048576 | tf_op jit(solution)/shard_map/top_layer/pallas_call | solution.py:521
Async XLA Ops:
  19.6 20.6 %copy-start = (s32[1,1024]{1,0:T(1,128)S(1)}, s32[1,1024]{1,0:T(1,128)}, u32[]{:S(2)}) copy-start(s32[1,1024]{1,0:T(1,128)} %coarse_row_far.1) | copy-start | bytes 12292
  19.7 20.6 %copy-start.1 = (s32[1,1024]{1,0:T(1,128)S(1)}, s32[1,1024]{1,0:T(1,128)}, u32[]{:S(2)}) copy-start(s32[1,1024]{1,0:T(1,128)} %param.25) | copy-start | bytes 12292
